TPU v7x, 32 devices: a whole 2x2x4 slice. The times are simulated.
32 devices in a mesh: dev: 32 (over z, y, x, core).
Axes of the slice: x: 2, y: 2, z: 4, core: 2. Of those that a mesh axis runs over, the one named last changes fastest.
Arguments:
- right_side: float32 [2048, 3, 128], P('dev'), may hold values from -105 to 105
- vertices: float32 [2048, 3, 128], P('dev'), may hold values from 0 to 1
- panels: int32 [2048, 3, 128], P('dev'), may hold values from 0 to 127
- near_owner: int32 [2048, 2], P('dev'), may hold values from 0 to 31, all different within a row; in each aligned block of 64 rows (0 to 63, 64 to 127, ...) at most 8 rows name the same one
- near_local: int32 [2048, 2], P('dev'), may hold values from 0 to 63
- far_owner: int32 [2048, 2], P('dev'), may hold values from 0 to 31, all different within a row; in each aligned block of 64 rows (0 to 63, 64 to 127, ...) at most 8 rows name the same one
- far_local: int32 [2048, 2], P('dev'), may hold values from 0 to 63
- far_left: float32 [2048, 16, 384], P('dev'), may hold values from -0.5 to 0.5
- far_right: float32 [2048, 16, 384], P('dev'), may hold values from -0.5 to 0.5
Outputs:
- krylov_basis: float32 [2, 2048, 3, 128], P(None, 'dev')
- hessenberg: float32 [3, 2], replicated
Inputs may be any that keep to these rules, and one draw needn't show every extreme that they name: `near_owner`: the two entries of a row differ. Within one device's 64 rows no device number appears more than 8 times, and in every draw some number appears exactly 8 times. `far_owner`: the two entries of a row differ. Within one device's 64 rows no device number appears more than 8 times, and in every draw some number appears exactly 8 times.
All inputs are finite; a program needn't handle non-finite values.
Results may differ from a plain program's by a relative error of at most 0.0003.
Values sent between devices are 32-bit elements; how exact they have to be, the bound alone decides.
No kernel may reach another device: no remote copies, remote signals or barrier semaphores. Data moves between devices by JAX's collectives and lax.ppermute only.
A program may use at most 64 MiB of HBM per device.

v0:
```python
import jax
import jax.numpy as jnp
from jax import lax
from jax.sharding import PartitionSpec as P

highest = lax.Precision.HIGHEST
soft_sq = 0.0025
area_floor = 6.25e-06
kelvin_diag = 1.8
norm_eps = 1e-06
barycentric = (
    (2.0 / 3.0, 1.0 / 6.0, 1.0 / 6.0),
    (1.0 / 6.0, 2.0 / 3.0, 1.0 / 6.0),
    (1.0 / 6.0, 1.0 / 6.0, 2.0 / 3.0),
)
index_pairs = ((0, 0), (0, 1), (0, 2), (1, 1), (1, 2), (2, 2))


def panel_corners(vertex_table, connect):
    table_rows = lax.broadcasted_iota(jnp.int32, (vertex_table.shape[1], 1), 0)
    corner_list = []
    for m in range(3):
        select = (table_rows == connect[m][None, :]).astype(jnp.float32)
        corner_list.append(
            jnp.dot(vertex_table, select, precision=highest, preferred_element_type=jnp.float32)
        )
    return jnp.stack(corner_list)


def quad_points(corners):
    edge_one = corners[1] - corners[0]
    edge_two = corners[2] - corners[0]
    cross_x = edge_one[1] * edge_two[2] - edge_one[2] * edge_two[1]
    cross_y = edge_one[2] * edge_two[0] - edge_one[0] * edge_two[2]
    cross_z = edge_one[0] * edge_two[1] - edge_one[1] * edge_two[0]
    weight = jnp.sqrt(cross_x * cross_x + cross_y * cross_y + cross_z * cross_z + area_floor) / 6.0
    points = jnp.stack(
        [
            coords[0] * corners[0] + coords[1] * corners[1] + coords[2] * corners[2]
            for coords in barycentric
        ]
    )
    return (points, weight)


def near_block(points_first, weight_first, points_second, weight_second):
    panel_count = weight_first.shape[0]
    diag_sum = jnp.zeros((panel_count, panel_count), jnp.float32)
    outer_terms = [jnp.zeros((panel_count, panel_count), jnp.float32) for pair_index in index_pairs]
    for s in range(3):
        for t in range(3):
            offset = points_first[s][:, :, None] - points_second[t][:, None, :]
            inverse = lax.rsqrt(
                offset[0] * offset[0] + offset[1] * offset[1] + offset[2] * offset[2] + soft_sq
            )
            diag_sum = diag_sum + inverse
            inverse_cube = inverse * inverse * inverse
            outer_terms = [
                partial_sum + inverse_cube * offset[i] * offset[j]
                for partial_sum, (i, j) in zip(outer_terms, index_pairs)
            ]
    weight_pair = weight_first[:, None] * weight_second[None, :]
    matrix_rows = []
    for i in range(3):
        matrix_row = []
        for j in range(3):
            entry_sum = outer_terms[index_pairs.index((min(i, j), max(i, j)))]
            if i == j:
                entry_sum = entry_sum + kelvin_diag * diag_sum
            matrix_row.append(weight_pair * entry_sum)
        matrix_rows.append(jnp.stack(matrix_row))
    return jnp.stack(matrix_rows)


def apply_near(block_matrix, dense_first, dense_second):
    into_first = jnp.einsum("ijkl,jl->ik", block_matrix, dense_second, precision=highest)
    into_second = jnp.einsum("ijkl,ik->jl", block_matrix, dense_first, precision=highest)
    return (into_first, into_second)


def apply_far(left_factors, right_factors, flat_first, flat_second):
    coef_second = jnp.einsum("frk,fk->fr", right_factors, flat_second, precision=highest)
    into_first = jnp.einsum("frk,fr->fk", left_factors, coef_second, precision=highest)
    coef_first = jnp.einsum("frk,fk->fr", left_factors, flat_first, precision=highest)
    into_second = jnp.einsum("frk,fr->fk", right_factors, coef_first, precision=highest)
    return (into_first, into_second)


def slot_rank(owner_ids):
    entries = owner_ids.shape[0]
    same_owner = owner_ids[:, None] == owner_ids[None, :]
    earlier = lax.broadcasted_iota(jnp.int32, (entries, entries), 1) < lax.broadcasted_iota(
        jnp.int32, (entries, entries), 0
    )
    return jnp.sum(jnp.where(same_owner & earlier, 1, 0), axis=1).astype(jnp.int32)


def per_device(
    right_side, vertices, panels, near_owner, near_local, far_owner, far_local, far_left, far_right
):
    group_size = lax.axis_size("dev")
    clusters_here = right_side.shape[0]
    panel_count = right_side.shape[2]
    near_count = near_owner.shape[0]
    far_count = far_owner.shape[0]
    cap_near = max(2, 4 * near_count // group_size)
    cap_far = max(2, 4 * far_count // group_size)
    slot_count = cap_near + cap_far
    owner_near = near_owner.reshape(-1)
    owner_far = far_owner.reshape(-1)
    rank_near = slot_rank(owner_near)
    flat_near = owner_near * slot_count + rank_near
    flat_far = owner_far * slot_count + cap_near + slot_rank(owner_far)
    corner_slot = owner_near * cap_near + rank_near
    request = jnp.zeros((group_size * slot_count,), jnp.int32)
    request = (
        request.at[flat_near].set(near_local.reshape(-1)).at[flat_far].set(far_local.reshape(-1))
    )
    asked_ids = lax.all_to_all(
        request.reshape(group_size, slot_count), "dev", split_axis=0, concat_axis=0, tiled=True
    )
    asked_near = asked_ids[:, :cap_near]
    one_hot = (
        asked_ids.reshape(-1)[:, None] == lax.broadcasted_iota(jnp.int32, (1, clusters_here), 1)
    ).astype(jnp.float32)
    size_all = float(clusters_here * group_size * 3 * panel_count)

    def near_points(corner_rows):
        flat_corners = corner_rows.reshape((group_size * cap_near,) + corner_rows.shape[2:])
        return jax.vmap(quad_points)(flat_corners[corner_slot])

    corners_here = jax.vmap(panel_corners)(vertices, panels)

    def fetch_data(density):
        received, corner_rows = (
            lax.all_to_all(density[asked_ids], "dev", split_axis=0, concat_axis=0, tiled=True),
            lax.all_to_all(
                corners_here[asked_near], "dev", split_axis=0, concat_axis=0, tiled=True
            ),
        )
        return (received, near_points(corner_rows))

    def product(density):
        received, point_pack = fetch_data(density)
        points_all, weights_all = point_pack
        received_flat = received.reshape(group_size * slot_count, 3, panel_count)
        dense_near = received_flat[flat_near].reshape(near_count, 2, 3, panel_count)
        points_all = points_all.reshape((near_count, 2) + points_all.shape[1:])
        weights_all = weights_all.reshape(near_count, 2, panel_count)
        group_count = near_count // 4

        def grouped(source_array):
            return source_array.reshape((group_count, 4) + source_array.shape[1:])

        def near_group(group_args):
            points_first, weight_first, points_second, weight_second, dense_first, dense_second = (
                group_args
            )
            blocks = jax.vmap(near_block)(points_first, weight_first, points_second, weight_second)
            return jax.vmap(apply_near)(blocks, dense_first, dense_second)

        into_first, into_second = lax.map(
            near_group,
            (
                grouped(points_all[:, 0]),
                grouped(weights_all[:, 0]),
                grouped(points_all[:, 1]),
                grouped(weights_all[:, 1]),
                grouped(dense_near[:, 0]),
                grouped(dense_near[:, 1]),
            ),
        )
        near_terms = jnp.stack(
            [
                into_first.reshape(near_count, 3, panel_count),
                into_second.reshape(near_count, 3, panel_count),
            ],
            axis=1,
        )
        near_terms = near_terms.reshape(2 * near_count, 3, panel_count)
        dense_far = received_flat[flat_far].reshape(far_count, 2, 3 * panel_count)
        far_first, far_second = apply_far(far_left, far_right, dense_far[:, 0], dense_far[:, 1])
        far_terms = jnp.stack([far_first, far_second], axis=1).reshape(
            2 * far_count, 3, panel_count
        )
        outgoing = jnp.zeros((group_size * slot_count, 3, panel_count), jnp.float32)
        outgoing = outgoing.at[flat_near].set(near_terms).at[flat_far].set(far_terms)
        returned = lax.all_to_all(
            outgoing.reshape(group_size, slot_count, 3, panel_count),
            "dev",
            split_axis=0,
            concat_axis=0,
            tiled=True,
        )
        image_sum = jnp.einsum(
            "sc,sk->ck",
            one_hot,
            returned.reshape(group_size * slot_count, 3 * panel_count),
            precision=highest,
        )
        return image_sum.reshape(clusters_here, 3, panel_count)

    def global_mean(pair_list):
        local_sums = jnp.stack([jnp.sum(left_vec * right_vec) for left_vec, right_vec in pair_list])
        return lax.psum(local_sums, "dev") / size_all

    rhs_scale = jnp.sqrt(global_mean([(right_side, right_side)])[0] + norm_eps)
    basis_one = right_side / rhs_scale
    image_one = product(basis_one)
    proj_first = global_mean([(basis_one, image_one)])[0]
    resid_one = image_one - proj_first * basis_one
    norm_first = jnp.sqrt(global_mean([(resid_one, resid_one)])[0] + norm_eps)
    basis_two = resid_one / norm_first
    image_two = product(basis_two)
    both_dots = global_mean([(basis_one, image_two), (basis_two, image_two)])
    proj_cross = both_dots[0]
    proj_second = both_dots[1]
    resid_two = image_two - proj_cross * basis_one - proj_second * basis_two
    norm_second = jnp.sqrt(global_mean([(resid_two, resid_two)])[0] + norm_eps)
    basis_three = resid_two / norm_second
    zero_entry = jnp.zeros((), jnp.float32)
    hessenberg = jnp.stack(
        [
            jnp.stack([proj_first, proj_cross]),
            jnp.stack([norm_first, proj_second]),
            jnp.stack([zero_entry, norm_second]),
        ]
    )
    return (jnp.stack([basis_two, basis_three]), hessenberg)


def solution(mesh):
    in_specs = (
        P("dev", None, None),
        P("dev", None, None),
        P("dev", None, None),
        P("dev", None),
        P("dev", None),
        P("dev", None),
        P("dev", None),
        P("dev", None, None),
        P("dev", None, None),
    )
    out_specs = (P(None, "dev", None, None), P())
    return jax.shard_map(
        per_device, mesh=mesh, in_specs=in_specs, out_specs=out_specs, check_vma=False
    )
```

profile of v0, /device:TPU:0, one launch (start us, length us, event | category | flops | bytes accessed | tf_op | source)
XLA Modules:
  0.0 821.5 jit_solution(12343021288751447077)
XLA Ops:
  10.1 7.3 all-to-all-start
  18.0 40.6 %psum.35 = f32[1]{0:T(128)} all-reduce(f32[1]{0:T(128)} %bitcast.131), channel_id=1, replica_groups=mesh['dev'=32] {'dev'}, use_global_device_ids=true, to_apply=%region_5.6 | all-reduce | flops 1 | bytes 8 | tf_op jit(solution)/shard_map/psum | solution.py:205
  63.4 4.8 all-to-all-start.2
  77.3 11.5 %all-to-all-done.2 = f32[32,16,3,128]{3,1,2,0:T(8,128)} async-done(((f32[32,16,3,128]{3,1,2,0:T(8,128)}), f32[32,16,3,128]{3,1,2,0:T(8,128)}, u32[]{:S(2)}, u32[]{:S(2)}) %all-to-all-start.2) | async-done | bytes 786464 | tf_op jit(solution)/shard_map/all_to_all | solution.py:136
  88.7 4.2 all-to-all-start.1
  93.0 2.7 copy.245
  98.4 2.7 gather_fusion.4
  112.6 9.4 %all-to-all-done.1 = f32[32,8,3,3,128]{4,1,3,2,0:T(8,128)} async-done(((f32[32,8,3,3,128]{4,1,3,2,0:T(8,128)}), f32[32,8,3,3,128]{4,1,3,2,0:T(8,128)}, u32[]{:S(2)}, u32[]{:S(2)}) %all-to-all-start.1) | async-done | bytes 1179680 | tf_op jit(solution)/shard_map/all_to_all | solution.py:137
  121.9 2.9 copy.238
  124.8 3.3 gather_fusion.1
  133.1 196.8 %while.24 = (s32[]{:T(128)}, f32[16,4,3,128]{3,2,1,0:T(4,128)S(1)}, f32[16,4,3,128]{3,2,1,0:T(4,128)}, f32[16,4,128]{2,1,0:T(4,128)}, f32[16,4,128]{2,1,0:T(4,12...) while((s32[]{:T(128)}, f32[16,4,3,128]{3,2,1,0:T(4,128)S(1)}, ...), condition=%wide.region_7.8_spmd, body=%wide.region_6.7_spmd.sunk | while | flops 43057152 | bytes 57729652 | solution.py:162
  333.1 13.3 %scatter_fusion.1 = f32[512,3,128]{2,1,0:T(4,128)} fusion(f32[512,3,128]{2,1,0:T(4,128)} %broadcast.845.clone, s32[128]{0:T(128)S(1)} %get-tuple-element.336, f32[128,3,128]{2,1,0:T(4,128)} %copy.253), kind=kCustom, calls=%fused_computation.10 | custom fusion | bytes 590336 | tf_op jit(solution)/shard_map/scatter | solution.py:187
  346.4 12.5 %scatter_fusion.2 = f32[512,3,128]{2,1,0:T(4,128)} fusion(f32[512,3,128]{2,1,0:T(4,128)} %scatter_fusion.1, s32[128]{0:T(128)S(1)} %fusion.76, f32[128,3,128]{2,1,0:T(4,128)S(1)} %reshape.4437), kind=kCustom, calls=%fused_computation.11 | custom fusion | bytes 590336 | tf_op jit(solution)/shard_map/scatter | solution.py:187
  361.1 3.7 all-to-all-start.3
  366.2 19.3 %all-to-all-done.3 = f32[32,16,3,128]{3,1,2,0:T(8,128)} async-done(((f32[32,16,3,128]{3,1,2,0:T(8,128)}), f32[32,16,3,128]{3,1,2,0:T(8,128)}, u32[]{:S(2)}, u32[]{:S(2)}) %all-to-all-start.3) | async-done | bytes 786464 | tf_op jit(solution)/shard_map/all_to_all | solution.py:188
  388.0 2.3 copy.258
  390.3 2.3 multiply_reduce_fusion.4
  392.7 39.5 %psum.36 = f32[1]{0:T(128)} all-reduce(f32[1]{0:T(128)} %bitcast.157), channel_id=1, replica_groups=mesh['dev'=32] {'dev'}, use_global_device_ids=true, to_apply=%region_11.12 | all-reduce | flops 1 | bytes 8 | tf_op jit(solution)/shard_map/psum | solution.py:205
  433.5 40.4 %psum.37 = f32[1]{0:T(128)} all-reduce(f32[1]{0:T(128)} %bitcast.159), channel_id=1, replica_groups=mesh['dev'=32] {'dev'}, use_global_device_ids=true, to_apply=%region_13.14 | all-reduce | flops 1 | bytes 8 | tf_op jit(solution)/shard_map/psum | solution.py:205
  475.6 2.6 gather_fusion.5
  479.5 25.2 %all_to_all.41 = f32[32,16,3,128]{3,1,2,0:T(8,128)S(1)} all-to-all(f32[32,16,3,128]{3,1,2,0:T(8,128)S(1)} %copy.260), channel_id=1, replica_groups=mesh['dev'=32] {'dev'}, dimensions={0} | all-to-all | bytes 1572864 | tf_op jit(solution)/shard_map/all_to_all | solution.py:136
  506.1 2.8 gather_fusion.7
  510.7 3.2 convolution_bitcast_fusion.1
  516.1 2.7 gather_fusion.6
  522.1 176.4 %while.25 = (s32[]{:T(128)}, f32[16,4,3,128]{3,2,1,0:T(4,128)S(1)}, f32[16,4,3,128]{3,2,1,0:T(4,128)S(1)}, f32[16,4,128]{2,1,0:T(4,128)}, f32[16,4,128]{2,1,0:T(...) while((s32[]{:T(128)}, f32[16,4,3,128]{3,2,1,0:T(4,128)S(1)}, ...), condition=%wide.region_15.16_spmd, body=%wide.region_14.15_spmd.sunk | while | flops 43057152 | bytes 57729144 | solution.py:162
  531.0 2.3 fusion.128
  542.1 2.3 fusion.128
  699.2 4.3 scatter_fusion.3
  703.5 4.3 scatter_fusion.4
  707.9 24.0 %all_to_all.42 = f32[32,16,3,128]{3,1,2,0:T(8,128)S(1)} all-to-all(f32[32,16,3,128]{3,1,2,0:T(8,128)S(1)} %copy.272), channel_id=1, replica_groups=mesh['dev'=32] {'dev'}, dimensions={0} | all-to-all | bytes 1572864 | tf_op jit(solution)/shard_map/all_to_all | solution.py:188
  735.8 39.1 %psum.38 = f32[2]{0:T(128)S(1)} all-reduce(f32[2]{0:T(128)S(1)} %pad_maximum_fusion.7), channel_id=1, replica_groups=mesh['dev'=32] {'dev'}, use_global_device_ids=true, to_apply=%region_20.21 | all-reduce | flops 2 | bytes 16 | tf_op jit(solution)/shard_map/psum | solution.py:205
  778.8 40.2 %psum.39 = f32[1]{0:T(128)} all-reduce(f32[1]{0:T(128)} %bitcast.189), channel_id=1, replica_groups=mesh['dev'=32] {'dev'}, use_global_device_ids=true, to_apply=%region_22.23 | all-reduce | flops 1 | bytes 8 | tf_op jit(solution)/shard_map/psum | solution.py:205
  (755 shorter events, 439.3 us)
Async XLA Ops:
  0.6 103.7 %copy-start = (f32[64,16,384]{2,1,0:T(8,128)S(1)}, f32[64,16,384]{2,1,0:T(8,128)}, u32[]{:S(2)}) copy-start(f32[64,16,384]{2,1,0:T(8,128)} %param.20) | copy-start | bytes 4718596
  0.6 16.8 %copy-start.2 = (f32[64,3,128]{2,0,1:T(8,128)S(1)}, f32[64,3,128]{2,0,1:T(8,128)}, u32[]{:S(2)}) copy-start(f32[64,3,128]{2,0,1:T(8,128)} %param.13) | copy-start | bytes 294916
  10.1 50.0 %all-to-all-start = ((s32[32,1,16]{2,1,0:T(1,128)}), s32[32,1,16]{2,1,0:T(1,128)S(1)}, u32[]{:S(2)}, u32[]{:S(2)}) async-start(s32[32,1,16]{2,1,0:T(1,128)} %bitcast.102), calls=%async_computation | async-start | bytes 32768 | tf_op jit(solution)/shard_map/all_to_all | solution.py:119
  59.4 0.6 copy-start.5
  60.1 14.1 %copy-start.10 = (s32[32,1,16]{2,1,0:T(1,128)}, s32[32,1,16]{2,1,0:T(1,128)S(1)}, u32[]{:S(2)}) copy-start(s32[32,1,16]{2,1,0:T(1,128)S(1)} %all-to-all-done) | copy-start | bytes 6148
  62.3 5.8 copy-start.12
  62.3 5.8 copy-start.15
  63.4 25.4 %all-to-all-start.2 = ((f32[32,16,3,128]{3,1,2,0:T(8,128)}), f32[32,16,3,128]{3,1,2,0:T(8,128)}, u32[]{:S(2)}, u32[]{:S(2)}) async-start(f32[32,16,3,128]{3,1,2,0:T(8,128)} %copy.244), calls=%async_computation.2 | async-start | bytes 1572864 | tf_op jit(solution)/shard_map/all_to_all | solution.py:136
  77.3 15.7 %copy-start.14 = (s32[128]{0:T(128)S(1)}, s32[128]{0:T(128)}, u32[]{:S(2)}) copy-start(s32[128]{0:T(128)} %get-tuple-element.335) | copy-start | bytes 1540
  88.7 33.2 %all-to-all-start.1 = ((f32[32,8,3,3,128]{4,1,3,2,0:T(8,128)}), f32[32,8,3,3,128]{4,1,3,2,0:T(8,128)}, u32[]{:S(2)}, u32[]{:S(2)}) async-start(f32[32,8,3,3,128]{4,1,3,2,0:T(8,128)} %copy.237), calls=%async_computation.1 | async-start | bytes 2359296 | tf_op jit(solution)/shard_map/all_to_all | solution.py:137
  93.0 8.1 copy-start.13
  93.0 9.2 %copy-start.1 = (f32[64,16,384]{2,1,0:T(8,128)S(1)}, f32[64,16,384]{2,1,0:T(8,128)}, u32[]{:S(2)}) copy-start(f32[64,16,384]{2,1,0:T(8,128)} %param.21) | copy-start | bytes 4718596
  358.9 6.5 copy-start.11
  361.1 24.3 %all-to-all-start.3 = ((f32[32,16,3,128]{3,1,2,0:T(8,128)}), f32[32,16,3,128]{3,1,2,0:T(8,128)}, u32[]{:S(2)}, u32[]{:S(2)}) async-start(f32[32,16,3,128]{3,1,2,0:T(8,128)} %copy.256), calls=%async_computation.3 | async-start | bytes 1572864 | tf_op jit(solution)/shard_map/all_to_all | solution.py:188
  387.0 3.3 copy-start.6
  388.0 44.8 %copy-start.3 = (f32[64,3,128]{2,0,1:T(8,128)S(1)}, f32[64,3,128]{2,0,1:T(8,128)}, u32[]{:S(2)}) copy-start(f32[64,3,128]{2,0,1:T(8,128)} %param.13) | copy-start | bytes 294916
  392.7 81.9 %copy-start.9 = (f32[64,3,128]{2,0,1:T(8,128)}, f32[64,3,128]{2,0,1:T(8,128)S(1)}, u32[]{:S(2)}) copy-start(f32[64,3,128]{2,0,1:T(8,128)S(1)} %get-tuple-element.338) | copy-start | bytes 294916
  510.7 3.2 copy-start.4
  520.9 1.0 copy-start.8
  732.3 0.9 copy-start.7
where the time goes:
time: 835 us; the launch traced here: 822 us
  blocking collectives  249 us (30%)
  other arithmetic  196 us (23%)
  local copies, waits for them, and re-layouts  169 us (20%)
  matrix products  141 us (17%)
  waiting for transfers between devices  40.1 us (5%)
  starting transfers between devices  20.1 us (2%)
    psum x5, blocking collectives, global_mean(): return lax.psum(local_sums, 'dev') / size_all  200 us
    mul x192, other arithmetic, near_block(): matrix_row.append(weight_pair * entry_sum)  144 us
    dot_general x32, matrix products, apply_near(): jnp.einsum('ijkl,jl->ik', block_matrix, dense_second, precision=highest)  72.2 us
    dot_general x32, matrix products, apply_near(): jnp.einsum('ijkl,ik->jl', block_matrix, dense_first, precision=highest)  45.4 us
    scatter x4, local copies, waits for them, and re-layouts, product(): outgoing.at[flat_near].set(near_terms).at[flat_far].set(far_terms)  34.4 us
    sub x32, other arithmetic, near_block(): offset = points_first[s][:, :, None] - points_second[t][:, None, :]  30.6 us
    all_to_all x1, blocking collectives, fetch_data(): lax.all_to_all(density[asked_ids], 'dev', split_axis=0, concat_axis=0, ti...  25.2 us
    squeeze x32, local copies, waits for them, and re-layouts, product(): lax.map(near_group, (grouped(points_all[:, 0]), grouped(weights_all[:, 0]...  24.3 us
  transfers between devices with their start and end apart: 4, of which 3 were waited for; matrix products, arithmetic and copies ran while one was open for 4% of the time, Pallas kernels for 0%

commit v1 on v0

v1 whole, which is shorter than its diff:
```python
import jax
import jax.numpy as jnp
from jax import lax
from jax.experimental import pallas as pl
from jax.experimental.pallas import tpu as pltpu
from jax.sharding import PartitionSpec as P

soft_sq = 0.0025
area_floor = 6.25e-06
kelvin_diag = 1.8
norm_eps = 1e-06
big = 2.0 / 3.0
small = 1.0 / 6.0
COMPS = 16
f32 = jnp.float32
VM = pl.BlockSpec(memory_space=pltpu.VMEM)
SM = pl.BlockSpec(memory_space=pltpu.SMEM)


def params(**kw):
    return pltpu.CompilerParams(vmem_limit_bytes=60 << 20, **kw)


def two_sum(a, b):
    s = a + b
    t = s - a
    return s, (a - (s - t)) + (b - t)


def split(a):
    c = a * 4097.0
    hi = c - (c - a)
    return hi, a - hi


def two_prod(a, b):
    p = a * b
    ah, al = split(a)
    bh, bl = split(b)
    return p, ((ah * bh - p) + ah * bl + al * bh) + al * bl


def dd_add(x, y):
    s, e = two_sum(x[0], y[0])
    e = e + (x[1] + y[1])
    hi = s + e
    return hi, e - (hi - s)


def dd_scale(x, f):
    p, e = two_prod(x[0], f)
    e = e + x[1] * f
    hi = p + e
    return hi, e - (hi - p)


def dd_neg(x):
    return -x[0], -x[1]


def prep_kernel(no_ref, nl_ref, fo_ref, fl_ref, ask_ref, idx_ref, *, cap, trash):
    n = ask_ref.shape[0]
    width = 2 * no_ref.shape[1]
    ask = jnp.full(ask_ref.shape, float(trash), f32)
    rows = []
    for part, (o_ref, l_ref) in enumerate(((no_ref, nl_ref), (fo_ref, fl_ref))):
        owner = jnp.concatenate([o_ref[0:1, :], o_ref[1:2, :]], axis=1).astype(f32)
        local = jnp.concatenate([l_ref[0:1, :], l_ref[1:2, :]], axis=1).astype(f32)
        across = jnp.broadcast_to(owner, (width, width))
        down = across.T
        row = lax.broadcasted_iota(jnp.int32, (width, width), 0)
        col = lax.broadcasted_iota(jnp.int32, (width, width), 1)
        earlier = jnp.where((across == down) & (row < col), 1.0, 0.0)
        rank = jnp.sum(earlier, axis=0, keepdims=True)
        dest = lax.broadcasted_iota(jnp.int32, (n, width), 0).astype(f32)
        lhs = jnp.where(dest == owner, local + 1.0, 0.0).astype(jnp.bfloat16)
        slot = lax.broadcasted_iota(jnp.int32, (ask_ref.shape[1], width), 0).astype(f32)
        rhs = jnp.where(slot == rank + float(part * cap), 1.0, 0.0).astype(jnp.bfloat16)
        found = lax.dot_general(
            lhs, rhs, (((1,), (1,)), ((), ())), preferred_element_type=f32
        )
        ask = jnp.where(found > 0.5, found - 1.0, ask)
        rows += [owner, rank]
    ask_ref[...] = ask.astype(jnp.int32)
    idx_ref[...] = jnp.concatenate(rows + rows, axis=0).astype(jnp.int32)


def pack_kernel(ask_ref, x_ref, v_ref, p_ref, near_ref, far_ref, pan_ref, *, cap):
    n = near_ref.shape[0]
    last = x_ref.shape[1] - 1
    pan_ref[...] = p_ref[...].astype(f32)

    def body(d, _):
        for s in range(cap):
            c = jnp.minimum(ask_ref[d, cap + s], last)
            for i in range(3):
                far_ref[d, i, pl.ds(s, 1), :] = x_ref[i, pl.ds(c, 1), :]
        for s in range(cap):
            c = jnp.minimum(ask_ref[d, s], last)
            for i in range(3):
                near_ref[d, i, pl.ds(s, 1), :] = v_ref[i, pl.ds(c, 1), :]
                near_ref[d, 3 + i, pl.ds(s, 1), :] = pan_ref[i, pl.ds(c, 1), :]
                near_ref[d, 6 + i, pl.ds(s, 1), :] = x_ref[i, pl.ds(c, 1), :]
        return 0

    lax.fori_loop(0, n, body, 0)


def far_kernel(idx_ref, x_ref, l_ref, r_ref, out_ref):
    count = l_ref.shape[0]

    def body(f, _):
        oa, ra = idx_ref[2, f], idx_ref[3, f]
        ob, rb = idx_ref[2, count + f], idx_ref[3, count + f]
        left = [l_ref[f, :, pl.ds(128 * i, 128)] for i in range(3)]
        right = [r_ref[f, :, pl.ds(128 * i, 128)] for i in range(3)]
        xa = [x_ref[oa, i, pl.ds(ra, 1), :] for i in range(3)]
        xb = [x_ref[ob, i, pl.ds(rb, 1), :] for i in range(3)]
        coef_b = jnp.sum(sum(right[i] * xb[i] for i in range(3)), axis=1, keepdims=True)
        coef_a = jnp.sum(sum(left[i] * xa[i] for i in range(3)), axis=1, keepdims=True)
        for i in range(3):
            out_ref[oa, i, pl.ds(ra, 1), :] = jnp.sum(left[i] * coef_b, axis=0, keepdims=True)
            out_ref[ob, i, pl.ds(rb, 1), :] = jnp.sum(right[i] * coef_a, axis=0, keepdims=True)
        return 0

    lax.fori_loop(0, count, body, 0, unroll=4)


def slot_geometry(in_ref, geo_ref, *, cap):
    n = in_ref.shape[0]

    def body(d, _):
        corner = []
        for m in range(3):
            pick = in_ref[d, 3 + m].astype(jnp.int32)
            corner.append(
                [jnp.take_along_axis(in_ref[d, i], pick, axis=1) for i in range(3)]
            )
        e1 = [corner[1][i] - corner[0][i] for i in range(3)]
        e2 = [corner[2][i] - corner[0][i] for i in range(3)]
        cx = e1[1] * e2[2] - e1[2] * e2[1]
        cy = e1[2] * e2[0] - e1[0] * e2[2]
        cz = e1[0] * e2[1] - e1[1] * e2[0]
        weight = jnp.sqrt(cx * cx + cy * cy + cz * cz + area_floor) / 6.0
        for s in range(3):
            for i in range(3):
                point = sum((big if m == s else small) * corner[m][i] for m in range(3))
                geo_ref[d, pl.ds((3 * s + i) * cap, cap), :] = point
        for i in range(3):
            geo_ref[d, pl.ds((9 + i) * cap, cap), :] = weight * in_ref[d, 6 + i]
        geo_ref[d, pl.ds(12 * cap, cap), :] = weight
        return 0

    lax.fori_loop(0, n, body, 0)


def to_columns(geo_ref, col_ref):
    def body(d, _):
        col_ref[d] = geo_ref[d].T
        return 0

    lax.fori_loop(0, geo_ref.shape[0], body, 0)


def spread(tile, lane):
    return jnp.take_along_axis(tile, jnp.full(tile.shape, lane, jnp.int32), axis=1)


def apply_tile(mats, ya, yb, second):
    kxx, kxy, kxz, kyy, kyz, kzz = mats
    full = ((kxx, kxy, kxz), (kxy, kyy, kyz), (kxz, kyz, kzz))
    firsts = [full[i][0] * yb[0] + full[i][1] * yb[1] + full[i][2] * yb[2] for i in range(3)]
    second = [
        second[j] + (full[0][j] * ya[0] + full[1][j] * ya[1] + full[2][j] * ya[2])
        for j in range(3)
    ]
    return [jnp.sum(t, axis=1, keepdims=True) for t in firsts], second


def keep_first(first_ref, sums, pair, t):
    block = pair // 32
    lane0 = (pair % 32) * 4
    lane = lax.broadcasted_iota(jnp.int32, (8, 128), 1)
    tile = first_ref[block, pl.ds(8 * t, 8), :]
    for i in range(3):
        tile = jnp.where(lane == lane0 + i, sums[i], tile)
    first_ref[block, pl.ds(8 * t, 8), :] = tile


def return_terms(idx_ref, first_ref, second_ref, weight_row, out_ref, *, count):
    blocks = first_ref.shape[0]
    for b in range(blocks):
        first_ref[b] = first_ref[b].T

    def body(p, _):
        oa, ra = idx_ref[0, p], idx_ref[1, p]
        ob, rb = idx_ref[0, count + p], idx_ref[1, count + p]
        wa = weight_row(oa, ra)
        wb = weight_row(ob, rb)
        for i in range(3):
            out_ref[oa, i, pl.ds(ra, 1), :] = (
                wa * first_ref[p // 32, pl.ds((p % 32) * 4 + i, 1), :]
            )
            out_ref[ob, i, pl.ds(rb, 1), :] = wb * jnp.sum(
                second_ref[p, i], axis=0, keepdims=True
            )
        return 0

    lax.fori_loop(0, count, body, 0, unroll=2)


def build_kernel(
    idx_ref, in_ref, k_ref, out_ref, w_ref, geo_ref, col_ref, first_ref, second_ref, *, cap, count
):
    step = pl.program_id(0)
    group = k_ref.shape[0]
    n = in_ref.shape[0]

    @pl.when(step == 0)
    def _():
        slot_geometry(in_ref, geo_ref, cap=cap)
        to_columns(geo_ref, col_ref)
        w_ref[...] = geo_ref[:, pl.ds(12 * cap, cap), :]

    def pair_body(g, _):
        pair = step * group + g
        oa, ra = idx_ref[0, pair], idx_ref[1, pair]
        ob, rb = idx_ref[0, count + pair], idx_ref[1, count + pair]
        row = [
            jnp.broadcast_to(geo_ref[ob, pl.ds(c * cap + rb, 1), :], (8, 128)) for c in range(12)
        ]

        def tile_body(t, second):
            cols = col_ref[oa, pl.ds(8 * t, 8), :]
            col = [spread(cols, c * cap + ra) for c in range(12)]
            su = sv = xx = xy = xz = yy = yz = None
            for s in range(3):
                for q in range(3):
                    x = col[3 * s] - row[3 * q]
                    y = col[3 * s + 1] - row[3 * q + 1]
                    z = col[3 * s + 2] - row[3 * q + 2]
                    u = lax.rsqrt(x * x + y * y + z * z + soft_sq)
                    v = u * u * u
                    vx = v * x
                    vy = v * y
                    if su is None:
                        su, sv = u, v
                        xx, xy, xz, yy, yz = vx * x, vx * y, vx * z, vy * y, vy * z
                    else:
                        su, sv = su + u, sv + v
                        xx, xy, xz = xx + vx * x, xy + vx * y, xz + vx * z
                        yy, yz = yy + vy * y, yz + vy * z
            zz = su - soft_sq * sv - xx - yy
            diag = kelvin_diag * su
            mats = (xx + diag, xy, xz, yy + diag, yz, zz + diag)
            for m in range(6):
                k_ref[g, m, pl.ds(8 * t, 8), :] = mats[m]
            sums, second = apply_tile(mats, col[9:12], row[9:12], second)
            keep_first(first_ref, sums, pair, t)
            return second

        zero = jnp.zeros((8, 128), f32)
        second = lax.fori_loop(0, 16, tile_body, [zero, zero, zero])
        for i in range(3):
            second_ref[pair, i] = second[i]
        return 0

    lax.fori_loop(0, group, pair_body, 0)

    @pl.when(step == pl.num_programs(0) - 1)
    def _():
        return_terms(
            idx_ref,
            first_ref,
            second_ref,
            lambda o, r: w_ref[o, pl.ds(r, 1), :],
            out_ref,
            count=count,
        )


def apply_kernel(
    idx_ref, x_ref, w_ref, k_ref, out_ref, geo_ref, col_ref, first_ref, second_ref, *, cap, count
):
    step = pl.program_id(0)
    group = k_ref.shape[0]
    n = x_ref.shape[0]

    @pl.when(step == 0)
    def _():

        def body(d, _):
            for i in range(3):
                geo_ref[d, pl.ds(i * cap, cap), :] = w_ref[d] * x_ref[d, i]
            return 0

        lax.fori_loop(0, n, body, 0)
        to_columns(geo_ref, col_ref)

    def pair_body(g, _):
        pair = step * group + g
        oa, ra = idx_ref[0, pair], idx_ref[1, pair]
        ob, rb = idx_ref[0, count + pair], idx_ref[1, count + pair]
        row = [
            jnp.broadcast_to(geo_ref[ob, pl.ds(c * cap + rb, 1), :], (8, 128)) for c in range(3)
        ]

        def tile_body(t, second):
            cols = col_ref[oa, pl.ds(8 * t, 8), :]
            col = [spread(cols, c * cap + ra) for c in range(3)]
            mats = [k_ref[g, m, pl.ds(8 * t, 8), :] for m in range(6)]
            sums, second = apply_tile(mats, col, row, second)
            keep_first(first_ref, sums, pair, t)
            return second

        zero = jnp.zeros((8, 128), f32)
        second = lax.fori_loop(0, 16, tile_body, [zero, zero, zero], unroll=4)
        for i in range(3):
            second_ref[pair, i] = second[i]
        return 0

    lax.fori_loop(0, group, pair_body, 0)

    @pl.when(step == pl.num_programs(0) - 1)
    def _():
        return_terms(
            idx_ref,
            first_ref,
            second_ref,
            lambda o, r: w_ref[o, pl.ds(r, 1), :],
            out_ref,
            count=count,
        )


def add_up(ask_ref, near_ref, far_ref, accs, out_ref, *, cap):
    clusters = out_ref.shape[1]
    for acc in accs:
        acc[...] = jnp.zeros(acc.shape, f32)

    def body(d, _):
        for s in range(cap):
            cn = ask_ref[d, s]
            cf = ask_ref[d, cap + s]
            for i in range(3):
                accs[i][pl.ds(cn, 1), :] += near_ref[d, i, pl.ds(s, 1), :]
                accs[3 + i][pl.ds(cf, 1), :] += far_ref[d, i, pl.ds(s, 1), :]
        return 0

    lax.fori_loop(0, near_ref.shape[0], body, 0)
    for i in range(3):
        out_ref[i] = accs[i][pl.ds(0, clusters), :] + accs[3 + i][pl.ds(0, clusters), :]


def merge_kernel(ask_ref, rn_ref, rf_ref, out_ref, near_ref, far_ref, *accs, cap):
    add_up(ask_ref, rn_ref, rf_ref, accs, out_ref, cap=cap)
    last = out_ref.shape[1] - 1

    def body(d, _):
        for s in range(cap):
            cn = jnp.minimum(ask_ref[d, s], last)
            cf = jnp.minimum(ask_ref[d, cap + s], last)
            for i in range(3):
                near_ref[d, i, pl.ds(s, 1), :] = out_ref[i, pl.ds(cn, 1), :]
                far_ref[d, i, pl.ds(s, 1), :] = out_ref[i, pl.ds(cf, 1), :]
        return 0

    lax.fori_loop(0, near_ref.shape[0], body, 0)


PRODUCTS = ((0, 0), (0, 1), (1, 1), (0, 2), (1, 2), (2, 2))


def gram_kernel(ask_ref, rn_ref, rf_ref, v0_ref, v1_ref, out_ref, part_ref, *accs, cap):
    add_up(ask_ref, rn_ref, rf_ref, accs, out_ref, cap=cap)
    clusters = out_ref.shape[1]
    refs = (v0_ref, v1_ref, out_ref)
    zero = jnp.zeros((8, 128), f32)
    totals = [(zero, zero)] * 6
    for i in range(3):

        def body(t, totals):
            tiles = [ref[i, pl.ds(8 * t, 8), :] for ref in refs]
            halves = [split(tile) for tile in tiles]
            new = []
            for k, (a, b) in enumerate(PRODUCTS):
                (ah, al), (bh, bl) = halves[a], halves[b]
                p = tiles[a] * tiles[b]
                e = ((ah * bh - p) + ah * bl + al * bh) + al * bl
                hi, lo = totals[k]
                s, err = two_sum(hi, p)
                new.append((s, lo + (err + e)))
            return new

        totals = lax.fori_loop(0, clusters // 8, body, totals)
    hi = jnp.concatenate([t[0] for t in totals], axis=0)
    lo = jnp.concatenate([t[1] for t in totals], axis=0)
    for shift in (64, 32, 16, 8, 4, 2, 1):
        hi, lo = dd_add((hi, lo), (pltpu.roll(hi, shift, 1), pltpu.roll(lo, shift, 1)))
    lane = lax.broadcasted_iota(jnp.int32, (8, 128), 1)
    shi = slo = zero
    for k in range(6):
        shi = jnp.where(lane == k, hi[8 * k : 8 * k + 8], shi)
        slo = jnp.where(lane == k, lo[8 * k : 8 * k + 8], slo)
    for shift in (4, 2, 1):
        shi, slo = dd_add((shi, slo), (pltpu.roll(shi, shift, 0), pltpu.roll(slo, shift, 0)))
    packed = jnp.where(lane < 8, shi, pltpu.roll(slo, 8, 1))
    part_ref[...] = jnp.broadcast_to(packed[0:1, :], part_ref.shape)


def final_kernel(part_ref, v0_ref, v1_ref, v2_ref, basis_ref, hess_ref, *, size_all):
    hi = part_ref[...]
    lo = pltpu.roll(hi, 120, 1)
    rows = hi.shape[0]
    while rows > 1:
        half = rows // 2
        hi, lo = dd_add((hi[:half], lo[:half]), (hi[half:], lo[half:]))
        rows = half
    inv = 1.0 / size_all
    hi, lo = dd_scale((hi, lo), jnp.full(hi.shape, inv, f32)) if size_all & (size_all - 1) == 0 else dd_div_const(hi, lo, size_all)
    g = [(hi[:, k : k + 1], lo[:, k : k + 1]) for k in range(6)]
    g00, g01, g11, g02, g12, g22 = g
    eps = jnp.full((1, 1), norm_eps, f32)
    none = jnp.zeros((1, 1), f32)
    s2 = dd_add(g00, (eps, none))
    s = jnp.sqrt(s2[0])
    p = g01[0] / s2[0]
    r1 = dd_add(g11, dd_scale(dd_add(dd_scale(g00, p), dd_scale(g01, none - 2.0)), p))
    nf = jnp.sqrt(jnp.maximum(r1[0], 0.0) / s2[0] + norm_eps)
    snf = s * nf
    c0 = dd_add(g02, dd_scale(g01, -p))
    pc = c0[0] / (s2[0] * nf)
    c1 = dd_add(dd_add(g12, dd_scale(g11, -p)), dd_scale(c0, -p))
    ps = c1[0] / (s2[0] * nf * nf)
    a1 = -(p + ps)
    a0 = ps * p - pc * nf
    t2 = dd_add(g22, dd_scale(dd_add(dd_scale(g12, a1), dd_scale(g02, a0)), none + 2.0))
    t1 = dd_scale(dd_add(dd_scale(g11, a1), dd_scale(g01, 2.0 * a0)), a1)
    t0 = dd_scale(dd_scale(g00, a0), a0)
    w2 = dd_add(dd_add(t2, t1), t0)
    n2 = jnp.sqrt(jnp.maximum(w2[0], 0.0) / (snf * snf) + norm_eps)
    k1 = 1.0 / snf
    k2 = 1.0 / (snf * n2)
    for i in range(3):
        v0, v1, v2 = v0_ref[i], v1_ref[i], v2_ref[i]
        basis_ref[0, i] = (v1 - p * v0) * k1
        basis_ref[1, i] = (v2 + a1 * v1 + a0 * v0) * k2
    top = jnp.concatenate([p, nf, none], axis=1)
    bottom = jnp.concatenate([pc, ps, n2], axis=1)
    hess_ref[...] = jnp.concatenate([top, bottom], axis=0)


def dd_div_const(hi, lo, size_all):
    d = jnp.full(hi.shape, float(size_all), f32)
    q = hi / d
    p, e = two_prod(q, d)
    rest = ((hi - p) - e) + lo
    return q, rest / d


def per_device(
    right_side, vertices, panels, near_owner, near_local, far_owner, far_local, far_left, far_right
):
    n = lax.axis_size("dev")
    clusters, _, width = right_side.shape
    near_count = near_owner.shape[0]
    far_count = far_owner.shape[0]
    cap = max(2, 4 * near_count // n)
    size_all = clusters * n * 3 * width
    x0 = right_side.transpose(1, 0, 2)
    shape = jax.ShapeDtypeStruct

    def exchange(block):
        return lax.all_to_all(block, "dev", split_axis=0, concat_axis=0, tiled=True)

    slots = max(128, 2 * cap)
    ask, idx = pl.pallas_call(
        lambda *refs: prep_kernel(*refs, cap=cap, trash=clusters),
        out_shape=(shape((n, slots), jnp.int32), shape((8, 2 * near_count), jnp.int32)),
        compiler_params=params(),
        name="prep",
    )(near_owner.T, near_local.T, far_owner.T, far_local.T)
    asked = exchange(ask)

    near_out, far_out = pl.pallas_call(
        lambda *refs: pack_kernel(*refs, cap=cap),
        out_shape=(shape((n, 9, cap, width), f32), shape((n, 3, cap, width), f32)),
        in_specs=[SM, VM, VM, VM],
        scratch_shapes=[pltpu.VMEM((3, clusters, width), f32)],
        compiler_params=params(),
        name="pack",
    )(asked, x0, vertices.transpose(1, 0, 2), panels.transpose(1, 0, 2))

    def far_product(received):
        return pl.pallas_call(
            far_kernel,
            out_shape=shape((n, 3, cap, width), f32),
            in_specs=[SM, VM, VM, VM],
            compiler_params=params(),
            name="far",
        )(idx, received, far_left, far_right)

    far_in = exchange(far_out)
    near_in = exchange(near_out)
    far_back = exchange(far_product(far_in))

    group = 4
    steps = near_count // group
    blocks = -(-near_count // 32)
    rows = -(-13 * cap // 128) * 128
    k_spec = pl.BlockSpec((group, 6, width, width), lambda g: (g, 0, 0, 0))

    def whole(*dims):
        return pl.BlockSpec(dims, lambda g: (0,) * len(dims))

    scratch = [
        pltpu.VMEM((n, rows, width), f32),
        pltpu.VMEM((n, width, rows), f32),
        pltpu.VMEM((blocks, width, 128), f32),
        pltpu.VMEM((near_count, 3, 8, width), f32),
    ]
    stored, near_terms, weights = pl.pallas_call(
        lambda *refs: build_kernel(*refs, cap=cap, count=near_count),
        out_shape=(
            shape((near_count, 6, width, width), f32),
            shape((n, 3, cap, width), f32),
            shape((n, cap, width), f32),
        ),
        grid=(steps,),
        in_specs=[SM, whole(n, 9, cap, width)],
        out_specs=(k_spec, whole(n, 3, cap, width), whole(n, cap, width)),
        scratch_shapes=scratch,
        compiler_params=params(),
        name="build",
    )(idx, near_in)
    near_back = exchange(near_terms)

    accs = [pltpu.VMEM((clusters + 8, width), f32)] * 6
    x1, near_out2, far_out2 = pl.pallas_call(
        lambda *refs: merge_kernel(*refs, cap=cap),
        out_shape=(
            shape((3, clusters, width), f32),
            shape((n, 3, cap, width), f32),
            shape((n, 3, cap, width), f32),
        ),
        in_specs=[SM, VM, VM],
        scratch_shapes=accs,
        compiler_params=params(),
        name="merge",
    )(asked, near_back, far_back)
    far_in2 = exchange(far_out2)
    near_in2 = exchange(near_out2)
    far_back2 = exchange(far_product(far_in2))
    rows2 = 128
    scratch2 = [
        pltpu.VMEM((n, rows2, width), f32),
        pltpu.VMEM((n, width, rows2), f32),
        pltpu.VMEM((blocks, width, 128), f32),
        pltpu.VMEM((near_count, 3, 8, width), f32),
    ]
    near_terms2 = pl.pallas_call(
        lambda *refs: apply_kernel(*refs, cap=cap, count=near_count),
        out_shape=shape((n, 3, cap, width), f32),
        grid=(steps,),
        in_specs=[SM, whole(n, 3, cap, width), whole(n, cap, width), k_spec],
        out_specs=whole(n, 3, cap, width),
        scratch_shapes=scratch2,
        compiler_params=params(),
        name="apply",
    )(idx, near_in2, weights, stored)
    near_back2 = exchange(near_terms2)

    x2, part = pl.pallas_call(
        lambda *refs: gram_kernel(*refs, cap=cap),
        out_shape=(shape((3, clusters, width), f32), shape((n, 128), f32)),
        in_specs=[SM, VM, VM, VM, VM],
        scratch_shapes=accs,
        compiler_params=params(),
        name="gram",
    )(asked, near_back2, far_back2, x0, x1)
    parts = exchange(part)
    basis, hess = pl.pallas_call(
        lambda *refs: final_kernel(*refs, size_all=size_all),
        out_shape=(shape((2, 3, clusters, width), f32), shape((2, 3), f32)),
        compiler_params=params(),
        name="final",
    )(parts, x0, x1, x2)
    return (basis.transpose(0, 2, 1, 3), hess.T)


def solution(mesh):
    per_cluster = P("dev", None, None)
    per_pair = P("dev", None)
    in_specs = (per_cluster,) * 3 + (per_pair,) * 4 + (per_cluster,) * 2
    out_specs = (P(None, "dev", None, None), P())
    return jax.shard_map(
        per_device, mesh=mesh, in_specs=in_specs, out_specs=out_specs, check_vma=False
    )
```

time: 835 us -> 468 us (0.56); the launches traced: 822 us -> 467 us
  Pallas kernels: 0 us -> 325 us
  other arithmetic: 196 us -> 0 us
  local copies, waits for them, and re-layouts: 169 us -> 0.02 us
  blocking collectives: 249 us -> 93.5 us
  matrix products: 141 us -> 0 us
    pallas_call x0 -> x9, Pallas kernels: none -> 325 us  [the longest x1 242 us: per_device(): pl.pallas_call(lambda *refs: build_kernel(*refs, cap=cap, count=near_coun...]
    psum x5 -> x0, blocking collectives: 200 us -> none  [global_mean(): return lax.psum(local_sums, 'dev') / size_all]
    mul x193 -> x0, other arithmetic: 145 us -> none  [the longest x192 144 us: near_block(): matrix_row.append(weight_pair * entry_sum)]
    dot_general x77 -> x0, matrix products: 141 us -> none  [the longest x32 72.2 us: apply_near(): jnp.einsum('ijkl,jl->ik', block_matrix, dense_second, precision=highest)]
    all_to_all x2 -> x6, blocking collectives: 49.2 us -> 93.5 us  [exchange(): return lax.all_to_all(block, 'dev', split_axis=0, concat_axis=0, tiled=True)]
    scatter x6 -> x0, local copies, waits for them, and re-layouts: 36.4 us -> none  [the longest x4 34.4 us: product(): outgoing.at[flat_near].set(near_terms).at[flat_far].set(far_terms)]
    sub x32 -> x0, other arithmetic: 30.6 us -> none  [near_block(): offset = points_first[s][:, :, None] - points_second[t][:, None, :]]
    squeeze x32 -> x0, local copies, waits for them, and re-layouts: 24.3 us -> none  [product(): lax.map(near_group, (grouped(points_all[:, 0]), grouped(weights_all[:, 0]...]
  transfers between devices with their start and end apart: 4 -> 4, of which waited for: 3 -> 2; matrix products, arithmetic and copies ran while one was open for 4% -> 0% of each run, Pallas kernels for 0% -> 66%
where the time goes in v1:
time: 468 us; the launch traced here: 467 us
  Pallas kernels  325 us (69%)
  blocking collectives  93.5 us (20%)
  waiting for transfers between devices  32.8 us (7%)
  starting transfers between devices  14.6 us (3%)
    pallas_call x1, Pallas kernels, per_device(): pl.pallas_call(lambda *refs: build_kernel(*refs, cap=cap, count=near_coun...  242 us
    all_to_all x6, blocking collectives, exchange(): return lax.all_to_all(block, 'dev', split_axis=0, concat_axis=0, tiled=True)  93.5 us
    pallas_call x1, Pallas kernels, per_device(): pl.pallas_call(lambda *refs: apply_kernel(*refs, cap=cap, count=near_coun...  55.7 us
    all_to_all x4, waiting for transfers between devices, exchange(): return lax.all_to_all(block, 'dev', split_axis=0, concat_axis=0, tiled=True)  32.8 us
    all_to_all x4, starting transfers between devices, exchange(): return lax.all_to_all(block, 'dev', split_axis=0, concat_axis=0, tiled=True)  14.6 us
    pallas_call x2, Pallas kernels, far_product(): pl.pallas_call(far_kernel, out_shape=shape((n, 3, cap, width), f32), in_s...  9.43 us
  transfers between devices with their start and end apart: 4, of which 2 were waited for; matrix products, arithmetic and copies ran while one was open for 0% of the time, Pallas kernels for 66%

profile of v1, /device:TPU:0, one launch (start us, length us, event | category | flops | bytes accessed | tf_op | source)
XLA Modules:
  0.0 467.1 jit_solution(2192103622555362417)
XLA Ops:
  0.6 1.7 prep.1
  2.3 14.5 %all_to_all.62 = s32[32,1,128]{2,1,0:T(1,128)} all-to-all(s32[32,1,128]{2,1,0:T(1,128)} %bitcast.27), channel_id=1, replica_groups=mesh['dev'=32] {'dev'}, dimensions={0} | all-to-all | bytes 32768 | tf_op jit(solution)/shard_map/all_to_all | solution.py:474
  16.8 4.1 pack.1
  20.9 16.5 %all_to_all.63.x_ref = f32[32,3,8,128]{3,2,1,0:T(8,128)} all-to-all(f32[32,3,8,128]{3,2,1,0:T(8,128)} %get-tuple-element.20), channel_id=1, replica_groups=mesh['dev'=32] {'dev'}, dimensions={0} | all-to-all | bytes 786432 | tf_op jit(solution)/shard_map/all_to_all | solution.py:474
  37.5 2.7 all-to-all-start.1
  40.1 4.7 %far.2 = f32[32,3,8,128]{3,2,1,0:T(8,128)} custom-call(s32[8,128]{1,0:T(8,128)} %get-tuple-element.17.refs_0_.idx_ref, f32[32,3,8,128]{3,2,1,0:T(8,128)} %all_to_all.63.x_ref, f32[64,16,384]{2,1,0:T(8,128)} %l_ref.3, f32[64,16,384]{2,1,0:T(8,128)} %r_ref.3), custom_call_target="tpu_custom_call" | custom-call | tf_op jit(solution)/shard_map/far/pallas_call | solution.py:495
  44.9 24.3 %all-to-all-done.1.refs_1_ = f32[32,9,8,128]{3,2,1,0:T(8,128)S(1)} async-done(((f32[32,9,8,128]{3,2,1,0:T(8,128)}), f32[32,9,8,128]{3,2,1,0:T(8,128)S(1)}, u32[]{:S(2)}, u32[]{:S(2)}) %all-to-all-start.1) | async-done | bytes 1179680 | tf_op jit(solution)/shard_map/all_to_all | solution.py:474
  69.1 0.0 copy-start
  69.1 3.5 all-to-all-start.4
  72.7 0.0 copy-done
  72.7 242.0 %build.1 = (f32[64,6,128,128]{3,2,1,0:T(8,128)}, f32[32,3,8,128]{3,2,1,0:T(8,128)}, f32[32,8,128]{2,1,0:T(8,128)}) custom-call(s32[8,128]{1,0:T(8,128)} %get-tuple-element.17.refs_0_.idx_ref, f32[32,9,8,128]{3,2,1,0:T(8,128)} %copy-done), custom_call_target="tpu_custom_call" | custom-call | tf_op jit(solution)/shard_map/build/pallas_call | solution.py:522
  314.7 0.0 all-to-all-done.4.refs_2_
  314.7 0.0 copy-start.2
  314.7 19.2 %all_to_all.64.refs_1_ = f32[32,3,8,128]{3,2,1,0:T(8,128)} all-to-all(f32[32,3,8,128]{3,2,1,0:T(8,128)} %get-tuple-element.19), channel_id=1, replica_groups=mesh['dev'=32] {'dev'}, dimensions={0} | all-to-all | bytes 786432 | tf_op jit(solution)/shard_map/all_to_all | solution.py:474
  333.9 0.0 copy-done.2
  333.9 4.6 merge.1
  338.5 16.5 %all_to_all.65.refs_1_ = f32[32,3,8,128]{3,2,1,0:T(8,128)} all-to-all(f32[32,3,8,128]{3,2,1,0:T(8,128)} %get-tuple-element.21), channel_id=1, replica_groups=mesh['dev'=32] {'dev'}, dimensions={0} | all-to-all | bytes 786432 | tf_op jit(solution)/shard_map/all_to_all | solution.py:474
  355.1 2.6 all-to-all-start.7
  357.7 55.7 %apply.1 = f32[32,3,8,128]{3,2,1,0:T(8,128)} custom-call(s32[8,128]{1,0:T(8,128)} %get-tuple-element.17.refs_0_.idx_ref, f32[32,3,8,128]{3,2,1,0:T(8,128)} %all_to_all.65.refs_1_, f32[32,8,128]{2,1,0:T(8,128)} %get-tuple-element.22.refs_2_, f32[64,6,128,128]{3,2,1,0:T(8,128)} %get-tuple-element.23.refs_3_), custom_call_target="tpu_custom_call" | custom-call | tf_op jit(solution)/shard_map/apply/pallas_call | solution.py:561
  413.4 0.0 all-to-all-done.7.x_ref
  413.4 0.0 copy-start.1
  413.4 5.8 %all-to-all-start.6 = ((f32[32,3,8,128]{3,2,1,0:T(8,128)}), f32[32,3,8,128]{3,2,1,0:T(8,128)S(1)}, u32[]{:S(2)}, u32[]{:S(2)}) async-start(f32[32,3,8,128]{3,2,1,0:T(8,128)} %apply.1), calls=%async_computation.6 | async-start | bytes 786432 | tf_op jit(solution)/shard_map/all_to_all | solution.py:474
  419.2 0.0 copy-done.1
  419.2 4.7 %far.3 = f32[32,3,8,128]{3,2,1,0:T(8,128)} custom-call(s32[8,128]{1,0:T(8,128)} %get-tuple-element.17.refs_0_.idx_ref, f32[32,3,8,128]{3,2,1,0:T(8,128)} %copy-done.1, f32[64,16,384]{2,1,0:T(8,128)} %l_ref.3, f32[64,16,384]{2,1,0:T(8,128)} %r_ref.3), custom_call_target="tpu_custom_call" | custom-call | tf_op jit(solution)/shard_map/far/pallas_call | solution.py:495
  423.9 8.5 %all-to-all-done.6.refs_1_ = f32[32,3,8,128]{3,2,1,0:T(8,128)S(1)} async-done(((f32[32,3,8,128]{3,2,1,0:T(8,128)}), f32[32,3,8,128]{3,2,1,0:T(8,128)S(1)}, u32[]{:S(2)}, u32[]{:S(2)}) %all-to-all-start.6) | async-done | bytes 393248 | tf_op jit(solution)/shard_map/all_to_all | solution.py:474
  432.5 0.0 copy-start.3
  432.5 16.5 %all_to_all.66.refs_2_ = f32[32,3,8,128]{3,2,1,0:T(8,128)} all-to-all(f32[32,3,8,128]{3,2,1,0:T(8,128)} %far.3), channel_id=1, replica_groups=mesh['dev'=32] {'dev'}, dimensions={0} | all-to-all | bytes 786432 | tf_op jit(solution)/shard_map/all_to_all | solution.py:474
  449.0 0.0 copy-done.3
  449.0 4.5 gram.1
  453.5 10.2 %all_to_all.67 = f32[32,1,128]{2,1,0:T(1,128)} all-to-all(f32[32,1,128]{2,1,0:T(1,128)} %bitcast.26), channel_id=1, replica_groups=mesh['dev'=32] {'dev'}, dimensions={0} | all-to-all | bytes 32768 | tf_op jit(solution)/shard_map/all_to_all | solution.py:474
  463.7 3.5 final.1
Async XLA Ops:
  37.5 31.7 %all-to-all-start.1 = ((f32[32,9,8,128]{3,2,1,0:T(8,128)}), f32[32,9,8,128]{3,2,1,0:T(8,128)S(1)}, u32[]{:S(2)}, u32[]{:S(2)}) async-start(f32[32,9,8,128]{3,2,1,0:T(8,128)} %get-tuple-element.18), calls=%async_computation.1 | async-start | bytes 2359296 | tf_op jit(solution)/shard_map/all_to_all | solution.py:474
  69.1 3.6 copy-start
  69.1 245.6 %all-to-all-start.4 = ((f32[32,3,8,128]{3,2,1,0:T(8,128)}), f32[32,3,8,128]{3,2,1,0:T(8,128)S(1)}, u32[]{:S(2)}, u32[]{:S(2)}) async-start(f32[32,3,8,128]{3,2,1,0:T(8,128)} %far.2), calls=%async_computation.4 | async-start | bytes 786432 | tf_op jit(solution)/shard_map/all_to_all | solution.py:474
  314.7 19.2 %copy-start.2 = (f32[32,3,8,128]{3,2,1,0:T(8,128)}, f32[32,3,8,128]{3,2,1,0:T(8,128)S(1)}, u32[]{:S(2)}) copy-start(f32[32,3,8,128]{3,2,1,0:T(8,128)S(1)} %all-to-all-done.4.refs_2_) | copy-start | bytes 1179652
  355.1 58.3 %all-to-all-start.7 = ((f32[32,3,8,128]{3,2,1,0:T(8,128)}), f32[32,3,8,128]{3,2,1,0:T(8,128)S(1)}, u32[]{:S(2)}, u32[]{:S(2)}) async-start(f32[32,3,8,128]{3,2,1,0:T(8,128)} %get-tuple-element.24), calls=%async_computation.7 | async-start | bytes 786432 | tf_op jit(solution)/shard_map/all_to_all | solution.py:474
  413.4 5.8 %copy-start.1 = (f32[32,3,8,128]{3,2,1,0:T(8,128)}, f32[32,3,8,128]{3,2,1,0:T(8,128)S(1)}, u32[]{:S(2)}) copy-start(f32[32,3,8,128]{3,2,1,0:T(8,128)S(1)} %all-to-all-done.7.x_ref) | copy-start | bytes 1179652
  413.4 19.1 %all-to-all-start.6 = ((f32[32,3,8,128]{3,2,1,0:T(8,128)}), f32[32,3,8,128]{3,2,1,0:T(8,128)S(1)}, u32[]{:S(2)}, u32[]{:S(2)}) async-start(f32[32,3,8,128]{3,2,1,0:T(8,128)} %apply.1), calls=%async_computation.6 | async-start | bytes 786432 | tf_op jit(solution)/shard_map/all_to_all | solution.py:474
  432.5 16.5 %copy-start.3 = (f32[32,3,8,128]{3,2,1,0:T(8,128)}, f32[32,3,8,128]{3,2,1,0:T(8,128)S(1)}, u32[]{:S(2)}) copy-start(f32[32,3,8,128]{3,2,1,0:T(8,128)S(1)} %all-to-all-done.6.refs_1_) | copy-start | bytes 1179652

commit v2 on v1

v2 whole, which is shorter than its diff:
```python
import jax
import jax.numpy as jnp
from jax import lax
from jax.experimental import pallas as pl
from jax.experimental.pallas import tpu as pltpu
from jax.sharding import PartitionSpec as P


soft_sq = 0.0025
area_floor = 6.25e-06
kelvin_diag = 1.8
norm_eps = 1e-06
big = 2.0 / 3.0
small = 1.0 / 6.0
BUILD_UNROLL = 4
APPLY_UNROLL = 16
f32 = jnp.float32
VM = pl.BlockSpec(memory_space=pltpu.VMEM)
SM = pl.BlockSpec(memory_space=pltpu.SMEM)
ANY = pl.BlockSpec(memory_space=pl.ANY)


def params(**kw):
    return pltpu.CompilerParams(vmem_limit_bytes=60 << 20, **kw)


def cost(us):
    return pl.CostEstimate(flops=0, transcendentals=0, bytes_accessed=int(us * 3.0e6))


def two_sum(a, b):
    s = a + b
    t = s - a
    return s, (a - (s - t)) + (b - t)


def split(a):
    c = a * 4097.0
    hi = c - (c - a)
    return hi, a - hi


def two_prod(a, b):
    p = a * b
    ah, al = split(a)
    bh, bl = split(b)
    return p, ((ah * bh - p) + ah * bl + al * bh) + al * bl


def dd_add(x, y):
    s, e = two_sum(x[0], y[0])
    e = e + (x[1] + y[1])
    hi = s + e
    return hi, e - (hi - s)


def dd_scale(x, f):
    p, e = two_prod(x[0], f)
    e = e + x[1] * f
    hi = p + e
    return hi, e - (hi - p)


def prep_kernel(no_ref, nl_ref, fo_ref, fl_ref, ask_ref, idx_ref, *, cap, trash):
    n = ask_ref.shape[0]
    width = 2 * no_ref.shape[1]
    ask = jnp.full(ask_ref.shape, float(trash), f32)
    rows = []
    for part, (o_ref, l_ref) in enumerate(((no_ref, nl_ref), (fo_ref, fl_ref))):
        owner = jnp.concatenate([o_ref[0:1, :], o_ref[1:2, :]], axis=1).astype(f32)
        local = jnp.concatenate([l_ref[0:1, :], l_ref[1:2, :]], axis=1).astype(f32)
        across = jnp.broadcast_to(owner, (width, width))
        down = across.T
        row = lax.broadcasted_iota(jnp.int32, (width, width), 0)
        col = lax.broadcasted_iota(jnp.int32, (width, width), 1)
        earlier = jnp.where((across == down) & (row < col), 1.0, 0.0)
        rank = jnp.sum(earlier, axis=0, keepdims=True)
        dest = lax.broadcasted_iota(jnp.int32, (n, width), 0).astype(f32)
        lhs = jnp.where(dest == owner, local + 1.0, 0.0).astype(jnp.bfloat16)
        slot = lax.broadcasted_iota(jnp.int32, (ask_ref.shape[1], width), 0).astype(f32)
        rhs = jnp.where(slot == rank + float(part * cap), 1.0, 0.0).astype(jnp.bfloat16)
        found = lax.dot_general(
            lhs, rhs, (((1,), (1,)), ((), ())), preferred_element_type=f32
        )
        ask = jnp.where(found > 0.5, found - 1.0, ask)
        rows += [owner, rank]
    ask_ref[...] = ask.astype(jnp.int32)
    idx_ref[...] = jnp.concatenate(rows + rows, axis=0).astype(jnp.int32)


def pack_rows(ask_ref, sources, out_ref):
    last = sources[0].shape[1] - 1

    def body(d, _):
        for s in range(out_ref.shape[2]):
            c = jnp.minimum(ask_ref[d, s], last)
            for k, source in enumerate(sources):
                for i in range(3):
                    out_ref[d, 3 * k + i, pl.ds(s, 1), :] = source[i, pl.ds(c, 1), :]
        return 0

    lax.fori_loop(0, out_ref.shape[0], body, 0, unroll=2)


def pack_kernel(ask_ref, x_ref, out_ref):
    pack_rows(ask_ref, (x_ref,), out_ref)


def pack_near_kernel(ask_ref, v_ref, p_ref, out_ref, pan_ref):
    pan_ref[...] = p_ref[...].astype(f32)
    pack_rows(ask_ref, (v_ref, pan_ref), out_ref)


def far_kernel(idx_ref, x_ref, l_ref, r_ref, out_ref, *, cap):
    count = l_ref.shape[0]

    def body(f, _):
        oa, ra = idx_ref[2, f], idx_ref[3, f]
        ob, rb = idx_ref[2, count + f], idx_ref[3, count + f]
        left = [l_ref[f, :, pl.ds(128 * i, 128)] for i in range(3)]
        right = [r_ref[f, :, pl.ds(128 * i, 128)] for i in range(3)]
        xa = [x_ref[oa, i, pl.ds(cap + ra, 1), :] for i in range(3)]
        xb = [x_ref[ob, i, pl.ds(cap + rb, 1), :] for i in range(3)]
        coef_b = jnp.sum(sum(right[i] * xb[i] for i in range(3)), axis=1, keepdims=True)
        coef_a = jnp.sum(sum(left[i] * xa[i] for i in range(3)), axis=1, keepdims=True)
        for i in range(3):
            out_ref[oa, i, pl.ds(ra, 1), :] = jnp.sum(left[i] * coef_b, axis=0, keepdims=True)
            out_ref[ob, i, pl.ds(rb, 1), :] = jnp.sum(right[i] * coef_a, axis=0, keepdims=True)
        return 0

    lax.fori_loop(0, count, body, 0, unroll=4)


def slot_geometry(in_ref, geo_ref, *, cap):
    n = in_ref.shape[0]

    def body(d, _):
        corner = []
        for m in range(3):
            pick = in_ref[d, 3 + m].astype(jnp.int32)
            corner.append(
                [jnp.take_along_axis(in_ref[d, i], pick, axis=1) for i in range(3)]
            )
        e1 = [corner[1][i] - corner[0][i] for i in range(3)]
        e2 = [corner[2][i] - corner[0][i] for i in range(3)]
        cx = e1[1] * e2[2] - e1[2] * e2[1]
        cy = e1[2] * e2[0] - e1[0] * e2[2]
        cz = e1[0] * e2[1] - e1[1] * e2[0]
        weight = jnp.sqrt(cx * cx + cy * cy + cz * cz + area_floor) / 6.0
        for s in range(3):
            for i in range(3):
                point = sum((big if m == s else small) * corner[m][i] for m in range(3))
                geo_ref[d, pl.ds((3 * s + i) * cap, cap), :] = point
        geo_ref[d, pl.ds(9 * cap, cap), :] = weight
        return 0

    lax.fori_loop(0, n, body, 0)


def pair_ends(idx_ref, pair, count):
    return (
        (idx_ref[0, pair], idx_ref[1, pair]),
        (idx_ref[0, count + pair], idx_ref[1, count + pair]),
    )


def skew_start(idx_ref, parts, base_ref, pair, *, cap, count):
    (oa, ra), _ = pair_ends(idx_ref, pair, count)
    at = 0
    for ref, comps in parts:
        for c in range(comps):
            row = jnp.broadcast_to(ref[oa, pl.ds(c * cap + ra, 1), :], (8, 128))
            base_ref[at + c] = pltpu.roll(row, 0, 1, stride=1, stride_axis=0)
        at += comps


def skew_tile(base_ref, dst_ref, t):
    for c in range(base_ref.shape[0]):
        dst_ref[c, pl.ds(pl.multiple_of(8 * t, 8), 8), :] = pltpu.roll(base_ref[c], 8 * t, 1)


def weighted(geo_ref, x_ref, y_ref, *, cap):
    def body(d, _):
        weight = geo_ref[d, pl.ds(9 * cap, cap), :]
        for i in range(3):
            y_ref[d, pl.ds(i * cap, cap), :] = weight * x_ref[d, i, pl.ds(0, cap), :]
        return 0

    lax.fori_loop(0, x_ref.shape[0], body, 0, unroll=4)


def apply_tile(mats, ya, yb, second):
    kxx, kxy, kxz, kyy, kyz, kzz = mats
    full = ((kxx, kxy, kxz), (kxy, kyy, kyz), (kxz, kyz, kzz))
    firsts = [full[i][0] * yb[0] + full[i][1] * yb[1] + full[i][2] * yb[2] for i in range(3)]
    second = [
        second[j] + (full[0][j] * ya[0] + full[1][j] * ya[1] + full[2][j] * ya[2])
        for j in range(3)
    ]
    return firsts, second


def return_terms(idx_ref, geo_ref, first_ref, second_ref, out_ref, *, cap, count):
    def body(p, _):
        (oa, ra), (ob, rb) = pair_ends(idx_ref, p, count)
        wa = geo_ref[oa, pl.ds(9 * cap + ra, 1), :]
        wb = geo_ref[ob, pl.ds(9 * cap + rb, 1), :]
        for i in range(3):
            first = first_ref[p, i]
            for half in (4, 2, 1):
                first = first + pltpu.roll(pltpu.roll(first, 8 - half, 0), 128 - half, 1)
            out_ref[oa, i, pl.ds(ra, 1), :] = wa * first[0:1]
            second = jnp.sum(second_ref[p, i], axis=0, keepdims=True)
            out_ref[ob, i, pl.ds(rb, 1), :] = wb * second
        return 0

    lax.fori_loop(0, count, body, 0, unroll=4)


def near_tile(col, row):
    su = sv = xx = xy = xz = yy = yz = None
    for s in range(3):
        for q in range(3):
            x = col[3 * s] - row[3 * q]
            y = col[3 * s + 1] - row[3 * q + 1]
            z = col[3 * s + 2] - row[3 * q + 2]
            u = lax.rsqrt(x * x + y * y + z * z + soft_sq)
            v = u * u * u
            vx = v * x
            vy = v * y
            if su is None:
                su, sv = u, v
                xx, xy, xz, yy, yz = vx * x, vx * y, vx * z, vy * y, vy * z
            else:
                su, sv = su + u, sv + v
                xx, xy, xz = xx + vx * x, xy + vx * y, xz + vx * z
                yy, yz = yy + vy * y, yz + vy * z
    zz = su - soft_sq * sv - xx - yy
    diag = kelvin_diag * su
    return (xx + diag, xy, xz, yy + diag, yz, zz + diag)


def sweep_pairs(
    idx_ref, parts, bases, bufs, tile_mats, sums, *, step, pair0, pairs, group, cap, count, unroll
):
    def two_pairs(h, _):
        for j in range(2):
            src, dst, base = bufs[j], bufs[1 - j], bases[j]
            g = 2 * h + j
            local = step * group + g
            pair = pair0 + local
            following = jnp.minimum(pair + 1, pair0 + pairs - 1)
            skew_start(idx_ref, parts, base, following, cap=cap, count=count)
            _, (ob, rb) = pair_ends(idx_ref, pair, count)
            row = [
                jnp.broadcast_to(ref[ob, pl.ds(c * cap + rb, 1), :], (8, 128))
                for ref, comps in parts
                for c in range(comps)
            ]
            comps = len(row)

            def tile_body(t, carry, g=g, src=src, dst=dst, base=base, row=row):
                if sums is not None:
                    held, first, second = carry
                    back = (128 - 8 * (t - 1)) % 128
                    first = [first[i] + pltpu.roll(held[i], back, 1) for i in range(3)]
                skew_tile(base, dst, t)
                tile = pl.ds(pl.multiple_of(8 * t, 8), 8)
                col = [src[c, tile, :] for c in range(comps)]
                mats = tile_mats(g, tile, col, row)
                if sums is None:
                    return carry
                held, second = apply_tile(mats, col[comps - 3 :], row[comps - 3 :], second)
                return held, first, second

            zero = [jnp.zeros((8, 128), f32)] * 3
            start = 0 if sums is None else (zero, zero, zero)
            carry = lax.fori_loop(0, 16, tile_body, start, unroll=unroll)
            if sums is not None:
                held, first, second = carry
                for i in range(3):
                    sums[0][local, i] = first[i] + pltpu.roll(held[i], 8, 1)
                    sums[1][local, i] = second[i]
        return 0

    lax.fori_loop(0, group // 2, two_pairs, 0)


def skew_first_pair(idx_ref, parts, base, buf, pair, *, cap, count):
    skew_start(idx_ref, parts, base, pair, cap=cap, count=count)

    def body(t, _):
        skew_tile(base, buf, t)
        return 0

    lax.fori_loop(0, 16, body, 0, unroll=4)


def build_blocks(idx_ref, geo_ref, k_ref, base0, base1, buf0, buf1, *, pair0, pairs, cap, count):
    step = pl.program_id(0)
    parts = ((geo_ref, 9),)

    @pl.when(step == 0)
    def _():
        skew_first_pair(idx_ref, parts, base1, buf0, pair0, cap=cap, count=count)

    def tile_mats(g, tile, col, row):
        mats = near_tile(col, row)
        for m in range(6):
            k_ref[g, m, tile, :] = mats[m]
        return mats

    sweep_pairs(
        idx_ref, parts, (base0, base1), (buf0, buf1), tile_mats, None,
        step=step, pair0=pair0, pairs=pairs, group=k_ref.shape[0], cap=cap, count=count,
        unroll=BUILD_UNROLL,
    )


def build_kernel(idx_ref, in_ref, k_ref, geo_ref, *skews, pairs, cap, count):
    @pl.when(pl.program_id(0) == 0)
    def _():
        slot_geometry(in_ref, geo_ref, cap=cap)

    build_blocks(idx_ref, geo_ref, k_ref, *skews, pair0=0, pairs=pairs, cap=cap, count=count)


def build_rest_kernel(idx_ref, geo_ref, old_ref, far_ref, k_ref, *skews, pair0, cap, count):
    build_blocks(
        idx_ref, geo_ref, k_ref, *skews, pair0=pair0, pairs=count - pair0, cap=cap, count=count
    )


def apply_kernel(
    idx_ref, geo_ref, x_ref, k_ref, out_ref,
    first_ref, second_ref, y_ref, base0, base1, buf0, buf1, *, cap, count,
):
    step = pl.program_id(0)
    parts = ((y_ref, 3),)

    @pl.when(step == 0)
    def _():
        weighted(geo_ref, x_ref, y_ref, cap=cap)
        skew_first_pair(idx_ref, parts, base1, buf0, 0, cap=cap, count=count)

    def tile_mats(g, tile, col, row):
        return [k_ref[g, m, tile, :] for m in range(6)]

    sweep_pairs(
        idx_ref, parts, (base0, base1), (buf0, buf1), tile_mats, (first_ref, second_ref),
        step=step, pair0=0, pairs=count, group=k_ref.shape[0], cap=cap, count=count,
        unroll=APPLY_UNROLL,
    )

    @pl.when(step == pl.num_programs(0) - 1)
    def _():
        return_terms(idx_ref, geo_ref, first_ref, second_ref, out_ref, cap=cap, count=count)


def add_up(ask_ref, near_ref, far_ref, accs, out_ref, *, cap):
    clusters = out_ref.shape[1]
    for acc in accs:
        acc[...] = jnp.zeros(acc.shape, f32)

    def body(d, _):
        for s in range(cap):
            cn = ask_ref[d, s]
            cf = ask_ref[d, cap + s]
            for i in range(3):
                accs[i][pl.ds(cn, 1), :] += near_ref[d, i, pl.ds(s, 1), :]
                accs[3 + i][pl.ds(cf, 1), :] += far_ref[d, i, pl.ds(s, 1), :]
        return 0

    lax.fori_loop(0, near_ref.shape[0], body, 0)
    for i in range(3):
        out_ref[i] = accs[i][pl.ds(0, clusters), :] + accs[3 + i][pl.ds(0, clusters), :]


def merge_kernel(ask_ref, rn_ref, rf_ref, out_ref, pack_ref, *accs, cap):
    add_up(ask_ref, rn_ref, rf_ref, accs, out_ref, cap=cap)
    pack_rows(ask_ref, (out_ref,), pack_ref)


PRODUCTS = ((0, 0), (0, 1), (1, 1), (0, 2), (1, 2), (2, 2))


def gram_kernel(ask_ref, rn_ref, rf_ref, v0_ref, v1_ref, out_ref, part_ref, *accs, cap):
    add_up(ask_ref, rn_ref, rf_ref, accs, out_ref, cap=cap)
    clusters = out_ref.shape[1]
    refs = (v0_ref, v1_ref, out_ref)
    zero = jnp.zeros((8, 128), f32)
    totals = [(zero, zero)] * 6
    for i in range(3):

        def body(t, totals):
            tiles = [ref[i, pl.ds(8 * t, 8), :] for ref in refs]
            halves = [split(tile) for tile in tiles]
            new = []
            for k, (a, b) in enumerate(PRODUCTS):
                (ah, al), (bh, bl) = halves[a], halves[b]
                p = tiles[a] * tiles[b]
                e = ((ah * bh - p) + ah * bl + al * bh) + al * bl
                hi, lo = totals[k]
                s, err = two_sum(hi, p)
                new.append((s, lo + (err + e)))
            return new

        totals = lax.fori_loop(0, clusters // 8, body, totals)
    hi = jnp.concatenate([t[0] for t in totals], axis=0)
    lo = jnp.concatenate([t[1] for t in totals], axis=0)
    for shift in (64, 32, 16, 8, 4, 2, 1):
        hi, lo = dd_add((hi, lo), (pltpu.roll(hi, shift, 1), pltpu.roll(lo, shift, 1)))
    lane = lax.broadcasted_iota(jnp.int32, (8, 128), 1)
    shi = slo = zero
    for k in range(6):
        shi = jnp.where(lane == k, hi[8 * k : 8 * k + 8], shi)
        slo = jnp.where(lane == k, lo[8 * k : 8 * k + 8], slo)
    for shift in (4, 2, 1):
        shi, slo = dd_add((shi, slo), (pltpu.roll(shi, shift, 0), pltpu.roll(slo, shift, 0)))
    packed = jnp.where(lane < 8, shi, pltpu.roll(slo, 8, 1))
    part_ref[...] = jnp.broadcast_to(packed[0:1, :], part_ref.shape)


def final_kernel(part_ref, v0_ref, v1_ref, v2_ref, basis_ref, hess_ref, *, size_all):
    hi = part_ref[...]
    lo = pltpu.roll(hi, 120, 1)
    rows = hi.shape[0]
    while rows > 1:
        half = rows // 2
        hi, lo = dd_add((hi[:half], lo[:half]), (hi[half:], lo[half:]))
        rows = half
    inv = 1.0 / size_all
    hi, lo = dd_scale((hi, lo), jnp.full(hi.shape, inv, f32)) if size_all & (size_all - 1) == 0 else dd_div_const(hi, lo, size_all)
    g = [(hi[:, k : k + 1], lo[:, k : k + 1]) for k in range(6)]
    g00, g01, g11, g02, g12, g22 = g
    eps = jnp.full((1, 1), norm_eps, f32)
    none = jnp.zeros((1, 1), f32)
    s2 = dd_add(g00, (eps, none))
    s = jnp.sqrt(s2[0])
    p = g01[0] / s2[0]
    r1 = dd_add(g11, dd_scale(dd_add(dd_scale(g00, p), dd_scale(g01, none - 2.0)), p))
    nf = jnp.sqrt(jnp.maximum(r1[0], 0.0) / s2[0] + norm_eps)
    snf = s * nf
    c0 = dd_add(g02, dd_scale(g01, -p))
    pc = c0[0] / (s2[0] * nf)
    c1 = dd_add(dd_add(g12, dd_scale(g11, -p)), dd_scale(c0, -p))
    ps = c1[0] / (s2[0] * nf * nf)
    a1 = -(p + ps)
    a0 = ps * p - pc * nf
    t2 = dd_add(g22, dd_scale(dd_add(dd_scale(g12, a1), dd_scale(g02, a0)), none + 2.0))
    t1 = dd_scale(dd_add(dd_scale(g11, a1), dd_scale(g01, 2.0 * a0)), a1)
    t0 = dd_scale(dd_scale(g00, a0), a0)
    w2 = dd_add(dd_add(t2, t1), t0)
    n2 = jnp.sqrt(jnp.maximum(w2[0], 0.0) / (snf * snf) + norm_eps)
    k1 = 1.0 / snf
    k2 = 1.0 / (snf * n2)
    for i in range(3):
        v0, v1, v2 = v0_ref[i], v1_ref[i], v2_ref[i]
        basis_ref[0, i] = (v1 - p * v0) * k1
        basis_ref[1, i] = (v2 + a1 * v1 + a0 * v0) * k2
    top = jnp.concatenate([p, nf, none], axis=1)
    bottom = jnp.concatenate([pc, ps, n2], axis=1)
    hess_ref[...] = jnp.concatenate([top, bottom], axis=0)


def dd_div_const(hi, lo, size_all):
    d = jnp.full(hi.shape, float(size_all), f32)
    q = hi / d
    p, e = two_prod(q, d)
    rest = ((hi - p) - e) + lo
    return q, rest / d


def per_device(
    right_side, vertices, panels, near_owner, near_local, far_owner, far_local, far_left, far_right
):
    n = lax.axis_size("dev")
    clusters, _, width = right_side.shape
    near_count = near_owner.shape[0]
    cap = max(2, 4 * near_count // n)
    size_all = clusters * n * 3 * width
    x0 = right_side.transpose(1, 0, 2)
    shape = jax.ShapeDtypeStruct

    def exchange(block):
        return lax.all_to_all(block, "dev", split_axis=0, concat_axis=0, tiled=True)

    slots = max(128, 2 * cap)
    ask, idx = pl.pallas_call(
        lambda *refs: prep_kernel(*refs, cap=cap, trash=clusters),
        out_shape=(shape((n, slots), jnp.int32), shape((8, 2 * near_count), jnp.int32)),
        compiler_params=params(),
        name="prep",
    )(near_owner.T, near_local.T, far_owner.T, far_local.T)
    asked = exchange(ask)

    rows3 = shape((n, 3, cap, width), f32)
    both = shape((n, 3, 2 * cap, width), f32)

    near_in = exchange(
        pl.pallas_call(
            pack_near_kernel,
            out_shape=shape((n, 6, cap, width), f32),
            in_specs=[SM, VM, VM],
            scratch_shapes=[pltpu.VMEM((3, clusters, width), f32)],
            compiler_params=params(),
            cost_estimate=cost(4.0),
            name="pack_near",
        )(asked, vertices.transpose(1, 0, 2), panels.transpose(1, 0, 2))
    )
    x0_out = pl.pallas_call(
        pack_kernel,
        out_shape=both,
        in_specs=[SM, VM],
        compiler_params=params(),
        cost_estimate=cost(3.0),
        name="pack",
    )(asked, x0)
    x0_in = exchange(x0_out)

    group = 8
    early = near_count // 2
    k_block = (group, 6, width, width)
    k_shape = shape((near_count, 6, width, width), f32)
    rows10 = (n, 10 * cap, width)

    def whole(*dims):
        return pl.BlockSpec(dims, lambda g: (0,) * len(dims))

    def skews(comps):
        return [pltpu.VMEM((comps, 8, width), f32)] * 2 + [
            pltpu.VMEM((comps, width, width), f32)
        ] * 2

    stored, geometry = pl.pallas_call(
        lambda *refs: build_kernel(*refs, pairs=early, cap=cap, count=near_count),
        out_shape=(k_shape, shape(rows10, f32)),
        grid=(early // group,),
        in_specs=[SM, whole(n, 6, cap, width)],
        out_specs=(pl.BlockSpec(k_block, lambda g: (g, 0, 0, 0)), whole(*rows10)),
        scratch_shapes=skews(9),
        compiler_params=params(),
        cost_estimate=cost(30.0),
        name="build",
    )(idx, near_in)

    def far_product(received):
        return pl.pallas_call(
            lambda *refs: far_kernel(*refs, cap=cap),
            out_shape=rows3,
            in_specs=[SM, VM, VM, VM],
            compiler_params=params(),
            cost_estimate=cost(5.0),
            name="far",
        )(idx, received, far_left, far_right)

    far_terms = far_product(x0_in)
    far_back = exchange(far_terms)
    stored = pl.pallas_call(
        lambda *refs: build_rest_kernel(*refs, pair0=early, cap=cap, count=near_count),
        out_shape=k_shape,
        grid=((near_count - early) // group,),
        in_specs=[SM, whole(*rows10), ANY, ANY],
        out_specs=pl.BlockSpec(k_block, lambda g: (g + early // group, 0, 0, 0)),
        scratch_shapes=skews(9),
        input_output_aliases={2: 0},
        compiler_params=params(),
        cost_estimate=cost(30.0),
        name="build_rest",
    )(idx, geometry, stored, far_terms)

    def apply_stored(received):
        return exchange(
            pl.pallas_call(
                lambda *refs: apply_kernel(*refs, cap=cap, count=near_count),
                out_shape=rows3,
                grid=(near_count // group,),
                in_specs=[
                    SM,
                    whole(*rows10),
                    whole(*both.shape),
                    pl.BlockSpec(k_block, lambda g: (g, 0, 0, 0)),
                ],
                out_specs=whole(n, 3, cap, width),
                scratch_shapes=[pltpu.VMEM((near_count, 3, 8, width), f32)] * 2
                + [pltpu.VMEM((n, 3 * cap, width), f32)]
                + skews(3),
                compiler_params=params(),
                cost_estimate=cost(18.0),
                name="apply",
            )(idx, geometry, received, stored)
        )

    near_back = apply_stored(x0_in)

    accs = [pltpu.VMEM((clusters + 8, width), f32)] * 6
    x1, x1_out = pl.pallas_call(
        lambda *refs: merge_kernel(*refs, cap=cap),
        out_shape=(shape((3, clusters, width), f32), both),
        in_specs=[SM, VM, VM],
        scratch_shapes=accs,
        compiler_params=params(),
        cost_estimate=cost(5.0),
        name="merge",
    )(asked, near_back, far_back)
    x1_in = exchange(x1_out)
    far_back2 = exchange(far_product(x1_in))
    near_back2 = apply_stored(x1_in)

    x2, part = pl.pallas_call(
        lambda *refs: gram_kernel(*refs, cap=cap),
        out_shape=(shape((3, clusters, width), f32), shape((n, 128), f32)),
        in_specs=[SM, VM, VM, VM, VM],
        scratch_shapes=accs,
        compiler_params=params(),
        cost_estimate=cost(5.0),
        name="gram",
    )(asked, near_back2, far_back2, x0, x1)
    parts = exchange(part)
    basis, hess = pl.pallas_call(
        lambda *refs: final_kernel(*refs, size_all=size_all),
        out_shape=(shape((2, 3, clusters, width), f32), shape((2, 3), f32)),
        compiler_params=params(),
        name="final",
    )(parts, x0, x1, x2)
    return (basis.transpose(0, 2, 1, 3), hess.T)


def solution(mesh):
    per_cluster = P("dev", None, None)
    per_pair = P("dev", None)
    in_specs = (per_cluster,) * 3 + (per_pair,) * 4 + (per_cluster,) * 2
    out_specs = (P(None, "dev", None, None), P())

    return jax.shard_map(
        per_device, mesh=mesh, in_specs=in_specs, out_specs=out_specs, check_vma=False
    )
```

time: 468 us -> 255 us (0.54)
  Pallas kernels: 325 us -> 122 us
  waiting for transfers between devices: 32.8 us -> 17.9 us
  blocking collectives: 93.5 us -> 103 us
  starting transfers between devices: 14.6 us -> 9.71 us
    pallas_call x5 -> x8, Pallas kernels: 311 us -> 108 us  [the longest x2 42.2 us: apply_stored(): pl.pallas_call(lambda *refs: apply_kernel(*refs, cap=cap, count=near_coun...]
    all_to_all x4 -> x3, waiting for transfers between devices: 32.8 us -> 17.9 us  [exchange(): return lax.all_to_all(block, 'dev', split_axis=0, concat_axis=0, tiled=True)]
    all_to_all x6, blocking collectives: 93.5 us -> 103 us  [exchange(): return lax.all_to_all(block, 'dev', split_axis=0, concat_axis=0, tiled=True)]
    all_to_all x4 -> x3, starting transfers between devices: 14.6 us -> 9.71 us  [exchange(): return lax.all_to_all(block, 'dev', split_axis=0, concat_axis=0, tiled=True)]
  transfers between devices with their start and end apart: 4 -> 3, of which waited for: 2 -> 1; matrix products, arithmetic and copies ran while one was open for 0% -> 0% of each run, Pallas kernels for 66% -> 20%
where the time goes in v2:
time: 255 us; the launch traced here: 254 us
  Pallas kernels  122 us (48%)
  blocking collectives  103 us (40%)
  waiting for transfers between devices  17.9 us (7%)
  starting transfers between devices  9.71 us (4%)
    all_to_all x6, blocking collectives, exchange(): return lax.all_to_all(block, 'dev', split_axis=0, concat_axis=0, tiled=True)  103 us
    pallas_call x2, Pallas kernels, apply_stored(): pl.pallas_call(lambda *refs: apply_kernel(*refs, cap=cap, count=near_coun...  42.2 us
    pallas_call x1, Pallas kernels, per_device(): pl.pallas_call(lambda *refs: build_kernel(*refs, pairs=early, cap=cap, co...  27 us
    pallas_call x1, Pallas kernels, per_device(): pl.pallas_call(lambda *refs: build_rest_kernel(*refs, pair0=early, cap=ca...  23.4 us
    all_to_all x3, waiting for transfers between devices, exchange(): return lax.all_to_all(block, 'dev', split_axis=0, concat_axis=0, tiled=True)  17.9 us
    all_to_all x3, starting transfers between devices, exchange(): return lax.all_to_all(block, 'dev', split_axis=0, concat_axis=0, tiled=True)  9.71 us
    pallas_call x2, Pallas kernels, far_product(): pl.pallas_call(lambda *refs: far_kernel(*refs, cap=cap), out_shape=rows3,...  9.69 us
  transfers between devices with their start and end apart: 3, of which 1 were waited for; matrix products, arithmetic and copies ran while one was open for 0% of the time, Pallas kernels for 20%

profile of v2, /device:TPU:0, one launch (start us, length us, event | category | flops | bytes accessed | tf_op | source)
XLA Modules:
  0.0 253.9 jit_solution(2696007208100037002)
XLA Ops:
  0.6 1.7 prep.1
  2.3 14.5 %all_to_all.57 = s32[32,1,128]{2,1,0:T(1,128)} all-to-all(s32[32,1,128]{2,1,0:T(1,128)} %bitcast.28), channel_id=1, replica_groups=mesh['dev'=32] {'dev'}, dimensions={0} | all-to-all | bytes 32768 | tf_op jit(solution)/shard_map/all_to_all | solution.py:486
  16.8 2.8 %pack_near.1 = f32[32,6,8,128]{3,2,1,0:T(8,128)} custom-call(s32[32,128]{1,0:T(8,128)} %bitcast.20, f32[3,64,128]{2,1,0:T(8,128)} %bitcast.24, s32[3,64,128]{2,1,0:T(8,128)} %bitcast.25), custom_call_target="tpu_custom_call" | custom-call | bytes 12000000 | tf_op jit(solution)/shard_map/pack_near/pallas_call | solution.py:501
  19.6 2.6 %all-to-all-start.1 = ((f32[32,6,8,128]{3,2,1,0:T(8,128)}), f32[32,6,8,128]{3,2,1,0:T(8,128)S(1)}, u32[]{:S(2)}, u32[]{:S(2)}) async-start(f32[32,6,8,128]{3,2,1,0:T(8,128)} %pack_near.1), calls=%async_computation.1 | async-start | bytes 1572864 | tf_op jit(solution)/shard_map/all_to_all | solution.py:486
  22.3 2.7 %pack.1 = f32[32,3,16,128]{3,2,1,0:T(8,128)} custom-call(s32[32,128]{1,0:T(8,128)} %bitcast.21, f32[3,64,128]{2,1,0:T(8,128)} %bitcast.17), custom_call_target="tpu_custom_call" | custom-call | bytes 9000000 | tf_op jit(solution)/shard_map/pack/pallas_call | solution.py:511
  25.0 17.9 %all-to-all-done.1.refs_1_ = f32[32,6,8,128]{3,2,1,0:T(8,128)S(1)} async-done(((f32[32,6,8,128]{3,2,1,0:T(8,128)}), f32[32,6,8,128]{3,2,1,0:T(8,128)S(1)}, u32[]{:S(2)}, u32[]{:S(2)}) %all-to-all-start.1) | async-done | bytes 786464 | tf_op jit(solution)/shard_map/all_to_all | solution.py:486
  42.8 0.0 copy-start.2
  42.8 3.5 %all-to-all-start.2 = ((f32[32,3,16,128]{3,2,1,0:T(8,128)}), f32[32,3,16,128]{3,2,1,0:T(8,128)S(1)}, u32[]{:S(2)}, u32[]{:S(2)}) async-start(f32[32,3,16,128]{3,2,1,0:T(8,128)} %pack.1), calls=%async_computation.2 | async-start | bytes 1572864 | tf_op jit(solution)/shard_map/all_to_all | solution.py:486
  46.4 0.0 copy-done.2
  46.4 27.0 %build.1 = (f32[64,6,128,128]{3,2,1,0:T(8,128)}, f32[32,80,128]{2,1,0:T(8,128)}) custom-call(s32[8,128]{1,0:T(8,128)} %get-tuple-element.13.refs_0_, f32[32,6,8,128]{3,2,1,0:T(8,128)} %copy-done.2), custom_call_target="tpu_custom_call" | custom-call | bytes 90000000 | tf_op jit(solution)/shard_map/build/pallas_call | solution.py:535
  73.4 0.0 all-to-all-done.2.refs_1_.refs_2_
  73.4 0.0 copy-start
  73.4 0.9 copy-done
  74.3 4.8 %far.2.refs_3_ = f32[32,3,8,128]{3,2,1,0:T(8,128)} custom-call(s32[8,128]{1,0:T(8,128)} %get-tuple-element.13.refs_0_, f32[32,3,16,128]{3,2,1,0:T(8,128)} %copy-done, f32[64,16,384]{2,1,0:T(8,128)} %refs_2_.3, f32[64,16,384]{2,1,0:T(8,128)} %refs_3_.3), custom_call_target="tpu_custom_call" | custom-call | bytes 15000000 | tf_op jit(solution)/shard_map/far/pallas_call | solution.py:548
  79.1 23.4 %build_rest.1.refs_3_ = f32[64,6,128,128]{3,2,1,0:T(8,128)} custom-call(s32[8,128]{1,0:T(8,128)} %get-tuple-element.13.refs_0_, f32[32,80,128]{2,1,0:T(8,128)} %get-tuple-element.14.refs_1_, f32[64,6,128,128]{3,2,1,0:T(8,128)} %get-tuple-element.15.refs_2_, f32[32,3,8,128]{3,2,1,0:T(8,128)} %far.2.refs_3_), custom_call_target="tpu_custom_call", output_to_operand_aliasing={{}: (2, {})} | custom-call | bytes 90000000 | tf_op jit(solution)/shard_map/build_rest/pallas_call | solution.py:559
  102.5 0.0 copy-start.1
  102.5 21.1 %apply.2 = f32[32,3,8,128]{3,2,1,0:T(8,128)} custom-call(s32[8,128]{1,0:T(8,128)} %get-tuple-element.13.refs_0_, f32[32,80,128]{2,1,0:T(8,128)} %get-tuple-element.14.refs_1_, f32[32,3,16,128]{3,2,1,0:T(8,128)} %copy-done, f32[64,6,128,128]{3,2,1,0:T(8,128)} %build_rest.1.refs_3_), custom_call_target="tpu_custom_call" | custom-call | bytes 54000000 | tf_op jit(solution)/shard_map/apply/pallas_call | solution.py:574
  123.7 19.2 %all_to_all.58.refs_1_ = f32[32,3,8,128]{3,2,1,0:T(8,128)} all-to-all(f32[32,3,8,128]{3,2,1,0:T(8,128)} %apply.2), channel_id=1, replica_groups=mesh['dev'=32] {'dev'}, dimensions={0} | all-to-all | bytes 786432 | tf_op jit(solution)/shard_map/all_to_all | solution.py:486
  142.8 0.0 copy-done.1
  142.8 15.7 %all_to_all.59.refs_2_ = f32[32,3,8,128]{3,2,1,0:T(8,128)} all-to-all(f32[32,3,8,128]{3,2,1,0:T(8,128)S(1)} %copy-done.1), channel_id=1, replica_groups=mesh['dev'=32] {'dev'}, dimensions={0} | all-to-all | bytes 786432 | tf_op jit(solution)/shard_map/all_to_all | solution.py:486
  158.5 4.6 %merge.1 = (f32[3,64,128]{2,1,0:T(8,128)}, f32[32,3,16,128]{3,2,1,0:T(8,128)}) custom-call(s32[32,128]{1,0:T(8,128)} %bitcast.22, f32[32,3,8,128]{3,2,1,0:T(8,128)} %all_to_all.58.refs_1_, f32[32,3,8,128]{3,2,1,0:T(8,128)} %all_to_all.59.refs_2_), custom_call_target="tpu_custom_call" | custom-call | bytes 15000000 | tf_op jit(solution)/shard_map/merge/pallas_call | solution.py:597
  163.1 23.9 %all_to_all.60.refs_2_.refs_1_ = f32[32,3,16,128]{3,2,1,0:T(8,128)} all-to-all(f32[32,3,16,128]{3,2,1,0:T(8,128)} %get-tuple-element.16), channel_id=1, replica_groups=mesh['dev'=32] {'dev'}, dimensions={0} | all-to-all | bytes 1572864 | tf_op jit(solution)/shard_map/all_to_all | solution.py:486
  187.0 4.8 %far.3 = f32[32,3,8,128]{3,2,1,0:T(8,128)} custom-call(s32[8,128]{1,0:T(8,128)} %get-tuple-element.13.refs_0_, f32[32,3,16,128]{3,2,1,0:T(8,128)} %all_to_all.60.refs_2_.refs_1_, f32[64,16,384]{2,1,0:T(8,128)} %refs_2_.3, f32[64,16,384]{2,1,0:T(8,128)} %refs_3_.3), custom_call_target="tpu_custom_call" | custom-call | bytes 15000000 | tf_op jit(solution)/shard_map/far/pallas_call | solution.py:548
  191.9 3.5 %all-to-all-start.7 = ((f32[32,3,8,128]{3,2,1,0:T(8,128)}), f32[32,3,8,128]{3,2,1,0:T(8,128)S(1)}, u32[]{:S(2)}, u32[]{:S(2)}) async-start(f32[32,3,8,128]{3,2,1,0:T(8,128)} %far.3), calls=%async_computation.7 | async-start | bytes 786432 | tf_op jit(solution)/shard_map/all_to_all | solution.py:486
  195.4 21.1 %apply.3 = f32[32,3,8,128]{3,2,1,0:T(8,128)} custom-call(s32[8,128]{1,0:T(8,128)} %get-tuple-element.13.refs_0_, f32[32,80,128]{2,1,0:T(8,128)} %get-tuple-element.14.refs_1_, f32[32,3,16,128]{3,2,1,0:T(8,128)} %all_to_all.60.refs_2_.refs_1_, f32[64,6,128,128]{3,2,1,0:T(8,128)} %build_rest.1.refs_3_), custom_call_target="tpu_custom_call" | custom-call | bytes 54000000 | tf_op jit(solution)/shard_map/apply/pallas_call | solution.py:574
  216.5 0.0 all-to-all-done.7.refs_2_
  216.5 0.0 copy-start.3
  216.6 19.2 %all_to_all.61.refs_1_ = f32[32,3,8,128]{3,2,1,0:T(8,128)} all-to-all(f32[32,3,8,128]{3,2,1,0:T(8,128)} %apply.3), channel_id=1, replica_groups=mesh['dev'=32] {'dev'}, dimensions={0} | all-to-all | bytes 786432 | tf_op jit(solution)/shard_map/all_to_all | solution.py:486
  235.7 0.0 copy-done.3
  235.8 4.6 %gram.1 = (f32[3,64,128]{2,1,0:T(8,128)}, f32[32,128]{1,0:T(8,128)}) custom-call(s32[32,128]{1,0:T(8,128)} %bitcast.23, f32[32,3,8,128]{3,2,1,0:T(8,128)} %all_to_all.61.refs_1_, f32[32,3,8,128]{3,2,1,0:T(8,128)} %copy-done.3, f32[3,64,128]{2,1,0:T(8,128)} %bitcast.18, f32[3,64,128]{2,1,0:T(8,128)} %get-tuple-element.17.refs_4_.refs_2_), custom_call_target="tpu_custom_call" | custom-call | bytes 15000000 | tf_op jit(solution)/shard_map/gram/pallas_call | solution.py:610
  240.4 10.1 %all_to_all.62 = f32[32,1,128]{2,1,0:T(1,128)} all-to-all(f32[32,1,128]{2,1,0:T(1,128)} %bitcast.27), channel_id=1, replica_groups=mesh['dev'=32] {'dev'}, dimensions={0} | all-to-all | bytes 32768 | tf_op jit(solution)/shard_map/all_to_all | solution.py:486
  250.5 3.5 %final.1 = (f32[2,3,64,128]{3,2,1,0:T(8,128)}, f32[2,3]{1,0:T(2,128)}) custom-call(f32[32,128]{1,0:T(8,128)} %bitcast.26, f32[3,64,128]{2,1,0:T(8,128)} %bitcast.19, f32[3,64,128]{2,1,0:T(8,128)} %get-tuple-element.17.refs_4_.refs_2_, f32[3,64,128]{2,1,0:T(8,128)} %get-tuple-element.19.refs_3_), custom_call_target="tpu_custom_call" | custom-call | tf_op jit(solution)/shard_map/final/pallas_call | solution.py:620
Async XLA Ops:
  19.6 23.2 %all-to-all-start.1 = ((f32[32,6,8,128]{3,2,1,0:T(8,128)}), f32[32,6,8,128]{3,2,1,0:T(8,128)S(1)}, u32[]{:S(2)}, u32[]{:S(2)}) async-start(f32[32,6,8,128]{3,2,1,0:T(8,128)} %pack_near.1), calls=%async_computation.1 | async-start | bytes 1572864 | tf_op jit(solution)/shard_map/all_to_all | solution.py:486
  42.8 3.6 %copy-start.2 = (f32[32,6,8,128]{3,2,1,0:T(8,128)}, f32[32,6,8,128]{3,2,1,0:T(8,128)S(1)}, u32[]{:S(2)}) copy-start(f32[32,6,8,128]{3,2,1,0:T(8,128)S(1)} %all-to-all-done.1.refs_1_) | copy-start | bytes 2359300
  42.8 30.6 %all-to-all-start.2 = ((f32[32,3,16,128]{3,2,1,0:T(8,128)}), f32[32,3,16,128]{3,2,1,0:T(8,128)S(1)}, u32[]{:S(2)}, u32[]{:S(2)}) async-start(f32[32,3,16,128]{3,2,1,0:T(8,128)} %pack.1), calls=%async_computation.2 | async-start | bytes 1572864 | tf_op jit(solution)/shard_map/all_to_all | solution.py:486
  73.4 0.9 copy-start
  102.5 40.3 %copy-start.1 = (f32[32,3,8,128]{3,2,1,0:T(8,128)S(1)}, f32[32,3,8,128]{3,2,1,0:T(8,128)}, u32[]{:S(2)}) copy-start(f32[32,3,8,128]{3,2,1,0:T(8,128)} %far.2.refs_3_) | copy-start | bytes 1179652
  191.9 24.7 %all-to-all-start.7 = ((f32[32,3,8,128]{3,2,1,0:T(8,128)}), f32[32,3,8,128]{3,2,1,0:T(8,128)S(1)}, u32[]{:S(2)}, u32[]{:S(2)}) async-start(f32[32,3,8,128]{3,2,1,0:T(8,128)} %far.3), calls=%async_computation.7 | async-start | bytes 786432 | tf_op jit(solution)/shard_map/all_to_all | solution.py:486
  216.5 19.2 %copy-start.3 = (f32[32,3,8,128]{3,2,1,0:T(8,128)}, f32[32,3,8,128]{3,2,1,0:T(8,128)S(1)}, u32[]{:S(2)}) copy-start(f32[32,3,8,128]{3,2,1,0:T(8,128)S(1)} %all-to-all-done.7.refs_2_) | copy-start | bytes 1179652

commit v3 on v2

--- a/solution.py
+++ b/solution.py
@@ -20,8 +20,8 @@
 ANY = pl.BlockSpec(memory_space=pl.ANY)
 
 
-def params(**kw):
-    return pltpu.CompilerParams(vmem_limit_bytes=60 << 20, **kw)
+def params(mib=8):
+    return pltpu.CompilerParams(vmem_limit_bytes=mib << 20)
 
 
 def cost(us):
@@ -88,47 +88,79 @@
     idx_ref[...] = jnp.concatenate(rows + rows, axis=0).astype(jnp.int32)
 
 
-def pack_rows(ask_ref, sources, out_ref):
-    last = sources[0].shape[1] - 1
-
+def pack_rows(ask_ref, fetch, out_ref, *, n, slots, kinds):
     def body(d, _):
-        for s in range(out_ref.shape[2]):
-            c = jnp.minimum(ask_ref[d, s], last)
-            for k, source in enumerate(sources):
-                for i in range(3):
-                    out_ref[d, 3 * k + i, pl.ds(s, 1), :] = source[i, pl.ds(c, 1), :]
-        return 0
-
-    lax.fori_loop(0, out_ref.shape[0], body, 0, unroll=2)
-
-
-def pack_kernel(ask_ref, x_ref, out_ref):
-    pack_rows(ask_ref, (x_ref,), out_ref)
-
-
-def pack_near_kernel(ask_ref, v_ref, p_ref, out_ref, pan_ref):
+        for s in range(slots):
+            rows = fetch(ask_ref[d, s])
+            for k in range(kinds):
+                at = (d * kinds + k) * 3 * slots + s
+                out_ref[pl.ds(at, 3, stride=slots), :] = rows[k]
+        return 0
+
+    lax.fori_loop(0, n, body, 0, unroll=2)
+
+
+def cluster_rows(refs):
+    clusters = refs[0].shape[0] // 3
+
+    def fetch(c):
+        c = jnp.minimum(c, clusters - 1)
+        return [ref[pl.ds(c, 3, stride=clusters), :] for ref in refs]
+
+    return fetch
+
+
+def pack_kernel(ask_ref, x_ref, out_ref, *, n, slots):
+    pack_rows(ask_ref, cluster_rows((x_ref,)), out_ref, n=n, slots=slots, kinds=1)
+
+
+def pack_near_kernel(ask_ref, v_ref, p_ref, out_ref, pan_ref, *, n, slots):
     pan_ref[...] = p_ref[...].astype(f32)
-    pack_rows(ask_ref, (v_ref, pan_ref), out_ref)
-
-
-def far_kernel(idx_ref, x_ref, l_ref, r_ref, out_ref, *, cap):
+    pack_rows(ask_ref, cluster_rows((v_ref, pan_ref)), out_ref, n=n, slots=slots, kinds=2)
+
+
+def far_kernel(idx_ref, x_ref, l_ref, r_ref, out_ref, sum_ref, row_ref, *, cap):
     count = l_ref.shape[0]
 
-    def body(f, _):
+    def ends(f):
         oa, ra = idx_ref[2, f], idx_ref[3, f]
         ob, rb = idx_ref[2, count + f], idx_ref[3, count + f]
+        return (oa, ra), (ob, rb)
+
+    def body(f, _):
+        (oa, ra), (ob, rb) = ends(f)
         left = [l_ref[f, :, pl.ds(128 * i, 128)] for i in range(3)]
         right = [r_ref[f, :, pl.ds(128 * i, 128)] for i in range(3)]
-        xa = [x_ref[oa, i, pl.ds(cap + ra, 1), :] for i in range(3)]
-        xb = [x_ref[ob, i, pl.ds(cap + rb, 1), :] for i in range(3)]
+        xa = [x_ref[pl.ds((oa * 3 + i) * 2 * cap + cap + ra, 1), :] for i in range(3)]
+        xb = [x_ref[pl.ds((ob * 3 + i) * 2 * cap + cap + rb, 1), :] for i in range(3)]
         coef_b = jnp.sum(sum(right[i] * xb[i] for i in range(3)), axis=1, keepdims=True)
         coef_a = jnp.sum(sum(left[i] * xa[i] for i in range(3)), axis=1, keepdims=True)
+        rank = left[0].shape[0]
         for i in range(3):
-            out_ref[oa, i, pl.ds(ra, 1), :] = jnp.sum(left[i] * coef_b, axis=0, keepdims=True)
-            out_ref[ob, i, pl.ds(rb, 1), :] = jnp.sum(right[i] * coef_a, axis=0, keepdims=True)
-        return 0
-
-    lax.fori_loop(0, count, body, 0, unroll=4)
+            for k, part in ((i, left[i] * coef_b), (3 + i, right[i] * coef_a)):
+                at = pl.ds(pl.multiple_of((6 * f + k) * 8, 8), 8)
+                sum_ref[at, :] = sum(part[8 * h : 8 * h + 8] for h in range(rank // 8))
+        return 0
+
+    lax.fori_loop(0, count, body, 0, unroll=8)
+
+    def add_rows(q, _):
+        for k in range(6):
+            rows = [sum_ref[pl.ds(48 * 8 * q + 8 * k + m, 8, stride=48), :] for m in range(8)]
+            row_ref[pl.ds(pl.multiple_of(k * count + 8 * q, 8), 8), :] = sum(rows)
+        return 0
+
+    lax.fori_loop(0, count // 8, add_rows, 0, unroll=2)
+
+    def send(f, _):
+        (oa, ra), (ob, rb) = ends(f)
+        out_ref[pl.ds(oa * 3 * cap + ra, 3, stride=cap), :] = row_ref[pl.ds(f, 3, stride=count), :]
+        out_ref[pl.ds(ob * 3 * cap + rb, 3, stride=cap), :] = row_ref[
+            pl.ds(3 * count + f, 3, stride=count), :
+        ]
+        return 0
+
+    lax.fori_loop(0, count, send, 0, unroll=8)
 
 
 def slot_geometry(in_ref, geo_ref, *, cap):
@@ -200,21 +232,32 @@
     return firsts, second
 
 
-def return_terms(idx_ref, geo_ref, first_ref, second_ref, out_ref, *, cap, count):
+def return_terms(idx_ref, geo_ref, first_ref, second_ref, out_ref, row_ref, *, cap, count):
+    def add_rows(q, _):
+        for i in range(3):
+            first = second = None
+            for m in range(8):
+                rows = pl.ds((24 * 8) * q + 8 * i + m, 8, stride=24)
+                one, two = first_ref[rows, :], second_ref[rows, :]
+                first = one if m == 0 else first + pltpu.roll(one, 128 - m, 1)
+                second = two if m == 0 else second + two
+            row_ref[pl.ds(pl.multiple_of(i * count + 8 * q, 8), 8), :] = first
+            row_ref[pl.ds(pl.multiple_of((3 + i) * count + 8 * q, 8), 8), :] = second
+        return 0
+
+    lax.fori_loop(0, count // 8, add_rows, 0)
+
     def body(p, _):
         (oa, ra), (ob, rb) = pair_ends(idx_ref, p, count)
         wa = geo_ref[oa, pl.ds(9 * cap + ra, 1), :]
         wb = geo_ref[ob, pl.ds(9 * cap + rb, 1), :]
-        for i in range(3):
-            first = first_ref[p, i]
-            for half in (4, 2, 1):
-                first = first + pltpu.roll(pltpu.roll(first, 8 - half, 0), 128 - half, 1)
-            out_ref[oa, i, pl.ds(ra, 1), :] = wa * first[0:1]
-            second = jnp.sum(second_ref[p, i], axis=0, keepdims=True)
-            out_ref[ob, i, pl.ds(rb, 1), :] = wb * second
-        return 0
-
-    lax.fori_loop(0, count, body, 0, unroll=4)
+        first = row_ref[pl.ds(p, 3, stride=count), :]
+        second = row_ref[pl.ds(3 * count + p, 3, stride=count), :]
+        out_ref[pl.ds(oa * 3 * cap + ra, 3, stride=cap), :] = wa * first
+        out_ref[pl.ds(ob * 3 * cap + rb, 3, stride=cap), :] = wb * second
+        return 0
+
+    lax.fori_loop(0, count, body, 0, unroll=8)
 
 
 def near_tile(col, row):
@@ -241,12 +284,12 @@
 
 
 def sweep_pairs(
-    idx_ref, parts, bases, bufs, tile_mats, sums, *, step, pair0, pairs, group, cap, count, unroll
+    idx_ref, parts, bases, bufs, tile_mats, sums, *, step, pair0, pairs, group, cap, count, unroll, block
 ):
-    def two_pairs(h, _):
-        for j in range(2):
-            src, dst, base = bufs[j], bufs[1 - j], bases[j]
-            g = 2 * h + j
+    def some_pairs(h, _):
+        for j in range(block):
+            src, dst, base = bufs[j % 2], bufs[1 - j % 2], bases[j % 2]
+            g = block * h + j
             local = step * group + g
             pair = pair0 + local
             following = jnp.minimum(pair + 1, pair0 + pairs - 1)
@@ -279,11 +322,12 @@
             if sums is not None:
                 held, first, second = carry
                 for i in range(3):
-                    sums[0][local, i] = first[i] + pltpu.roll(held[i], 8, 1)
-                    sums[1][local, i] = second[i]
-        return 0
-
-    lax.fori_loop(0, group // 2, two_pairs, 0)
+                    at = pl.ds(pl.multiple_of(24 * local + 8 * i, 8), 8)
+                    sums[0][at, :] = first[i] + pltpu.roll(held[i], 8, 1)
+                    sums[1][at, :] = second[i]
+        return 0
+
+    lax.fori_loop(0, group // block, some_pairs, 0)
 
 
 def skew_first_pair(idx_ref, parts, base, buf, pair, *, cap, count):
@@ -313,7 +357,7 @@
     sweep_pairs(
         idx_ref, parts, (base0, base1), (buf0, buf1), tile_mats, None,
         step=step, pair0=pair0, pairs=pairs, group=k_ref.shape[0], cap=cap, count=count,
-        unroll=BUILD_UNROLL,
+        unroll=BUILD_UNROLL, block=2,
     )
 
 
@@ -333,7 +377,7 @@
 
 def apply_kernel(
     idx_ref, geo_ref, x_ref, k_ref, out_ref,
-    first_ref, second_ref, y_ref, base0, base1, buf0, buf1, *, cap, count,
+    first_ref, second_ref, row_ref, y_ref, base0, base1, buf0, buf1, *, cap, count,
 ):
     step = pl.program_id(0)
     parts = ((y_ref, 3),)
@@ -349,43 +393,58 @@
     sweep_pairs(
         idx_ref, parts, (base0, base1), (buf0, buf1), tile_mats, (first_ref, second_ref),
         step=step, pair0=0, pairs=count, group=k_ref.shape[0], cap=cap, count=count,
-        unroll=APPLY_UNROLL,
+        unroll=APPLY_UNROLL, block=4,
     )
 
     @pl.when(step == pl.num_programs(0) - 1)
     def _():
-        return_terms(idx_ref, geo_ref, first_ref, second_ref, out_ref, cap=cap, count=count)
-
-
-def add_up(ask_ref, near_ref, far_ref, accs, out_ref, *, cap):
+        return_terms(
+            idx_ref, geo_ref, first_ref, second_ref, out_ref, row_ref, cap=cap, count=count
+        )
+
+
+def add_up(ask_ref, near_ref, far_ref, accs, out_ref, *, n, cap):
     clusters = out_ref.shape[1]
     for acc in accs:
         acc[...] = jnp.zeros(acc.shape, f32)
 
     def body(d, _):
         for s in range(cap):
-            cn = ask_ref[d, s]
-            cf = ask_ref[d, cap + s]
-            for i in range(3):
-                accs[i][pl.ds(cn, 1), :] += near_ref[d, i, pl.ds(s, 1), :]
-                accs[3 + i][pl.ds(cf, 1), :] += far_ref[d, i, pl.ds(s, 1), :]
-        return 0
-
-    lax.fori_loop(0, near_ref.shape[0], body, 0)
-    for i in range(3):
-        out_ref[i] = accs[i][pl.ds(0, clusters), :] + accs[3 + i][pl.ds(0, clusters), :]
-
-
-def merge_kernel(ask_ref, rn_ref, rf_ref, out_ref, pack_ref, *accs, cap):
-    add_up(ask_ref, rn_ref, rf_ref, accs, out_ref, cap=cap)
-    pack_rows(ask_ref, (out_ref,), pack_ref)
+            for part, ref in enumerate((near_ref, far_ref)):
+                acc = accs[2 * part + s % 2]
+                at = pl.ds(pl.multiple_of(8 * ask_ref[d, part * cap + s], 8), 3)
+                acc[at, :] += ref[pl.ds(d * 3 * cap + s, 3, stride=cap), :]
+        return 0
+
+    lax.fori_loop(0, n, body, 0)
+
+    def total(q, _):
+        at = pl.ds(pl.multiple_of(64 * q, 64), 64)
+        accs[0][at, :] = (accs[0][at, :] + accs[1][at, :]) + (accs[2][at, :] + accs[3][at, :])
+        for i in range(3):
+            out_ref[i, pl.ds(pl.multiple_of(8 * q, 8), 8), :] = accs[0][
+                pl.ds(64 * q + i, 8, stride=8), :
+            ]
+        return 0
+
+    lax.fori_loop(0, clusters // 8, total, 0)
+
+
+def merge_kernel(ask_ref, rn_ref, rf_ref, out_ref, pack_ref, *accs, n, cap):
+    add_up(ask_ref, rn_ref, rf_ref, accs, out_ref, n=n, cap=cap)
+    last = out_ref.shape[1] - 1
+
+    def fetch(c):
+        return [accs[0][pl.ds(pl.multiple_of(8 * jnp.minimum(c, last), 8), 3), :]]
+
+    pack_rows(ask_ref, fetch, pack_ref, n=n, slots=2 * cap, kinds=1)
 
 
 PRODUCTS = ((0, 0), (0, 1), (1, 1), (0, 2), (1, 2), (2, 2))
 
 
-def gram_kernel(ask_ref, rn_ref, rf_ref, v0_ref, v1_ref, out_ref, part_ref, *accs, cap):
-    add_up(ask_ref, rn_ref, rf_ref, accs, out_ref, cap=cap)
+def gram_kernel(ask_ref, rn_ref, rf_ref, v0_ref, v1_ref, out_ref, part_ref, *accs, n, cap):
+    add_up(ask_ref, rn_ref, rf_ref, accs, out_ref, n=n, cap=cap)
     clusters = out_ref.shape[1]
     refs = (v0_ref, v1_ref, out_ref)
     zero = jnp.zeros((8, 128), f32)
@@ -477,6 +536,7 @@
     n = lax.axis_size("dev")
     clusters, _, width = right_side.shape
     near_count = near_owner.shape[0]
+    far_count = far_owner.shape[0]
     cap = max(2, 4 * near_count // n)
     size_all = clusters * n * 3 * width
     x0 = right_side.transpose(1, 0, 2)
@@ -489,33 +549,37 @@
     ask, idx = pl.pallas_call(
         lambda *refs: prep_kernel(*refs, cap=cap, trash=clusters),
         out_shape=(shape((n, slots), jnp.int32), shape((8, 2 * near_count), jnp.int32)),
-        compiler_params=params(),
+        compiler_params=params(60),
         name="prep",
     )(near_owner.T, near_local.T, far_owner.T, far_local.T)
     asked = exchange(ask)
 
-    rows3 = shape((n, 3, cap, width), f32)
-    both = shape((n, 3, 2 * cap, width), f32)
-
-    near_in = exchange(
+    rows3 = shape((n * 3 * cap, width), f32)
+    both = shape((n * 6 * cap, width), f32)
+
+    def flat(array):
+        return array.reshape(-1, width)
+
+    near_out = (
         pl.pallas_call(
-            pack_near_kernel,
-            out_shape=shape((n, 6, cap, width), f32),
+            lambda *refs: pack_near_kernel(*refs, n=n, slots=cap),
+            out_shape=shape((n * 6 * cap, width), f32),
             in_specs=[SM, VM, VM],
-            scratch_shapes=[pltpu.VMEM((3, clusters, width), f32)],
-            compiler_params=params(),
+            scratch_shapes=[pltpu.VMEM((3 * clusters, width), f32)],
+            compiler_params=params(60),
             cost_estimate=cost(4.0),
             name="pack_near",
-        )(asked, vertices.transpose(1, 0, 2), panels.transpose(1, 0, 2))
+        )(asked, flat(vertices.transpose(1, 0, 2)), flat(panels.transpose(1, 0, 2)))
     )
+    near_in = exchange(near_out)
     x0_out = pl.pallas_call(
-        pack_kernel,
+        lambda *refs: pack_kernel(*refs, n=n, slots=2 * cap),
         out_shape=both,
         in_specs=[SM, VM],
         compiler_params=params(),
         cost_estimate=cost(3.0),
         name="pack",
-    )(asked, x0)
+    )(asked, flat(x0))
     x0_in = exchange(x0_out)
 
     group = 8
@@ -539,17 +603,21 @@
         in_specs=[SM, whole(n, 6, cap, width)],
         out_specs=(pl.BlockSpec(k_block, lambda g: (g, 0, 0, 0)), whole(*rows10)),
         scratch_shapes=skews(9),
-        compiler_params=params(),
+        compiler_params=params(44),
         cost_estimate=cost(30.0),
         name="build",
-    )(idx, near_in)
+    )(idx, near_in.reshape(n, 6, cap, width))
 
     def far_product(received):
         return pl.pallas_call(
             lambda *refs: far_kernel(*refs, cap=cap),
             out_shape=rows3,
             in_specs=[SM, VM, VM, VM],
-            compiler_params=params(),
+            scratch_shapes=[
+                pltpu.VMEM((far_count * 48, width), f32),
+                pltpu.VMEM((6 * far_count, width), f32),
+            ],
+            compiler_params=params(8),
             cost_estimate=cost(5.0),
             name="far",
         )(idx, received, far_left, far_right)
@@ -564,13 +632,13 @@
         out_specs=pl.BlockSpec(k_block, lambda g: (g + early // group, 0, 0, 0)),
         scratch_shapes=skews(9),
         input_output_aliases={2: 0},
-        compiler_params=params(),
+        compiler_params=params(44),
         cost_estimate=cost(30.0),
         name="build_rest",
     )(idx, geometry, stored, far_terms)
 
     def apply_stored(received):
-        return exchange(
+        return (
             pl.pallas_call(
                 lambda *refs: apply_kernel(*refs, cap=cap, count=near_count),
                 out_shape=rows3,
@@ -578,24 +646,26 @@
                 in_specs=[
                     SM,
                     whole(*rows10),
-                    whole(*both.shape),
+                    whole(n, 3, 2 * cap, width),
                     pl.BlockSpec(k_block, lambda g: (g, 0, 0, 0)),
                 ],
-                out_specs=whole(n, 3, cap, width),
-                scratch_shapes=[pltpu.VMEM((near_count, 3, 8, width), f32)] * 2
+                out_specs=whole(*rows3.shape),
+                scratch_shapes=[pltpu.VMEM((near_count * 24, width), f32)] * 2
+                + [pltpu.VMEM((6 * near_count, width), f32)]
                 + [pltpu.VMEM((n, 3 * cap, width), f32)]
                 + skews(3),
-                compiler_params=params(),
+                compiler_params=params(44),
                 cost_estimate=cost(18.0),
                 name="apply",
-            )(idx, geometry, received, stored)
+            )(idx, geometry, received.reshape(n, 3, 2 * cap, width), stored)
         )
 
-    near_back = apply_stored(x0_in)
-
-    accs = [pltpu.VMEM((clusters + 8, width), f32)] * 6
+    near_terms = apply_stored(x0_in)
+    near_back = exchange(near_terms)
+
+    accs = [pltpu.VMEM(((clusters + 1) * 8, width), f32)] * 4
     x1, x1_out = pl.pallas_call(
-        lambda *refs: merge_kernel(*refs, cap=cap),
+        lambda *refs: merge_kernel(*refs, n=n, cap=cap),
         out_shape=(shape((3, clusters, width), f32), both),
         in_specs=[SM, VM, VM],
         scratch_shapes=accs,
@@ -604,11 +674,13 @@
         name="merge",
     )(asked, near_back, far_back)
     x1_in = exchange(x1_out)
-    far_back2 = exchange(far_product(x1_in))
-    near_back2 = apply_stored(x1_in)
+    far_terms2 = far_product(x1_in)
+    far_back2 = exchange(far_terms2)
+    near_terms2 = apply_stored(x1_in)
+    near_back2 = exchange(near_terms2)
 
     x2, part = pl.pallas_call(
-        lambda *refs: gram_kernel(*refs, cap=cap),
+        lambda *refs: gram_kernel(*refs, n=n, cap=cap),
         out_shape=(shape((3, clusters, width), f32), shape((n, 128), f32)),
         in_specs=[SM, VM, VM, VM, VM],
         scratch_shapes=accs,

time: 255 us -> 236 us (0.925)
  Pallas kernels: 122 us -> 104 us
  blocking collectives: 103 us -> 100 us
    pallas_call x2, Pallas kernels: 42.2 us -> 33.4 us  [apply_stored(): pl.pallas_call(lambda *refs: apply_kernel(*refs, cap=cap, count=near_coun...]
    pallas_call x2, Pallas kernels: 9.69 us -> 6.02 us  [far_product(): pl.pallas_call(lambda *refs: far_kernel(*refs, cap=cap), out_shape=rows3,...]
    pallas_call x4, Pallas kernels: 14.7 us -> 11.8 us  [the longest x1 3.01 us: per_device(): pl.pallas_call(lambda *refs: gram_kernel(*refs, n=n, cap=cap), out_shape=...]
  transfers between devices with their start and end apart: 3 -> 3, of which waited for: 1 -> 1; matrix products, arithmetic and copies ran while one was open for 0% -> 0% of each run, Pallas kernels for 20% -> 19%
where the time goes in v3:
time: 236 us; the launch traced here: 235 us
  Pallas kernels  104 us (44%)
  blocking collectives  100 us (42%)
  waiting for transfers between devices  17.7 us (8%)
  starting transfers between devices  9.78 us (4%)
  local copies, waits for them, and re-layouts  2.84 us (1%)
    all_to_all x6, blocking collectives, exchange(): return lax.all_to_all(block, 'dev', split_axis=0, concat_axis=0, tiled=True)  100 us
    pallas_call x2, Pallas kernels, apply_stored(): pl.pallas_call(lambda *refs: apply_kernel(*refs, cap=cap, count=near_coun...  33.4 us
    pallas_call x1, Pallas kernels, per_device(): pl.pallas_call(lambda *refs: build_kernel(*refs, pairs=early, cap=cap, co...  26 us
    pallas_call x1, Pallas kernels, per_device(): pl.pallas_call(lambda *refs: build_rest_kernel(*refs, pair0=early, cap=ca...  22.7 us
    all_to_all x3, waiting for transfers between devices, exchange(): return lax.all_to_all(block, 'dev', split_axis=0, concat_axis=0, tiled=True)  17.7 us
    all_to_all x3, starting transfers between devices, exchange(): return lax.all_to_all(block, 'dev', split_axis=0, concat_axis=0, tiled=True)  9.78 us
    pallas_call x2, Pallas kernels, far_product(): pl.pallas_call(lambda *refs: far_kernel(*refs, cap=cap), out_shape=rows3,...  6.02 us
  transfers between devices with their start and end apart: 3, of which 1 were waited for; matrix products, arithmetic and copies ran while one was open for 0% of the time, Pallas kernels for 19%

profile of v3, /device:TPU:0, one launch (start us, length us, event | category | flops | bytes accessed | tf_op | source)
XLA Modules:
  0.0 235.4 jit_solution(10370911817299614281)
XLA Ops:
  0.6 0.0 copy-start.4
  0.6 1.7 prep.1
  2.3 14.5 %all_to_all.97 = s32[32,1,128]{2,1,0:T(1,128)} all-to-all(s32[32,1,128]{2,1,0:T(1,128)} %bitcast.64), channel_id=1, replica_groups=mesh['dev'=32] {'dev'}, dimensions={0} | all-to-all | bytes 32768 | tf_op jit(solution)/shard_map/all_to_all | solution.py:546
  16.9 2.9 %pack_near.1 = f32[1536,128]{1,0:T(8,128)} custom-call(s32[32,128]{1,0:T(8,128)} %bitcast.55, f32[192,128]{1,0:T(8,128)} %bitcast.62, s32[192,128]{1,0:T(8,128)} %bitcast.63), custom_call_target="tpu_custom_call" | custom-call | bytes 12000000 | tf_op jit(solution)/shard_map/pack_near/pallas_call | solution.py:564
  19.8 2.6 %all-to-all-start.1 = ((f32[32,48,128]{2,1,0:T(8,128)}), f32[32,48,128]{2,1,0:T(8,128)S(1)}, u32[]{:S(2)}, u32[]{:S(2)}) async-start(f32[32,48,128]{2,1,0:T(8,128)} %bitcast.61), calls=%async_computation.1 | async-start | bytes 1572864 | tf_op jit(solution)/shard_map/all_to_all | solution.py:546
  22.4 0.0 copy-start.6
  22.4 0.0 copy-done.4
  22.4 0.0 copy-done.5
  22.5 2.9 %pack.1 = f32[1536,128]{1,0:T(8,128)} custom-call(s32[32,128]{1,0:T(8,128)S(1)} %bitcast.56, f32[192,128]{1,0:T(8,128)S(1)} %bitcast.51), custom_call_target="tpu_custom_call" | custom-call | bytes 9000000 | tf_op jit(solution)/shard_map/pack/pallas_call | solution.py:575
  25.3 17.7 %all-to-all-done.1 = f32[32,48,128]{2,1,0:T(8,128)S(1)} async-done(((f32[32,48,128]{2,1,0:T(8,128)}), f32[32,48,128]{2,1,0:T(8,128)S(1)}, u32[]{:S(2)}, u32[]{:S(2)}) %all-to-all-start.1) | async-done | bytes 786464 | tf_op jit(solution)/shard_map/all_to_all | solution.py:546
  43.0 3.5 %all-to-all-start.2 = ((f32[32,48,128]{2,1,0:T(8,128)}), f32[32,48,128]{2,1,0:T(8,128)S(1)}, u32[]{:S(2)}, u32[]{:S(2)}) async-start(f32[32,48,128]{2,1,0:T(8,128)} %bitcast.15), calls=%async_computation.2 | async-start | bytes 1572864 | tf_op jit(solution)/shard_map/all_to_all | solution.py:546
  46.5 0.0 copy-done.6
  46.6 26.0 %build.1 = (f32[64,6,128,128]{3,2,1,0:T(8,128)}, f32[32,80,128]{2,1,0:T(8,128)S(1)}) custom-call(s32[8,128]{1,0:T(8,128)S(1)} %copy-done.6, f32[32,6,8,128]{3,2,1,0:T(8,128)S(1)} %bitcast.44), custom_call_target="tpu_custom_call" | custom-call | bytes 90000000 | tf_op jit(solution)/shard_map/build/pallas_call | solution.py:599
  72.6 0.0 all-to-all-done.2
  72.6 1.4 copy-done
  74.0 1.4 copy-done.2
  75.4 2.6 %far.2.refs_3_ = f32[768,128]{1,0:T(8,128)S(1)} custom-call(s32[8,128]{1,0:T(8,128)S(1)} %copy-done.6, f32[1536,128]{1,0:T(8,128)S(1)} %bitcast.39, f32[64,16,384]{2,1,0:T(8,128)S(1)} %copy-done, f32[64,16,384]{2,1,0:T(8,128)S(1)} %copy-done.2), custom_call_target="tpu_custom_call" | custom-call | bytes 15000000 | tf_op jit(solution)/shard_map/far/pallas_call | solution.py:612
  78.0 22.7 %build_rest.1.refs_3_ = f32[64,6,128,128]{3,2,1,0:T(8,128)} custom-call(s32[8,128]{1,0:T(8,128)S(1)} %copy-done.6, f32[32,80,128]{2,1,0:T(8,128)S(1)} %get-tuple-element.14.refs_1_, f32[64,6,128,128]{3,2,1,0:T(8,128)} %get-tuple-element.15.refs_2_, f32[768,128]{1,0:T(8,128)S(1)} %far.2.refs_3_), custom_call_target="tpu_custom_call", output_to_operand_aliasing={{}: (2, {})} | custom-call | bytes 90000000 | tf_op jit(solution)/shard_map/build_rest/pallas_call | solution.py:627
  100.8 16.7 %apply.2 = f32[768,128]{1,0:T(8,128)S(1)} custom-call(s32[8,128]{1,0:T(8,128)S(1)} %copy-done.6, f32[32,80,128]{2,1,0:T(8,128)S(1)} %get-tuple-element.14.refs_1_, f32[32,3,16,128]{3,2,1,0:T(8,128)S(1)} %bitcast.40, f32[64,6,128,128]{3,2,1,0:T(8,128)} %build_rest.1.refs_3_), custom_call_target="tpu_custom_call" | custom-call | bytes 54000000 | tf_op jit(solution)/shard_map/apply/pallas_call | solution.py:642
  117.5 18.9 %all_to_all.98 = f32[32,24,128]{2,1,0:T(8,128)S(1)} all-to-all(f32[32,24,128]{2,1,0:T(8,128)S(1)} %bitcast.50), channel_id=1, replica_groups=mesh['dev'=32] {'dev'}, dimensions={0} | all-to-all | bytes 786432 | tf_op jit(solution)/shard_map/all_to_all | solution.py:546
  136.4 15.6 %all_to_all.99 = f32[32,24,128]{2,1,0:T(8,128)S(1)} all-to-all(f32[32,24,128]{2,1,0:T(8,128)S(1)} %bitcast.43), channel_id=1, replica_groups=mesh['dev'=32] {'dev'}, dimensions={0} | all-to-all | bytes 786432 | tf_op jit(solution)/shard_map/all_to_all | solution.py:546
  151.9 3.0 %merge.1 = (f32[3,64,128]{2,1,0:T(8,128)S(1)}, f32[1536,128]{1,0:T(8,128)S(1)}) custom-call(s32[32,128]{1,0:T(8,128)S(1)} %bitcast.57, f32[768,128]{1,0:T(8,128)S(1)} %bitcast.45, f32[768,128]{1,0:T(8,128)S(1)} %bitcast.46), custom_call_target="tpu_custom_call" | custom-call | bytes 15000000 | tf_op jit(solution)/shard_map/merge/pallas_call | solution.py:667
  154.9 22.9 %all_to_all.100 = f32[32,48,128]{2,1,0:T(8,128)S(1)} all-to-all(f32[32,48,128]{2,1,0:T(8,128)S(1)} %bitcast.54), channel_id=1, replica_groups=mesh['dev'=32] {'dev'}, dimensions={0} | all-to-all | bytes 1572864 | tf_op jit(solution)/shard_map/all_to_all | solution.py:546
  177.8 0.0 copy-done.3
  177.8 3.4 %far.3 = f32[768,128]{1,0:T(8,128)} custom-call(s32[8,128]{1,0:T(8,128)S(1)} %copy-done.6, f32[1536,128]{1,0:T(8,128)S(1)} %bitcast.41, f32[64,16,384]{2,1,0:T(8,128)S(1)} %copy-done.1, f32[64,16,384]{2,1,0:T(8,128)S(1)} %copy-done.3), custom_call_target="tpu_custom_call" | custom-call | bytes 15000000 | tf_op jit(solution)/shard_map/far/pallas_call | solution.py:612
  181.2 3.6 %all-to-all-start.7 = ((f32[32,24,128]{2,1,0:T(8,128)}), f32[32,24,128]{2,1,0:T(8,128)S(1)}, u32[]{:S(2)}, u32[]{:S(2)}) async-start(f32[32,24,128]{2,1,0:T(8,128)} %bitcast.27), calls=%async_computation.7 | async-start | bytes 786432 | tf_op jit(solution)/shard_map/all_to_all | solution.py:546
  184.8 16.7 %apply.3 = f32[768,128]{1,0:T(8,128)S(1)} custom-call(s32[8,128]{1,0:T(8,128)S(1)} %copy-done.6, f32[32,80,128]{2,1,0:T(8,128)S(1)} %get-tuple-element.14.refs_1_, f32[32,3,16,128]{3,2,1,0:T(8,128)S(1)} %bitcast.42, f32[64,6,128,128]{3,2,1,0:T(8,128)} %build_rest.1.refs_3_), custom_call_target="tpu_custom_call" | custom-call | bytes 54000000 | tf_op jit(solution)/shard_map/apply/pallas_call | solution.py:642
  201.6 0.0 all-to-all-done.7
  201.6 18.9 %all_to_all.101 = f32[32,24,128]{2,1,0:T(8,128)S(1)} all-to-all(f32[32,24,128]{2,1,0:T(8,128)S(1)} %bitcast.49), channel_id=1, replica_groups=mesh['dev'=32] {'dev'}, dimensions={0} | all-to-all | bytes 786432 | tf_op jit(solution)/shard_map/all_to_all | solution.py:546
  220.5 3.0 %gram.1 = (f32[3,64,128]{2,1,0:T(8,128)S(1)}, f32[32,128]{1,0:T(8,128)S(1)}) custom-call(s32[32,128]{1,0:T(8,128)S(1)} %bitcast.58, f32[768,128]{1,0:T(8,128)S(1)} %bitcast.48, f32[768,128]{1,0:T(8,128)S(1)} %bitcast.47, f32[3,64,128]{2,1,0:T(8,128)S(1)} %bitcast.52, f32[3,64,128]{2,1,0:T(8,128)S(1)} %get-tuple-element.17.refs_4_.refs_2_), custom_call_target="tpu_custom_call" | custom-call | bytes 15000000 | tf_op jit(solution)/shard_map/gram/pallas_call | solution.py:682
  223.5 9.5 %all_to_all.102 = f32[32,1,128]{2,1,0:T(1,128)S(1)} all-to-all(f32[32,1,128]{2,1,0:T(1,128)S(1)} %bitcast.60), channel_id=1, replica_groups=mesh['dev'=32] {'dev'}, dimensions={0} | all-to-all | bytes 32768 | tf_op jit(solution)/shard_map/all_to_all | solution.py:546
  232.9 2.5 %final.1 = (f32[2,3,64,128]{3,2,1,0:T(8,128)}, f32[2,3]{1,0:T(2,128)}) custom-call(f32[32,128]{1,0:T(8,128)S(1)} %bitcast.59, f32[3,64,128]{2,1,0:T(8,128)S(1)} %bitcast.53, f32[3,64,128]{2,1,0:T(8,128)S(1)} %get-tuple-element.17.refs_4_.refs_2_, f32[3,64,128]{2,1,0:T(8,128)S(1)} %get-tuple-element.19.refs_3_), custom_call_target="tpu_custom_call" | custom-call | tf_op jit(solution)/shard_map/final/pallas_call | solution.py:692
  (6 shorter events, 0.0 us)
Async XLA Ops:
  0.6 21.8 %copy-start.4 = (f32[64,3,128]{2,0,1:T(8,128)S(1)}, f32[64,3,128]{2,0,1:T(8,128)}, u32[]{:S(2)}) copy-start(f32[64,3,128]{2,0,1:T(8,128)} %param.9) | copy-start | bytes 294916
  16.9 5.6 %copy-start.5 = (s32[32,1,128]{2,1,0:T(1,128)S(1)}, s32[32,1,128]{2,1,0:T(1,128)}, u32[]{:S(2)}) copy-start(s32[32,1,128]{2,1,0:T(1,128)} %all_to_all.97) | copy-start | bytes 49156
  19.8 23.2 %all-to-all-start.1 = ((f32[32,48,128]{2,1,0:T(8,128)}), f32[32,48,128]{2,1,0:T(8,128)S(1)}, u32[]{:S(2)}, u32[]{:S(2)}) async-start(f32[32,48,128]{2,1,0:T(8,128)} %bitcast.61), calls=%async_computation.1 | async-start | bytes 1572864 | tf_op jit(solution)/shard_map/all_to_all | solution.py:546
  22.4 24.1 %copy-start.6 = (s32[8,128]{1,0:T(8,128)S(1)}, s32[8,128]{1,0:T(8,128)}, u32[]{:S(2)}) copy-start(s32[8,128]{1,0:T(8,128)} %get-tuple-element.13.refs_0_) | copy-start | bytes 12292
  43.0 29.6 %all-to-all-start.2 = ((f32[32,48,128]{2,1,0:T(8,128)}), f32[32,48,128]{2,1,0:T(8,128)S(1)}, u32[]{:S(2)}, u32[]{:S(2)}) async-start(f32[32,48,128]{2,1,0:T(8,128)} %bitcast.15), calls=%async_computation.2 | async-start | bytes 1572864 | tf_op jit(solution)/shard_map/all_to_all | solution.py:546
  72.6 1.4 copy-start
  74.0 1.4 copy-start.2
  136.4 41.4 %copy-start.1 = (f32[64,16,384]{2,1,0:T(8,128)S(1)}, f32[64,16,384]{2,1,0:T(8,128)}, u32[]{:S(2)}) copy-start(f32[64,16,384]{2,1,0:T(8,128)} %refs_2_.3) | copy-start | bytes 4718596
  136.4 41.4 %copy-start.3 = (f32[64,16,384]{2,1,0:T(8,128)S(1)}, f32[64,16,384]{2,1,0:T(8,128)}, u32[]{:S(2)}) copy-start(f32[64,16,384]{2,1,0:T(8,128)} %refs_3_.3) | copy-start | bytes 4718596
  181.2 20.4 %all-to-all-start.7 = ((f32[32,24,128]{2,1,0:T(8,128)}), f32[32,24,128]{2,1,0:T(8,128)S(1)}, u32[]{:S(2)}, u32[]{:S(2)}) async-start(f32[32,24,128]{2,1,0:T(8,128)} %bitcast.27), calls=%async_computation.7 | async-start | bytes 786432 | tf_op jit(solution)/shard_map/all_to_all | solution.py:546

commit v4 on v3

--- a/solution.py
+++ b/solution.py
@@ -17,7 +17,6 @@
 f32 = jnp.float32
 VM = pl.BlockSpec(memory_space=pltpu.VMEM)
 SM = pl.BlockSpec(memory_space=pltpu.SMEM)
-ANY = pl.BlockSpec(memory_space=pl.ANY)
 
 
 def params(mib=8):
@@ -137,9 +136,9 @@
         coef_a = jnp.sum(sum(left[i] * xa[i] for i in range(3)), axis=1, keepdims=True)
         rank = left[0].shape[0]
         for i in range(3):
-            for k, part in ((i, left[i] * coef_b), (3 + i, right[i] * coef_a)):
+            for k, term in ((i, left[i] * coef_b), (3 + i, right[i] * coef_a)):
                 at = pl.ds(pl.multiple_of((6 * f + k) * 8, 8), 8)
-                sum_ref[at, :] = sum(part[8 * h : 8 * h + 8] for h in range(rank // 8))
+                sum_ref[at, :] = sum(term[8 * h : 8 * h + 8] for h in range(rank // 8))
         return 0
 
     lax.fori_loop(0, count, body, 0, unroll=8)
@@ -163,7 +162,7 @@
     lax.fori_loop(0, count, send, 0, unroll=8)
 
 
-def slot_geometry(in_ref, geo_ref, *, cap):
+def slot_geometry(in_ref, geo_ref, w_ref, *, cap):
     n = in_ref.shape[0]
 
     def body(d, _):
@@ -183,7 +182,7 @@
             for i in range(3):
                 point = sum((big if m == s else small) * corner[m][i] for m in range(3))
                 geo_ref[d, pl.ds((3 * s + i) * cap, cap), :] = point
-        geo_ref[d, pl.ds(9 * cap, cap), :] = weight
+        w_ref[d] = weight
         return 0
 
     lax.fori_loop(0, n, body, 0)
@@ -211,11 +210,10 @@
         dst_ref[c, pl.ds(pl.multiple_of(8 * t, 8), 8), :] = pltpu.roll(base_ref[c], 8 * t, 1)
 
 
-def weighted(geo_ref, x_ref, y_ref, *, cap):
+def weighted(w_ref, x_ref, y_ref, *, cap):
     def body(d, _):
-        weight = geo_ref[d, pl.ds(9 * cap, cap), :]
         for i in range(3):
-            y_ref[d, pl.ds(i * cap, cap), :] = weight * x_ref[d, i, pl.ds(0, cap), :]
+            y_ref[d, pl.ds(i * cap, cap), :] = w_ref[d] * x_ref[d, i, pl.ds(0, cap), :]
         return 0
 
     lax.fori_loop(0, x_ref.shape[0], body, 0, unroll=4)
@@ -232,7 +230,7 @@
     return firsts, second
 
 
-def return_terms(idx_ref, geo_ref, first_ref, second_ref, out_ref, row_ref, *, cap, count):
+def return_terms(idx_ref, w_ref, first_ref, second_ref, out_ref, row_ref, *, cap, count):
     def add_rows(q, _):
         for i in range(3):
             first = second = None
@@ -249,8 +247,8 @@
 
     def body(p, _):
         (oa, ra), (ob, rb) = pair_ends(idx_ref, p, count)
-        wa = geo_ref[oa, pl.ds(9 * cap + ra, 1), :]
-        wb = geo_ref[ob, pl.ds(9 * cap + rb, 1), :]
+        wa = w_ref[oa, pl.ds(ra, 1), :]
+        wb = w_ref[ob, pl.ds(rb, 1), :]
         first = row_ref[pl.ds(p, 3, stride=count), :]
         second = row_ref[pl.ds(3 * count + p, 3, stride=count), :]
         out_ref[pl.ds(oa * 3 * cap + ra, 3, stride=cap), :] = wa * first
@@ -284,15 +282,15 @@
 
 
 def sweep_pairs(
-    idx_ref, parts, bases, bufs, tile_mats, sums, *, step, pair0, pairs, group, cap, count, unroll, block
+    idx_ref, parts, bases, bufs, tile_mats, sums, *, step, pairs, group, cap, count, unroll, block
 ):
     def some_pairs(h, _):
         for j in range(block):
             src, dst, base = bufs[j % 2], bufs[1 - j % 2], bases[j % 2]
             g = block * h + j
             local = step * group + g
-            pair = pair0 + local
-            following = jnp.minimum(pair + 1, pair0 + pairs - 1)
+            pair = local
+            following = jnp.minimum(pair + 1, pairs - 1)
             skew_start(idx_ref, parts, base, following, cap=cap, count=count)
             _, (ob, rb) = pair_ends(idx_ref, pair, count)
             row = [
@@ -340,13 +338,14 @@
     lax.fori_loop(0, 16, body, 0, unroll=4)
 
 
-def build_blocks(idx_ref, geo_ref, k_ref, base0, base1, buf0, buf1, *, pair0, pairs, cap, count):
+def build_kernel(idx_ref, in_ref, k_ref, w_ref, geo_ref, base0, base1, buf0, buf1, *, cap, count):
     step = pl.program_id(0)
     parts = ((geo_ref, 9),)
 
     @pl.when(step == 0)
     def _():
-        skew_first_pair(idx_ref, parts, base1, buf0, pair0, cap=cap, count=count)
+        slot_geometry(in_ref, geo_ref, w_ref, cap=cap)
+        skew_first_pair(idx_ref, parts, base1, buf0, 0, cap=cap, count=count)
 
     def tile_mats(g, tile, col, row):
         mats = near_tile(col, row)
@@ -356,51 +355,48 @@
 
     sweep_pairs(
         idx_ref, parts, (base0, base1), (buf0, buf1), tile_mats, None,
-        step=step, pair0=pair0, pairs=pairs, group=k_ref.shape[0], cap=cap, count=count,
+        step=step, pairs=count, group=k_ref.shape[0], cap=cap, count=count,
         unroll=BUILD_UNROLL, block=2,
     )
 
 
-def build_kernel(idx_ref, in_ref, k_ref, geo_ref, *skews, pairs, cap, count):
-    @pl.when(pl.program_id(0) == 0)
-    def _():
-        slot_geometry(in_ref, geo_ref, cap=cap)
-
-    build_blocks(idx_ref, geo_ref, k_ref, *skews, pair0=0, pairs=pairs, cap=cap, count=count)
-
-
-def build_rest_kernel(idx_ref, geo_ref, old_ref, far_ref, k_ref, *skews, pair0, cap, count):
-    build_blocks(
-        idx_ref, geo_ref, k_ref, *skews, pair0=pair0, pairs=count - pair0, cap=cap, count=count
-    )
-
-
 def apply_kernel(
-    idx_ref, geo_ref, x_ref, k_ref, out_ref,
-    first_ref, second_ref, row_ref, y_ref, base0, base1, buf0, buf1, *, cap, count,
+    idx_ref, w_ref, x_ref, k_hbm, out_ref,
+    first_ref, second_ref, row_ref, y_ref, k_ref, sems, base0, base1, buf0, buf1, *, cap, count,
 ):
-    step = pl.program_id(0)
+    depth, part = k_ref.shape[:2]
+    groups = count // part
     parts = ((y_ref, 3),)
 
-    @pl.when(step == 0)
-    def _():
-        weighted(geo_ref, x_ref, y_ref, cap=cap)
-        skew_first_pair(idx_ref, parts, base1, buf0, 0, cap=cap, count=count)
-
-    def tile_mats(g, tile, col, row):
-        return [k_ref[g, m, tile, :] for m in range(6)]
-
-    sweep_pairs(
-        idx_ref, parts, (base0, base1), (buf0, buf1), tile_mats, (first_ref, second_ref),
-        step=step, pair0=0, pairs=count, group=k_ref.shape[0], cap=cap, count=count,
-        unroll=APPLY_UNROLL, block=4,
-    )
-
-    @pl.when(step == pl.num_programs(0) - 1)
-    def _():
-        return_terms(
-            idx_ref, geo_ref, first_ref, second_ref, out_ref, row_ref, cap=cap, count=count
+    def fetch(q, slot):
+        return pltpu.make_async_copy(k_hbm.at[pl.ds(q * part, part)], k_ref.at[slot], sems.at[slot])
+
+    for q in range(min(depth, groups)):
+        fetch(q, q).start()
+    weighted(w_ref, x_ref, y_ref, cap=cap)
+    skew_first_pair(idx_ref, parts, base1, buf0, 0, cap=cap, count=count)
+
+    def body(q, _):
+        slot = lax.rem(q, depth)
+        fetch(q, slot).wait()
+
+        def tile_mats(g, tile, col, row):
+            return [k_ref[slot, g, m, tile, :] for m in range(6)]
+
+        sweep_pairs(
+            idx_ref, parts, (base0, base1), (buf0, buf1), tile_mats, (first_ref, second_ref),
+            step=q, pairs=count, group=part, cap=cap, count=count,
+            unroll=APPLY_UNROLL, block=part,
         )
+
+        @pl.when(q + depth < groups)
+        def _():
+            fetch(q + depth, slot).start()
+
+        return 0
+
+    lax.fori_loop(0, groups, body, 0)
+    return_terms(idx_ref, w_ref, first_ref, second_ref, out_ref, row_ref, cap=cap, count=count)
 
 
 def add_up(ask_ref, near_ref, far_ref, accs, out_ref, *, n, cap):
@@ -583,10 +579,9 @@
     x0_in = exchange(x0_out)
 
     group = 8
-    early = near_count // 2
     k_block = (group, 6, width, width)
     k_shape = shape((near_count, 6, width, width), f32)
-    rows10 = (n, 10 * cap, width)
+    weight_shape = (n, cap, width)
 
     def whole(*dims):
         return pl.BlockSpec(dims, lambda g: (0,) * len(dims))
@@ -596,15 +591,15 @@
             pltpu.VMEM((comps, width, width), f32)
         ] * 2
 
-    stored, geometry = pl.pallas_call(
-        lambda *refs: build_kernel(*refs, pairs=early, cap=cap, count=near_count),
-        out_shape=(k_shape, shape(rows10, f32)),
-        grid=(early // group,),
+    stored, weights = pl.pallas_call(
+        lambda *refs: build_kernel(*refs, cap=cap, count=near_count),
+        out_shape=(k_shape, shape(weight_shape, f32)),
+        grid=(near_count // group,),
         in_specs=[SM, whole(n, 6, cap, width)],
-        out_specs=(pl.BlockSpec(k_block, lambda g: (g, 0, 0, 0)), whole(*rows10)),
-        scratch_shapes=skews(9),
+        out_specs=(pl.BlockSpec(k_block, lambda g: (g, 0, 0, 0)), whole(*weight_shape)),
+        scratch_shapes=[pltpu.VMEM((n, 9 * cap, width), f32)] + skews(9),
         compiler_params=params(44),
-        cost_estimate=cost(30.0),
+        cost_estimate=cost(50.0),
         name="build",
     )(idx, near_in.reshape(n, 6, cap, width))
 
@@ -624,40 +619,22 @@
 
     far_terms = far_product(x0_in)
     far_back = exchange(far_terms)
-    stored = pl.pallas_call(
-        lambda *refs: build_rest_kernel(*refs, pair0=early, cap=cap, count=near_count),
-        out_shape=k_shape,
-        grid=((near_count - early) // group,),
-        in_specs=[SM, whole(*rows10), ANY, ANY],
-        out_specs=pl.BlockSpec(k_block, lambda g: (g + early // group, 0, 0, 0)),
-        scratch_shapes=skews(9),
-        input_output_aliases={2: 0},
-        compiler_params=params(44),
-        cost_estimate=cost(30.0),
-        name="build_rest",
-    )(idx, geometry, stored, far_terms)
 
     def apply_stored(received):
         return (
             pl.pallas_call(
                 lambda *refs: apply_kernel(*refs, cap=cap, count=near_count),
                 out_shape=rows3,
-                grid=(near_count // group,),
-                in_specs=[
-                    SM,
-                    whole(*rows10),
-                    whole(n, 3, 2 * cap, width),
-                    pl.BlockSpec(k_block, lambda g: (g, 0, 0, 0)),
-                ],
-                out_specs=whole(*rows3.shape),
+                in_specs=[SM, VM, VM, pl.BlockSpec(memory_space=pl.ANY)],
                 scratch_shapes=[pltpu.VMEM((near_count * 24, width), f32)] * 2
                 + [pltpu.VMEM((6 * near_count, width), f32)]
                 + [pltpu.VMEM((n, 3 * cap, width), f32)]
+                + [pltpu.VMEM((4, 4, 6, width, width), f32), pltpu.SemaphoreType.DMA((4,))]
                 + skews(3),
                 compiler_params=params(44),
                 cost_estimate=cost(18.0),
                 name="apply",
-            )(idx, geometry, received.reshape(n, 3, 2 * cap, width), stored)
+            )(idx, weights, received.reshape(n, 3, 2 * cap, width), stored)
         )
 
     near_terms = apply_stored(x0_in)

time: 236 us -> 232 us (0.983)
  blocking collectives: 100 us -> 77.9 us
  waiting for transfers between devices: 17.7 us -> 36.1 us
  starting transfers between devices: 9.78 us -> 15.6 us
  Pallas kernels: 104 us -> 98.3 us
    all_to_all x6 -> x5, blocking collectives: 100 us -> 77.9 us  [exchange(): return lax.all_to_all(block, 'dev', split_axis=0, concat_axis=0, tiled=True)]
    all_to_all x3 -> x4, waiting for transfers between devices: 17.7 us -> 36.1 us  [exchange(): return lax.all_to_all(block, 'dev', split_axis=0, concat_axis=0, tiled=True)]
    all_to_all x3 -> x4, starting transfers between devices: 9.78 us -> 15.6 us  [exchange(): return lax.all_to_all(block, 'dev', split_axis=0, concat_axis=0, tiled=True)]
    pallas_call x2 -> x1, Pallas kernels: 48.8 us -> 46 us  [per_device(): pl.pallas_call(lambda *refs: build_kernel(*refs, cap=cap, count=near_coun...]
  transfers between devices with their start and end apart: 3 -> 4, of which waited for: 1 -> 3; matrix products, arithmetic and copies ran while one was open for 0% -> 0% of each run, Pallas kernels for 19% -> 23%
where the time goes in v4:
time: 232 us
  Pallas kernels  98.3 us (42%)
  blocking collectives  77.9 us (34%)
  waiting for transfers between devices  36.1 us (16%)
  starting transfers between devices  15.6 us (7%)
  local copies, waits for them, and re-layouts  2.82 us (1%)
    all_to_all x5, blocking collectives, exchange(): return lax.all_to_all(block, 'dev', split_axis=0, concat_axis=0, tiled=True)  77.9 us
    pallas_call x1, Pallas kernels, per_device(): pl.pallas_call(lambda *refs: build_kernel(*refs, cap=cap, count=near_coun...  46 us
    all_to_all x4, waiting for transfers between devices, exchange(): return lax.all_to_all(block, 'dev', split_axis=0, concat_axis=0, tiled=True)  36.1 us
    pallas_call x2, Pallas kernels, apply_stored(): pl.pallas_call(lambda *refs: apply_kernel(*refs, cap=cap, count=near_coun...  31.2 us
    all_to_all x4, starting transfers between devices, exchange(): return lax.all_to_all(block, 'dev', split_axis=0, concat_axis=0, tiled=True)  15.6 us
    pallas_call x2, Pallas kernels, far_product(): pl.pallas_call(lambda *refs: far_kernel(*refs, cap=cap), out_shape=rows3,...  5.24 us
  transfers between devices with their start and end apart: 4, of which 3 were waited for; matrix products, arithmetic and copies ran while one was open for 0% of the time, Pallas kernels for 23%

profile of v4, /device:TPU:0, one launch (start us, length us, event | category | flops | bytes accessed | tf_op | source)
XLA Modules:
  0.0 231.5 jit_solution(17916121859707005271)
XLA Ops:
  0.6 0.0 copy-start.3
  0.6 1.7 prep.1
  2.3 14.4 %all_to_all.97 = s32[32,1,128]{2,1,0:T(1,128)} all-to-all(s32[32,1,128]{2,1,0:T(1,128)} %bitcast.63), channel_id=1, replica_groups=mesh['dev'=32] {'dev'}, dimensions={0} | all-to-all | bytes 32768 | tf_op jit(solution)/shard_map/all_to_all | solution.py:542
  16.7 2.9 %pack_near.1 = f32[1536,128]{1,0:T(8,128)} custom-call(s32[32,128]{1,0:T(8,128)} %bitcast.54, f32[192,128]{1,0:T(8,128)} %bitcast.61, s32[192,128]{1,0:T(8,128)} %bitcast.62), custom_call_target="tpu_custom_call" | custom-call | bytes 12000000 | tf_op jit(solution)/shard_map/pack_near/pallas_call | solution.py:560
  19.6 2.6 %all-to-all-start.1 = ((f32[32,48,128]{2,1,0:T(8,128)}), f32[32,48,128]{2,1,0:T(8,128)S(1)}, u32[]{:S(2)}, u32[]{:S(2)}) async-start(f32[32,48,128]{2,1,0:T(8,128)} %bitcast.60), calls=%async_computation.1 | async-start | bytes 1572864 | tf_op jit(solution)/shard_map/all_to_all | solution.py:542
  22.3 0.0 copy-start.5
  22.3 0.0 copy-done.3
  22.3 2.9 %pack.1 = f32[1536,128]{1,0:T(8,128)} custom-call(s32[32,128]{1,0:T(8,128)S(1)} %bitcast.55, f32[192,128]{1,0:T(8,128)S(1)} %bitcast.50), custom_call_target="tpu_custom_call" | custom-call | bytes 9000000 | tf_op jit(solution)/shard_map/pack/pallas_call | solution.py:571
  25.2 17.7 %all-to-all-done.1 = f32[32,48,128]{2,1,0:T(8,128)S(1)} async-done(((f32[32,48,128]{2,1,0:T(8,128)}), f32[32,48,128]{2,1,0:T(8,128)S(1)}, u32[]{:S(2)}, u32[]{:S(2)}) %all-to-all-start.1) | async-done | bytes 786464 | tf_op jit(solution)/shard_map/all_to_all | solution.py:542
  42.8 3.5 %all-to-all-start.2 = ((f32[32,48,128]{2,1,0:T(8,128)}), f32[32,48,128]{2,1,0:T(8,128)S(1)}, u32[]{:S(2)}, u32[]{:S(2)}) async-start(f32[32,48,128]{2,1,0:T(8,128)} %bitcast.15), calls=%async_computation.2 | async-start | bytes 1572864 | tf_op jit(solution)/shard_map/all_to_all | solution.py:542
  46.4 46.0 %build.1 = (f32[64,6,128,128]{3,2,1,0:T(8,128)}, f32[32,8,128]{2,1,0:T(8,128)S(1)}) custom-call(s32[8,128]{1,0:T(8,128)S(1)} %copy-done.5, f32[32,6,8,128]{3,2,1,0:T(8,128)S(1)} %bitcast.43), custom_call_target="tpu_custom_call" | custom-call | bytes 150000000 | tf_op jit(solution)/shard_map/build/pallas_call | solution.py:594
  92.4 0.0 all-to-all-done.2
  92.4 15.6 %apply.2 = f32[768,128]{1,0:T(8,128)} custom-call(s32[8,128]{1,0:T(8,128)S(1)} %copy-done.5, f32[32,8,128]{2,1,0:T(8,128)S(1)} %get-tuple-element.14.refs_1_, f32[32,3,16,128]{3,2,1,0:T(8,128)S(1)} %bitcast.39, f32[64,6,128,128]{3,2,1,0:T(8,128)} %get-tuple-element.15.refs_3_), custom_call_target="tpu_custom_call" | custom-call | bytes 54000000 | tf_op jit(solution)/shard_map/apply/pallas_call | solution.py:625
  108.0 5.8 %all-to-all-start.3 = ((f32[32,24,128]{2,1,0:T(8,128)}), f32[32,24,128]{2,1,0:T(8,128)S(1)}, u32[]{:S(2)}, u32[]{:S(2)}) async-start(f32[32,24,128]{2,1,0:T(8,128)} %bitcast.17), calls=%async_computation.3 | async-start | bytes 786432 | tf_op jit(solution)/shard_map/all_to_all | solution.py:542
  113.8 0.0 copy-done
  113.8 0.0 copy-start.1
  113.9 1.4 copy-done.1
  115.3 2.6 %far.2 = f32[768,128]{1,0:T(8,128)S(1)} custom-call(s32[8,128]{1,0:T(8,128)S(1)} %copy-done.5, f32[1536,128]{1,0:T(8,128)S(1)} %bitcast.40, f32[64,16,384]{2,1,0:T(8,128)S(1)} %copy-done, f32[64,16,384]{2,1,0:T(8,128)S(1)} %copy-done.1), custom_call_target="tpu_custom_call" | custom-call | bytes 15000000 | tf_op jit(solution)/shard_map/far/pallas_call | solution.py:607
  117.9 9.2 %all-to-all-done.3 = f32[32,24,128]{2,1,0:T(8,128)S(1)} async-done(((f32[32,24,128]{2,1,0:T(8,128)}), f32[32,24,128]{2,1,0:T(8,128)S(1)}, u32[]{:S(2)}, u32[]{:S(2)}) %all-to-all-start.3) | async-done | bytes 393248 | tf_op jit(solution)/shard_map/all_to_all | solution.py:542
  127.1 15.6 %all_to_all.98 = f32[32,24,128]{2,1,0:T(8,128)S(1)} all-to-all(f32[32,24,128]{2,1,0:T(8,128)S(1)} %bitcast.46), channel_id=1, replica_groups=mesh['dev'=32] {'dev'}, dimensions={0} | all-to-all | bytes 786432 | tf_op jit(solution)/shard_map/all_to_all | solution.py:542
  142.7 3.0 %merge.1 = (f32[3,64,128]{2,1,0:T(8,128)S(1)}, f32[1536,128]{1,0:T(8,128)S(1)}) custom-call(s32[32,128]{1,0:T(8,128)S(1)} %bitcast.56, f32[768,128]{1,0:T(8,128)S(1)} %bitcast.44, f32[768,128]{1,0:T(8,128)S(1)} %bitcast.47), custom_call_target="tpu_custom_call" | custom-call | bytes 15000000 | tf_op jit(solution)/shard_map/merge/pallas_call | solution.py:644
  145.6 22.9 %all_to_all.99 = f32[32,48,128]{2,1,0:T(8,128)S(1)} all-to-all(f32[32,48,128]{2,1,0:T(8,128)S(1)} %bitcast.53), channel_id=1, replica_groups=mesh['dev'=32] {'dev'}, dimensions={0} | all-to-all | bytes 1572864 | tf_op jit(solution)/shard_map/all_to_all | solution.py:542
  168.5 15.6 %apply.3 = f32[768,128]{1,0:T(8,128)} custom-call(s32[8,128]{1,0:T(8,128)S(1)} %copy-done.5, f32[32,8,128]{2,1,0:T(8,128)S(1)} %get-tuple-element.14.refs_1_, f32[32,3,16,128]{3,2,1,0:T(8,128)S(1)} %bitcast.41, f32[64,6,128,128]{3,2,1,0:T(8,128)} %get-tuple-element.15.refs_3_), custom_call_target="tpu_custom_call" | custom-call | bytes 54000000 | tf_op jit(solution)/shard_map/apply/pallas_call | solution.py:625
  184.1 3.6 %all-to-all-start.6 = ((f32[32,24,128]{2,1,0:T(8,128)}), f32[32,24,128]{2,1,0:T(8,128)S(1)}, u32[]{:S(2)}, u32[]{:S(2)}) async-start(f32[32,24,128]{2,1,0:T(8,128)} %bitcast.24), calls=%async_computation.6 | async-start | bytes 786432 | tf_op jit(solution)/shard_map/all_to_all | solution.py:542
  187.8 0.0 copy-start.2
  187.8 1.4 copy-done.2
  189.2 2.6 %far.3 = f32[768,128]{1,0:T(8,128)S(1)} custom-call(s32[8,128]{1,0:T(8,128)S(1)} %copy-done.5, f32[1536,128]{1,0:T(8,128)S(1)} %bitcast.42, f32[64,16,384]{2,1,0:T(8,128)S(1)} %copy-done, f32[64,16,384]{2,1,0:T(8,128)S(1)} %copy-done.2), custom_call_target="tpu_custom_call" | custom-call | bytes 15000000 | tf_op jit(solution)/shard_map/far/pallas_call | solution.py:607
  191.8 9.2 %all-to-all-done.6 = f32[32,24,128]{2,1,0:T(8,128)S(1)} async-done(((f32[32,24,128]{2,1,0:T(8,128)}), f32[32,24,128]{2,1,0:T(8,128)S(1)}, u32[]{:S(2)}, u32[]{:S(2)}) %all-to-all-start.6) | async-done | bytes 393248 | tf_op jit(solution)/shard_map/all_to_all | solution.py:542
  201.0 15.6 %all_to_all.100 = f32[32,24,128]{2,1,0:T(8,128)S(1)} all-to-all(f32[32,24,128]{2,1,0:T(8,128)S(1)} %bitcast.45), channel_id=1, replica_groups=mesh['dev'=32] {'dev'}, dimensions={0} | all-to-all | bytes 786432 | tf_op jit(solution)/shard_map/all_to_all | solution.py:542
  216.6 3.0 %gram.1 = (f32[3,64,128]{2,1,0:T(8,128)S(1)}, f32[32,128]{1,0:T(8,128)S(1)}) custom-call(s32[32,128]{1,0:T(8,128)S(1)} %bitcast.57, f32[768,128]{1,0:T(8,128)S(1)} %bitcast.48, f32[768,128]{1,0:T(8,128)S(1)} %bitcast.49, f32[3,64,128]{2,1,0:T(8,128)S(1)} %bitcast.51, f32[3,64,128]{2,1,0:T(8,128)S(1)} %get-tuple-element.17.refs_4_.refs_2_), custom_call_target="tpu_custom_call" | custom-call | bytes 15000000 | tf_op jit(solution)/shard_map/gram/pallas_call | solution.py:659
  219.6 9.5 %all_to_all.101 = f32[32,1,128]{2,1,0:T(1,128)S(1)} all-to-all(f32[32,1,128]{2,1,0:T(1,128)S(1)} %bitcast.59), channel_id=1, replica_groups=mesh['dev'=32] {'dev'}, dimensions={0} | all-to-all | bytes 32768 | tf_op jit(solution)/shard_map/all_to_all | solution.py:542
  229.1 2.5 %final.1 = (f32[2,3,64,128]{3,2,1,0:T(8,128)}, f32[2,3]{1,0:T(2,128)}) custom-call(f32[32,128]{1,0:T(8,128)S(1)} %bitcast.58, f32[3,64,128]{2,1,0:T(8,128)S(1)} %bitcast.52, f32[3,64,128]{2,1,0:T(8,128)S(1)} %get-tuple-element.17.refs_4_.refs_2_, f32[3,64,128]{2,1,0:T(8,128)S(1)} %get-tuple-element.19.refs_3_), custom_call_target="tpu_custom_call" | custom-call | tf_op jit(solution)/shard_map/final/pallas_call | solution.py:669
  (4 shorter events, 0.0 us)
Async XLA Ops:
  0.6 21.7 %copy-start.3 = (f32[64,3,128]{2,0,1:T(8,128)S(1)}, f32[64,3,128]{2,0,1:T(8,128)}, u32[]{:S(2)}) copy-start(f32[64,3,128]{2,0,1:T(8,128)} %param.9) | copy-start | bytes 294916
  16.7 5.6 %copy-start.4 = (s32[32,1,128]{2,1,0:T(1,128)S(1)}, s32[32,1,128]{2,1,0:T(1,128)}, u32[]{:S(2)}) copy-start(s32[32,1,128]{2,1,0:T(1,128)} %all_to_all.97) | copy-start | bytes 49156
  19.6 23.2 %all-to-all-start.1 = ((f32[32,48,128]{2,1,0:T(8,128)}), f32[32,48,128]{2,1,0:T(8,128)S(1)}, u32[]{:S(2)}, u32[]{:S(2)}) async-start(f32[32,48,128]{2,1,0:T(8,128)} %bitcast.60), calls=%async_computation.1 | async-start | bytes 1572864 | tf_op jit(solution)/shard_map/all_to_all | solution.py:542
  22.3 24.1 %copy-start.5 = (s32[8,128]{1,0:T(8,128)S(1)}, s32[8,128]{1,0:T(8,128)}, u32[]{:S(2)}) copy-start(s32[8,128]{1,0:T(8,128)} %get-tuple-element.13.refs_0_) | copy-start | bytes 12292
  42.8 49.5 %all-to-all-start.2 = ((f32[32,48,128]{2,1,0:T(8,128)}), f32[32,48,128]{2,1,0:T(8,128)S(1)}, u32[]{:S(2)}, u32[]{:S(2)}) async-start(f32[32,48,128]{2,1,0:T(8,128)} %bitcast.15), calls=%async_computation.2 | async-start | bytes 1572864 | tf_op jit(solution)/shard_map/all_to_all | solution.py:542
  92.4 21.5 %copy-start = (f32[64,16,384]{2,1,0:T(8,128)S(1)}, f32[64,16,384]{2,1,0:T(8,128)}, u32[]{:S(2)}) copy-start(f32[64,16,384]{2,1,0:T(8,128)} %refs_2_.3) | copy-start | bytes 4718596
  108.0 19.1 %all-to-all-start.3 = ((f32[32,24,128]{2,1,0:T(8,128)}), f32[32,24,128]{2,1,0:T(8,128)S(1)}, u32[]{:S(2)}, u32[]{:S(2)}) async-start(f32[32,24,128]{2,1,0:T(8,128)} %bitcast.17), calls=%async_computation.3 | async-start | bytes 786432 | tf_op jit(solution)/shard_map/all_to_all | solution.py:542
  113.8 1.4 copy-start.1
  184.1 16.9 %all-to-all-start.6 = ((f32[32,24,128]{2,1,0:T(8,128)}), f32[32,24,128]{2,1,0:T(8,128)S(1)}, u32[]{:S(2)}, u32[]{:S(2)}) async-start(f32[32,24,128]{2,1,0:T(8,128)} %bitcast.24), calls=%async_computation.6 | async-start | bytes 786432 | tf_op jit(solution)/shard_map/all_to_all | solution.py:542
  187.8 1.4 copy-start.2

commit v5 on v4

--- a/solution.py
+++ b/solution.py
@@ -12,7 +12,7 @@
 norm_eps = 1e-06
 big = 2.0 / 3.0
 small = 1.0 / 6.0
-BUILD_UNROLL = 4
+BUILD_UNROLL = 16
 APPLY_UNROLL = 16
 f32 = jnp.float32
 VM = pl.BlockSpec(memory_space=pltpu.VMEM)
@@ -87,35 +87,33 @@
     idx_ref[...] = jnp.concatenate(rows + rows, axis=0).astype(jnp.int32)
 
 
-def pack_rows(ask_ref, fetch, out_ref, *, n, slots, kinds):
+def pack_rows(ask_ref, fetch, out_ref, *, n, slots, rows):
     def body(d, _):
         for s in range(slots):
-            rows = fetch(ask_ref[d, s])
-            for k in range(kinds):
-                at = (d * kinds + k) * 3 * slots + s
-                out_ref[pl.ds(at, 3, stride=slots), :] = rows[k]
+            out_ref[pl.ds(d * rows * slots + s, rows, stride=slots), :] = fetch(ask_ref[d, s])
         return 0
 
     lax.fori_loop(0, n, body, 0, unroll=2)
 
 
-def cluster_rows(refs):
-    clusters = refs[0].shape[0] // 3
+def cluster_rows(ref, rows):
+    clusters = ref.shape[0] // rows
 
     def fetch(c):
-        c = jnp.minimum(c, clusters - 1)
-        return [ref[pl.ds(c, 3, stride=clusters), :] for ref in refs]
+        return ref[pl.ds(jnp.minimum(c, clusters - 1), rows, stride=clusters), :]
 
     return fetch
 
 
 def pack_kernel(ask_ref, x_ref, out_ref, *, n, slots):
-    pack_rows(ask_ref, cluster_rows((x_ref,)), out_ref, n=n, slots=slots, kinds=1)
-
-
-def pack_near_kernel(ask_ref, v_ref, p_ref, out_ref, pan_ref, *, n, slots):
-    pan_ref[...] = p_ref[...].astype(f32)
-    pack_rows(ask_ref, cluster_rows((v_ref, pan_ref)), out_ref, n=n, slots=slots, kinds=2)
+    pack_rows(ask_ref, cluster_rows(x_ref, 3), out_ref, n=n, slots=slots, rows=3)
+
+
+def pack_near_kernel(ask_ref, v_ref, p_ref, out_ref, all_ref, *, n, slots):
+    half = v_ref.shape[0]
+    all_ref[pl.ds(0, half), :] = v_ref[...]
+    all_ref[pl.ds(half, half), :] = p_ref[...].astype(f32)
+    pack_rows(ask_ref, cluster_rows(all_ref, 6), out_ref, n=n, slots=slots, rows=6)
 
 
 def far_kernel(idx_ref, x_ref, l_ref, r_ref, out_ref, sum_ref, row_ref, *, cap):
@@ -205,9 +203,17 @@
         at += comps
 
 
+def tile_rows(t):
+    return pl.ds(8 * t if isinstance(t, int) else pl.multiple_of(8 * t, 8), 8)
+
+
+def lane_roll(x, shift):
+    return x if isinstance(shift, int) and shift == 0 else pltpu.roll(x, shift, 1)
+
+
 def skew_tile(base_ref, dst_ref, t):
     for c in range(base_ref.shape[0]):
-        dst_ref[c, pl.ds(pl.multiple_of(8 * t, 8), 8), :] = pltpu.roll(base_ref[c], 8 * t, 1)
+        dst_ref[c, tile_rows(t), :] = lane_roll(base_ref[c], 8 * t)
 
 
 def weighted(w_ref, x_ref, y_ref, *, cap):
@@ -303,10 +309,11 @@
             def tile_body(t, carry, g=g, src=src, dst=dst, base=base, row=row):
                 if sums is not None:
                     held, first, second = carry
-                    back = (128 - 8 * (t - 1)) % 128
-                    first = [first[i] + pltpu.roll(held[i], back, 1) for i in range(3)]
+                    if not isinstance(t, int) or t > 0:
+                        back = (128 - 8 * (t - 1)) % 128
+                        first = [first[i] + lane_roll(held[i], back) for i in range(3)]
                 skew_tile(base, dst, t)
-                tile = pl.ds(pl.multiple_of(8 * t, 8), 8)
+                tile = tile_rows(t)
                 col = [src[c, tile, :] for c in range(comps)]
                 mats = tile_mats(g, tile, col, row)
                 if sums is None:
@@ -316,7 +323,12 @@
 
             zero = [jnp.zeros((8, 128), f32)] * 3
             start = 0 if sums is None else (zero, zero, zero)
-            carry = lax.fori_loop(0, 16, tile_body, start, unroll=unroll)
+            if unroll == 16:
+                carry = start
+                for t in range(16):
+                    carry = tile_body(t, carry)
+            else:
+                carry = lax.fori_loop(0, 16, tile_body, start, unroll=unroll)
             if sums is not None:
                 held, first, second = carry
                 for i in range(3):
@@ -356,7 +368,7 @@
     sweep_pairs(
         idx_ref, parts, (base0, base1), (buf0, buf1), tile_mats, None,
         step=step, pairs=count, group=k_ref.shape[0], cap=cap, count=count,
-        unroll=BUILD_UNROLL, block=2,
+        unroll=BUILD_UNROLL, block=4,
     )
 
 
@@ -431,9 +443,9 @@
     last = out_ref.shape[1] - 1
 
     def fetch(c):
-        return [accs[0][pl.ds(pl.multiple_of(8 * jnp.minimum(c, last), 8), 3), :]]
-
-    pack_rows(ask_ref, fetch, pack_ref, n=n, slots=2 * cap, kinds=1)
+        return accs[0][pl.ds(pl.multiple_of(8 * jnp.minimum(c, last), 8), 3), :]
+
+    pack_rows(ask_ref, fetch, pack_ref, n=n, slots=2 * cap, rows=3)
 
 
 PRODUCTS = ((0, 0), (0, 1), (1, 1), (0, 2), (1, 2), (2, 2))
@@ -561,7 +573,7 @@
             lambda *refs: pack_near_kernel(*refs, n=n, slots=cap),
             out_shape=shape((n * 6 * cap, width), f32),
             in_specs=[SM, VM, VM],
-            scratch_shapes=[pltpu.VMEM((3 * clusters, width), f32)],
+            scratch_shapes=[pltpu.VMEM((6 * clusters, width), f32)],
             compiler_params=params(60),
             cost_estimate=cost(4.0),
             name="pack_near",

time: 232 us -> 227 us (0.978)
  Pallas kernels: 98.3 us -> 93.1 us
    pallas_call x1, Pallas kernels: 46 us -> 40.6 us  [per_device(): pl.pallas_call(lambda *refs: build_kernel(*refs, cap=cap, count=near_coun...]
  transfers between devices with their start and end apart: 4 -> 4, of which waited for: 3 -> 3; matrix products, arithmetic and copies ran while one was open for 0% -> 0% of each run, Pallas kernels for 23% -> 22%
where the time goes in v5:
time: 227 us; the launch traced here: 226 us
  Pallas kernels  93.1 us (41%)
  blocking collectives  77.9 us (34%)
  waiting for transfers between devices  36.1 us (16%)
  starting transfers between devices  15.6 us (7%)
  local copies, waits for them, and re-layouts  2.82 us (1%)
    all_to_all x5, blocking collectives, exchange(): return lax.all_to_all(block, 'dev', split_axis=0, concat_axis=0, tiled=True)  77.9 us
    pallas_call x1, Pallas kernels, per_device(): pl.pallas_call(lambda *refs: build_kernel(*refs, cap=cap, count=near_coun...  40.6 us
    all_to_all x4, waiting for transfers between devices, exchange(): return lax.all_to_all(block, 'dev', split_axis=0, concat_axis=0, tiled=True)  36.1 us
    pallas_call x2, Pallas kernels, apply_stored(): pl.pallas_call(lambda *refs: apply_kernel(*refs, cap=cap, count=near_coun...  31.2 us
    all_to_all x4, starting transfers between devices, exchange(): return lax.all_to_all(block, 'dev', split_axis=0, concat_axis=0, tiled=True)  15.6 us
    pallas_call x2, Pallas kernels, far_product(): pl.pallas_call(lambda *refs: far_kernel(*refs, cap=cap), out_shape=rows3,...  5.24 us
  transfers between devices with their start and end apart: 4, of which 3 were waited for; matrix products, arithmetic and copies ran while one was open for 0% of the time, Pallas kernels for 22%

profile of v5, /device:TPU:0, one launch (start us, length us, event | category | flops | bytes accessed | tf_op | source)
XLA Modules:
  0.0 226.3 jit_solution(14775992346825548310)
XLA Ops:
  0.6 0.0 copy-start.3
  0.6 1.7 prep.1
  2.3 14.4 %all_to_all.97 = s32[32,1,128]{2,1,0:T(1,128)} all-to-all(s32[32,1,128]{2,1,0:T(1,128)} %bitcast.63), channel_id=1, replica_groups=mesh['dev'=32] {'dev'}, dimensions={0} | all-to-all | bytes 32768 | tf_op jit(solution)/shard_map/all_to_all | solution.py:554
  16.7 3.0 %pack_near.1 = f32[1536,128]{1,0:T(8,128)} custom-call(s32[32,128]{1,0:T(8,128)} %bitcast.54, f32[192,128]{1,0:T(8,128)} %bitcast.61, s32[192,128]{1,0:T(8,128)} %bitcast.62), custom_call_target="tpu_custom_call" | custom-call | bytes 12000000 | tf_op jit(solution)/shard_map/pack_near/pallas_call | solution.py:572
  19.7 2.6 %all-to-all-start.1 = ((f32[32,48,128]{2,1,0:T(8,128)}), f32[32,48,128]{2,1,0:T(8,128)S(1)}, u32[]{:S(2)}, u32[]{:S(2)}) async-start(f32[32,48,128]{2,1,0:T(8,128)} %bitcast.60), calls=%async_computation.1 | async-start | bytes 1572864 | tf_op jit(solution)/shard_map/all_to_all | solution.py:554
  22.4 0.0 copy-start.5
  22.4 0.0 copy-done.3
  22.4 2.9 %pack.1 = f32[1536,128]{1,0:T(8,128)} custom-call(s32[32,128]{1,0:T(8,128)S(1)} %bitcast.55, f32[192,128]{1,0:T(8,128)S(1)} %bitcast.50), custom_call_target="tpu_custom_call" | custom-call | bytes 9000000 | tf_op jit(solution)/shard_map/pack/pallas_call | solution.py:583
  25.3 17.7 %all-to-all-done.1 = f32[32,48,128]{2,1,0:T(8,128)S(1)} async-done(((f32[32,48,128]{2,1,0:T(8,128)}), f32[32,48,128]{2,1,0:T(8,128)S(1)}, u32[]{:S(2)}, u32[]{:S(2)}) %all-to-all-start.1) | async-done | bytes 786464 | tf_op jit(solution)/shard_map/all_to_all | solution.py:554
  42.9 3.5 %all-to-all-start.2 = ((f32[32,48,128]{2,1,0:T(8,128)}), f32[32,48,128]{2,1,0:T(8,128)S(1)}, u32[]{:S(2)}, u32[]{:S(2)}) async-start(f32[32,48,128]{2,1,0:T(8,128)} %bitcast.15), calls=%async_computation.2 | async-start | bytes 1572864 | tf_op jit(solution)/shard_map/all_to_all | solution.py:554
  46.5 0.0 copy-done.5
  46.5 40.6 %build.1 = (f32[64,6,128,128]{3,2,1,0:T(8,128)}, f32[32,8,128]{2,1,0:T(8,128)S(1)}) custom-call(s32[8,128]{1,0:T(8,128)S(1)} %copy-done.5, f32[32,6,8,128]{3,2,1,0:T(8,128)S(1)} %bitcast.43), custom_call_target="tpu_custom_call" | custom-call | bytes 150000000 | tf_op jit(solution)/shard_map/build/pallas_call | solution.py:606
  87.2 0.0 all-to-all-done.2
  87.2 15.6 %apply.2 = f32[768,128]{1,0:T(8,128)} custom-call(s32[8,128]{1,0:T(8,128)S(1)} %copy-done.5, f32[32,8,128]{2,1,0:T(8,128)S(1)} %get-tuple-element.14.refs_1_, f32[32,3,16,128]{3,2,1,0:T(8,128)S(1)} %bitcast.39, f32[64,6,128,128]{3,2,1,0:T(8,128)} %get-tuple-element.15.refs_3_), custom_call_target="tpu_custom_call" | custom-call | bytes 54000000 | tf_op jit(solution)/shard_map/apply/pallas_call | solution.py:637
  102.8 5.8 %all-to-all-start.3 = ((f32[32,24,128]{2,1,0:T(8,128)}), f32[32,24,128]{2,1,0:T(8,128)S(1)}, u32[]{:S(2)}, u32[]{:S(2)}) async-start(f32[32,24,128]{2,1,0:T(8,128)} %bitcast.17), calls=%async_computation.3 | async-start | bytes 786432 | tf_op jit(solution)/shard_map/all_to_all | solution.py:554
  108.6 0.0 copy-start.1
  108.6 1.4 copy-done.1
  110.0 2.6 %far.2 = f32[768,128]{1,0:T(8,128)S(1)} custom-call(s32[8,128]{1,0:T(8,128)S(1)} %copy-done.5, f32[1536,128]{1,0:T(8,128)S(1)} %bitcast.40, f32[64,16,384]{2,1,0:T(8,128)S(1)} %copy-done, f32[64,16,384]{2,1,0:T(8,128)S(1)} %copy-done.1), custom_call_target="tpu_custom_call" | custom-call | bytes 15000000 | tf_op jit(solution)/shard_map/far/pallas_call | solution.py:619
  112.7 9.2 %all-to-all-done.3 = f32[32,24,128]{2,1,0:T(8,128)S(1)} async-done(((f32[32,24,128]{2,1,0:T(8,128)}), f32[32,24,128]{2,1,0:T(8,128)S(1)}, u32[]{:S(2)}, u32[]{:S(2)}) %all-to-all-start.3) | async-done | bytes 393248 | tf_op jit(solution)/shard_map/all_to_all | solution.py:554
  121.8 15.6 %all_to_all.98 = f32[32,24,128]{2,1,0:T(8,128)S(1)} all-to-all(f32[32,24,128]{2,1,0:T(8,128)S(1)} %bitcast.46), channel_id=1, replica_groups=mesh['dev'=32] {'dev'}, dimensions={0} | all-to-all | bytes 786432 | tf_op jit(solution)/shard_map/all_to_all | solution.py:554
  137.4 3.0 %merge.1 = (f32[3,64,128]{2,1,0:T(8,128)S(1)}, f32[1536,128]{1,0:T(8,128)S(1)}) custom-call(s32[32,128]{1,0:T(8,128)S(1)} %bitcast.56, f32[768,128]{1,0:T(8,128)S(1)} %bitcast.44, f32[768,128]{1,0:T(8,128)S(1)} %bitcast.47), custom_call_target="tpu_custom_call" | custom-call | bytes 15000000 | tf_op jit(solution)/shard_map/merge/pallas_call | solution.py:656
  140.4 22.9 %all_to_all.99 = f32[32,48,128]{2,1,0:T(8,128)S(1)} all-to-all(f32[32,48,128]{2,1,0:T(8,128)S(1)} %bitcast.53), channel_id=1, replica_groups=mesh['dev'=32] {'dev'}, dimensions={0} | all-to-all | bytes 1572864 | tf_op jit(solution)/shard_map/all_to_all | solution.py:554
  163.3 15.6 %apply.3 = f32[768,128]{1,0:T(8,128)} custom-call(s32[8,128]{1,0:T(8,128)S(1)} %copy-done.5, f32[32,8,128]{2,1,0:T(8,128)S(1)} %get-tuple-element.14.refs_1_, f32[32,3,16,128]{3,2,1,0:T(8,128)S(1)} %bitcast.41, f32[64,6,128,128]{3,2,1,0:T(8,128)} %get-tuple-element.15.refs_3_), custom_call_target="tpu_custom_call" | custom-call | bytes 54000000 | tf_op jit(solution)/shard_map/apply/pallas_call | solution.py:637
  178.9 3.6 %all-to-all-start.6 = ((f32[32,24,128]{2,1,0:T(8,128)}), f32[32,24,128]{2,1,0:T(8,128)S(1)}, u32[]{:S(2)}, u32[]{:S(2)}) async-start(f32[32,24,128]{2,1,0:T(8,128)} %bitcast.24), calls=%async_computation.6 | async-start | bytes 786432 | tf_op jit(solution)/shard_map/all_to_all | solution.py:554
  182.5 0.0 copy-start.2
  182.5 1.4 copy-done.2
  183.9 2.6 %far.3 = f32[768,128]{1,0:T(8,128)S(1)} custom-call(s32[8,128]{1,0:T(8,128)S(1)} %copy-done.5, f32[1536,128]{1,0:T(8,128)S(1)} %bitcast.42, f32[64,16,384]{2,1,0:T(8,128)S(1)} %copy-done, f32[64,16,384]{2,1,0:T(8,128)S(1)} %copy-done.2), custom_call_target="tpu_custom_call" | custom-call | bytes 15000000 | tf_op jit(solution)/shard_map/far/pallas_call | solution.py:619
  186.5 9.2 %all-to-all-done.6 = f32[32,24,128]{2,1,0:T(8,128)S(1)} async-done(((f32[32,24,128]{2,1,0:T(8,128)}), f32[32,24,128]{2,1,0:T(8,128)S(1)}, u32[]{:S(2)}, u32[]{:S(2)}) %all-to-all-start.6) | async-done | bytes 393248 | tf_op jit(solution)/shard_map/all_to_all | solution.py:554
  195.7 15.6 %all_to_all.100 = f32[32,24,128]{2,1,0:T(8,128)S(1)} all-to-all(f32[32,24,128]{2,1,0:T(8,128)S(1)} %bitcast.45), channel_id=1, replica_groups=mesh['dev'=32] {'dev'}, dimensions={0} | all-to-all | bytes 786432 | tf_op jit(solution)/shard_map/all_to_all | solution.py:554
  211.3 3.0 %gram.1 = (f32[3,64,128]{2,1,0:T(8,128)S(1)}, f32[32,128]{1,0:T(8,128)S(1)}) custom-call(s32[32,128]{1,0:T(8,128)S(1)} %bitcast.57, f32[768,128]{1,0:T(8,128)S(1)} %bitcast.48, f32[768,128]{1,0:T(8,128)S(1)} %bitcast.49, f32[3,64,128]{2,1,0:T(8,128)S(1)} %bitcast.51, f32[3,64,128]{2,1,0:T(8,128)S(1)} %get-tuple-element.17.refs_4_.refs_2_), custom_call_target="tpu_custom_call" | custom-call | bytes 15000000 | tf_op jit(solution)/shard_map/gram/pallas_call | solution.py:671
  214.3 9.5 %all_to_all.101 = f32[32,1,128]{2,1,0:T(1,128)S(1)} all-to-all(f32[32,1,128]{2,1,0:T(1,128)S(1)} %bitcast.59), channel_id=1, replica_groups=mesh['dev'=32] {'dev'}, dimensions={0} | all-to-all | bytes 32768 | tf_op jit(solution)/shard_map/all_to_all | solution.py:554
  223.8 2.5 %final.1 = (f32[2,3,64,128]{3,2,1,0:T(8,128)}, f32[2,3]{1,0:T(2,128)}) custom-call(f32[32,128]{1,0:T(8,128)S(1)} %bitcast.58, f32[3,64,128]{2,1,0:T(8,128)S(1)} %bitcast.52, f32[3,64,128]{2,1,0:T(8,128)S(1)} %get-tuple-element.17.refs_4_.refs_2_, f32[3,64,128]{2,1,0:T(8,128)S(1)} %get-tuple-element.19.refs_3_), custom_call_target="tpu_custom_call" | custom-call | tf_op jit(solution)/shard_map/final/pallas_call | solution.py:681
  (4 shorter events, 0.0 us)
Async XLA Ops:
  0.6 21.8 %copy-start.3 = (f32[64,3,128]{2,0,1:T(8,128)S(1)}, f32[64,3,128]{2,0,1:T(8,128)}, u32[]{:S(2)}) copy-start(f32[64,3,128]{2,0,1:T(8,128)} %param.9) | copy-start | bytes 294916
  16.7 5.7 %copy-start.4 = (s32[32,1,128]{2,1,0:T(1,128)S(1)}, s32[32,1,128]{2,1,0:T(1,128)}, u32[]{:S(2)}) copy-start(s32[32,1,128]{2,1,0:T(1,128)} %all_to_all.97) | copy-start | bytes 49156
  19.7 23.2 %all-to-all-start.1 = ((f32[32,48,128]{2,1,0:T(8,128)}), f32[32,48,128]{2,1,0:T(8,128)S(1)}, u32[]{:S(2)}, u32[]{:S(2)}) async-start(f32[32,48,128]{2,1,0:T(8,128)} %bitcast.60), calls=%async_computation.1 | async-start | bytes 1572864 | tf_op jit(solution)/shard_map/all_to_all | solution.py:554
  22.4 24.1 %copy-start.5 = (s32[8,128]{1,0:T(8,128)S(1)}, s32[8,128]{1,0:T(8,128)}, u32[]{:S(2)}) copy-start(s32[8,128]{1,0:T(8,128)} %get-tuple-element.13.refs_0_) | copy-start | bytes 12292
  42.9 44.2 %all-to-all-start.2 = ((f32[32,48,128]{2,1,0:T(8,128)}), f32[32,48,128]{2,1,0:T(8,128)S(1)}, u32[]{:S(2)}, u32[]{:S(2)}) async-start(f32[32,48,128]{2,1,0:T(8,128)} %bitcast.15), calls=%async_computation.2 | async-start | bytes 1572864 | tf_op jit(solution)/shard_map/all_to_all | solution.py:554
  87.2 21.5 %copy-start = (f32[64,16,384]{2,1,0:T(8,128)S(1)}, f32[64,16,384]{2,1,0:T(8,128)}, u32[]{:S(2)}) copy-start(f32[64,16,384]{2,1,0:T(8,128)} %refs_2_.3) | copy-start | bytes 4718596
  102.8 19.1 %all-to-all-start.3 = ((f32[32,24,128]{2,1,0:T(8,128)}), f32[32,24,128]{2,1,0:T(8,128)S(1)}, u32[]{:S(2)}, u32[]{:S(2)}) async-start(f32[32,24,128]{2,1,0:T(8,128)} %bitcast.17), calls=%async_computation.3 | async-start | bytes 786432 | tf_op jit(solution)/shard_map/all_to_all | solution.py:554
  108.6 1.4 copy-start.1
  178.9 16.9 %all-to-all-start.6 = ((f32[32,24,128]{2,1,0:T(8,128)}), f32[32,24,128]{2,1,0:T(8,128)S(1)}, u32[]{:S(2)}, u32[]{:S(2)}) async-start(f32[32,24,128]{2,1,0:T(8,128)} %bitcast.24), calls=%async_computation.6 | async-start | bytes 786432 | tf_op jit(solution)/shard_map/all_to_all | solution.py:554
  182.5 1.4 copy-start.2

commit v6 on v5

--- a/solution.py
+++ b/solution.py
@@ -368,7 +368,7 @@
     sweep_pairs(
         idx_ref, parts, (base0, base1), (buf0, buf1), tile_mats, None,
         step=step, pairs=count, group=k_ref.shape[0], cap=cap, count=count,
-        unroll=BUILD_UNROLL, block=4,
+        unroll=BUILD_UNROLL, block=8,
     )
 
 
@@ -424,7 +424,7 @@
                 acc[at, :] += ref[pl.ds(d * 3 * cap + s, 3, stride=cap), :]
         return 0
 
-    lax.fori_loop(0, n, body, 0)
+    lax.fori_loop(0, n, body, 0, unroll=4)
 
     def total(q, _):
         at = pl.ds(pl.multiple_of(64 * q, 64), 64)
@@ -435,7 +435,7 @@
             ]
         return 0
 
-    lax.fori_loop(0, clusters // 8, total, 0)
+    lax.fori_loop(0, clusters // 8, total, 0, unroll=2)
 
 
 def merge_kernel(ask_ref, rn_ref, rf_ref, out_ref, pack_ref, *accs, n, cap):
@@ -472,7 +472,7 @@
                 new.append((s, lo + (err + e)))
             return new
 
-        totals = lax.fori_loop(0, clusters // 8, body, totals)
+        totals = lax.fori_loop(0, clusters // 8, body, totals, unroll=2)
     hi = jnp.concatenate([t[0] for t in totals], axis=0)
     lo = jnp.concatenate([t[1] for t in totals], axis=0)
     for shift in (64, 32, 16, 8, 4, 2, 1):

time: 227 us -> 226 us (level)
  transfers between devices with their start and end apart: 4 -> 4, of which waited for: 3 -> 3; matrix products, arithmetic and copies ran while one was open for 0% -> 0% of each run, Pallas kernels for 22% -> 21%
where the time goes in v6:
time: 226 us; the launch traced here: 225 us
  Pallas kernels  91.8 us (41%)
  blocking collectives  77.8 us (34%)
  waiting for transfers between devices  36.1 us (16%)
  starting transfers between devices  15.6 us (7%)
  local copies, waits for them, and re-layouts  2.82 us (1%)
    all_to_all x5, blocking collectives, exchange(): return lax.all_to_all(block, 'dev', split_axis=0, concat_axis=0, tiled=True)  77.8 us
    pallas_call x1, Pallas kernels, per_device(): pl.pallas_call(lambda *refs: build_kernel(*refs, cap=cap, count=near_coun...  39.7 us
    all_to_all x4, waiting for transfers between devices, exchange(): return lax.all_to_all(block, 'dev', split_axis=0, concat_axis=0, tiled=True)  36.1 us
    pallas_call x2, Pallas kernels, apply_stored(): pl.pallas_call(lambda *refs: apply_kernel(*refs, cap=cap, count=near_coun...  31.2 us
    all_to_all x4, starting transfers between devices, exchange(): return lax.all_to_all(block, 'dev', split_axis=0, concat_axis=0, tiled=True)  15.6 us
    pallas_call x2, Pallas kernels, far_product(): pl.pallas_call(lambda *refs: far_kernel(*refs, cap=cap), out_shape=rows3,...  5.24 us
  transfers between devices with their start and end apart: 4, of which 3 were waited for; matrix products, arithmetic and copies ran while one was open for 0% of the time, Pallas kernels for 21%

profile of v6, /device:TPU:0, one launch (start us, length us, event | category | flops | bytes accessed | tf_op | source)
XLA Modules:
  0.0 224.9 jit_solution(3769179937745552877)
XLA Ops:
  0.6 0.0 copy-start.3
  0.6 1.7 prep.1
  2.3 14.4 %all_to_all.97 = s32[32,1,128]{2,1,0:T(1,128)} all-to-all(s32[32,1,128]{2,1,0:T(1,128)} %bitcast.63), channel_id=1, replica_groups=mesh['dev'=32] {'dev'}, dimensions={0} | all-to-all | bytes 32768 | tf_op jit(solution)/shard_map/all_to_all | solution.py:554
  16.7 3.0 %pack_near.1 = f32[1536,128]{1,0:T(8,128)} custom-call(s32[32,128]{1,0:T(8,128)} %bitcast.54, f32[192,128]{1,0:T(8,128)} %bitcast.61, s32[192,128]{1,0:T(8,128)} %bitcast.62), custom_call_target="tpu_custom_call" | custom-call | bytes 12000000 | tf_op jit(solution)/shard_map/pack_near/pallas_call | solution.py:572
  19.7 2.6 %all-to-all-start.1 = ((f32[32,48,128]{2,1,0:T(8,128)}), f32[32,48,128]{2,1,0:T(8,128)S(1)}, u32[]{:S(2)}, u32[]{:S(2)}) async-start(f32[32,48,128]{2,1,0:T(8,128)} %bitcast.60), calls=%async_computation.1 | async-start | bytes 1572864 | tf_op jit(solution)/shard_map/all_to_all | solution.py:554
  22.4 0.0 copy-start.5
  22.4 0.0 copy-done.3
  22.4 2.9 %pack.1 = f32[1536,128]{1,0:T(8,128)} custom-call(s32[32,128]{1,0:T(8,128)S(1)} %bitcast.55, f32[192,128]{1,0:T(8,128)S(1)} %bitcast.50), custom_call_target="tpu_custom_call" | custom-call | bytes 9000000 | tf_op jit(solution)/shard_map/pack/pallas_call | solution.py:583
  25.3 17.7 %all-to-all-done.1 = f32[32,48,128]{2,1,0:T(8,128)S(1)} async-done(((f32[32,48,128]{2,1,0:T(8,128)}), f32[32,48,128]{2,1,0:T(8,128)S(1)}, u32[]{:S(2)}, u32[]{:S(2)}) %all-to-all-start.1) | async-done | bytes 786464 | tf_op jit(solution)/shard_map/all_to_all | solution.py:554
  42.9 3.5 %all-to-all-start.2 = ((f32[32,48,128]{2,1,0:T(8,128)}), f32[32,48,128]{2,1,0:T(8,128)S(1)}, u32[]{:S(2)}, u32[]{:S(2)}) async-start(f32[32,48,128]{2,1,0:T(8,128)} %bitcast.15), calls=%async_computation.2 | async-start | bytes 1572864 | tf_op jit(solution)/shard_map/all_to_all | solution.py:554
  46.5 0.0 copy-done.5
  46.5 39.7 %build.1 = (f32[64,6,128,128]{3,2,1,0:T(8,128)}, f32[32,8,128]{2,1,0:T(8,128)S(1)}) custom-call(s32[8,128]{1,0:T(8,128)S(1)} %copy-done.5, f32[32,6,8,128]{3,2,1,0:T(8,128)S(1)} %bitcast.43), custom_call_target="tpu_custom_call" | custom-call | bytes 150000000 | tf_op jit(solution)/shard_map/build/pallas_call | solution.py:606
  86.2 0.0 all-to-all-done.2
  86.2 15.6 %apply.2 = f32[768,128]{1,0:T(8,128)} custom-call(s32[8,128]{1,0:T(8,128)S(1)} %copy-done.5, f32[32,8,128]{2,1,0:T(8,128)S(1)} %get-tuple-element.14.refs_1_, f32[32,3,16,128]{3,2,1,0:T(8,128)S(1)} %bitcast.39, f32[64,6,128,128]{3,2,1,0:T(8,128)} %get-tuple-element.15.refs_3_), custom_call_target="tpu_custom_call" | custom-call | bytes 54000000 | tf_op jit(solution)/shard_map/apply/pallas_call | solution.py:637
  101.8 5.8 %all-to-all-start.3 = ((f32[32,24,128]{2,1,0:T(8,128)}), f32[32,24,128]{2,1,0:T(8,128)S(1)}, u32[]{:S(2)}, u32[]{:S(2)}) async-start(f32[32,24,128]{2,1,0:T(8,128)} %bitcast.17), calls=%async_computation.3 | async-start | bytes 786432 | tf_op jit(solution)/shard_map/all_to_all | solution.py:554
  107.6 0.0 copy-start.1
  107.6 1.4 copy-done.1
  109.0 2.6 %far.2 = f32[768,128]{1,0:T(8,128)S(1)} custom-call(s32[8,128]{1,0:T(8,128)S(1)} %copy-done.5, f32[1536,128]{1,0:T(8,128)S(1)} %bitcast.40, f32[64,16,384]{2,1,0:T(8,128)S(1)} %copy-done, f32[64,16,384]{2,1,0:T(8,128)S(1)} %copy-done.1), custom_call_target="tpu_custom_call" | custom-call | bytes 15000000 | tf_op jit(solution)/shard_map/far/pallas_call | solution.py:619
  111.7 9.2 %all-to-all-done.3 = f32[32,24,128]{2,1,0:T(8,128)S(1)} async-done(((f32[32,24,128]{2,1,0:T(8,128)}), f32[32,24,128]{2,1,0:T(8,128)S(1)}, u32[]{:S(2)}, u32[]{:S(2)}) %all-to-all-start.3) | async-done | bytes 393248 | tf_op jit(solution)/shard_map/all_to_all | solution.py:554
  120.9 15.6 %all_to_all.98 = f32[32,24,128]{2,1,0:T(8,128)S(1)} all-to-all(f32[32,24,128]{2,1,0:T(8,128)S(1)} %bitcast.46), channel_id=1, replica_groups=mesh['dev'=32] {'dev'}, dimensions={0} | all-to-all | bytes 786432 | tf_op jit(solution)/shard_map/all_to_all | solution.py:554
  136.4 2.9 %merge.1 = (f32[3,64,128]{2,1,0:T(8,128)S(1)}, f32[1536,128]{1,0:T(8,128)S(1)}) custom-call(s32[32,128]{1,0:T(8,128)S(1)} %bitcast.56, f32[768,128]{1,0:T(8,128)S(1)} %bitcast.44, f32[768,128]{1,0:T(8,128)S(1)} %bitcast.47), custom_call_target="tpu_custom_call" | custom-call | bytes 15000000 | tf_op jit(solution)/shard_map/merge/pallas_call | solution.py:656
  139.3 22.9 %all_to_all.99 = f32[32,48,128]{2,1,0:T(8,128)S(1)} all-to-all(f32[32,48,128]{2,1,0:T(8,128)S(1)} %bitcast.53), channel_id=1, replica_groups=mesh['dev'=32] {'dev'}, dimensions={0} | all-to-all | bytes 1572864 | tf_op jit(solution)/shard_map/all_to_all | solution.py:554
  162.2 15.6 %apply.3 = f32[768,128]{1,0:T(8,128)} custom-call(s32[8,128]{1,0:T(8,128)S(1)} %copy-done.5, f32[32,8,128]{2,1,0:T(8,128)S(1)} %get-tuple-element.14.refs_1_, f32[32,3,16,128]{3,2,1,0:T(8,128)S(1)} %bitcast.41, f32[64,6,128,128]{3,2,1,0:T(8,128)} %get-tuple-element.15.refs_3_), custom_call_target="tpu_custom_call" | custom-call | bytes 54000000 | tf_op jit(solution)/shard_map/apply/pallas_call | solution.py:637
  177.8 3.6 %all-to-all-start.6 = ((f32[32,24,128]{2,1,0:T(8,128)}), f32[32,24,128]{2,1,0:T(8,128)S(1)}, u32[]{:S(2)}, u32[]{:S(2)}) async-start(f32[32,24,128]{2,1,0:T(8,128)} %bitcast.24), calls=%async_computation.6 | async-start | bytes 786432 | tf_op jit(solution)/shard_map/all_to_all | solution.py:554
  181.4 0.0 copy-start.2
  181.4 1.4 copy-done.2
  182.8 2.6 %far.3 = f32[768,128]{1,0:T(8,128)S(1)} custom-call(s32[8,128]{1,0:T(8,128)S(1)} %copy-done.5, f32[1536,128]{1,0:T(8,128)S(1)} %bitcast.42, f32[64,16,384]{2,1,0:T(8,128)S(1)} %copy-done, f32[64,16,384]{2,1,0:T(8,128)S(1)} %copy-done.2), custom_call_target="tpu_custom_call" | custom-call | bytes 15000000 | tf_op jit(solution)/shard_map/far/pallas_call | solution.py:619
  185.4 9.2 %all-to-all-done.6 = f32[32,24,128]{2,1,0:T(8,128)S(1)} async-done(((f32[32,24,128]{2,1,0:T(8,128)}), f32[32,24,128]{2,1,0:T(8,128)S(1)}, u32[]{:S(2)}, u32[]{:S(2)}) %all-to-all-start.6) | async-done | bytes 393248 | tf_op jit(solution)/shard_map/all_to_all | solution.py:554
  194.6 15.6 %all_to_all.100 = f32[32,24,128]{2,1,0:T(8,128)S(1)} all-to-all(f32[32,24,128]{2,1,0:T(8,128)S(1)} %bitcast.45), channel_id=1, replica_groups=mesh['dev'=32] {'dev'}, dimensions={0} | all-to-all | bytes 786432 | tf_op jit(solution)/shard_map/all_to_all | solution.py:554
  210.2 2.8 %gram.1 = (f32[3,64,128]{2,1,0:T(8,128)S(1)}, f32[32,128]{1,0:T(8,128)S(1)}) custom-call(s32[32,128]{1,0:T(8,128)S(1)} %bitcast.57, f32[768,128]{1,0:T(8,128)S(1)} %bitcast.48, f32[768,128]{1,0:T(8,128)S(1)} %bitcast.49, f32[3,64,128]{2,1,0:T(8,128)S(1)} %bitcast.51, f32[3,64,128]{2,1,0:T(8,128)S(1)} %get-tuple-element.17.refs_4_.refs_2_), custom_call_target="tpu_custom_call" | custom-call | bytes 15000000 | tf_op jit(solution)/shard_map/gram/pallas_call | solution.py:671
  213.0 9.4 %all_to_all.101 = f32[32,1,128]{2,1,0:T(1,128)S(1)} all-to-all(f32[32,1,128]{2,1,0:T(1,128)S(1)} %bitcast.59), channel_id=1, replica_groups=mesh['dev'=32] {'dev'}, dimensions={0} | all-to-all | bytes 32768 | tf_op jit(solution)/shard_map/all_to_all | solution.py:554
  222.5 2.5 %final.1 = (f32[2,3,64,128]{3,2,1,0:T(8,128)}, f32[2,3]{1,0:T(2,128)}) custom-call(f32[32,128]{1,0:T(8,128)S(1)} %bitcast.58, f32[3,64,128]{2,1,0:T(8,128)S(1)} %bitcast.52, f32[3,64,128]{2,1,0:T(8,128)S(1)} %get-tuple-element.17.refs_4_.refs_2_, f32[3,64,128]{2,1,0:T(8,128)S(1)} %get-tuple-element.19.refs_3_), custom_call_target="tpu_custom_call" | custom-call | tf_op jit(solution)/shard_map/final/pallas_call | solution.py:681
  (4 shorter events, 0.0 us)
Async XLA Ops:
  0.6 21.8 %copy-start.3 = (f32[64,3,128]{2,0,1:T(8,128)S(1)}, f32[64,3,128]{2,0,1:T(8,128)}, u32[]{:S(2)}) copy-start(f32[64,3,128]{2,0,1:T(8,128)} %param.9) | copy-start | bytes 294916
  16.7 5.7 %copy-start.4 = (s32[32,1,128]{2,1,0:T(1,128)S(1)}, s32[32,1,128]{2,1,0:T(1,128)}, u32[]{:S(2)}) copy-start(s32[32,1,128]{2,1,0:T(1,128)} %all_to_all.97) | copy-start | bytes 49156
  19.7 23.2 %all-to-all-start.1 = ((f32[32,48,128]{2,1,0:T(8,128)}), f32[32,48,128]{2,1,0:T(8,128)S(1)}, u32[]{:S(2)}, u32[]{:S(2)}) async-start(f32[32,48,128]{2,1,0:T(8,128)} %bitcast.60), calls=%async_computation.1 | async-start | bytes 1572864 | tf_op jit(solution)/shard_map/all_to_all | solution.py:554
  22.4 24.1 %copy-start.5 = (s32[8,128]{1,0:T(8,128)S(1)}, s32[8,128]{1,0:T(8,128)}, u32[]{:S(2)}) copy-start(s32[8,128]{1,0:T(8,128)} %get-tuple-element.13.refs_0_) | copy-start | bytes 12292
  42.9 43.2 %all-to-all-start.2 = ((f32[32,48,128]{2,1,0:T(8,128)}), f32[32,48,128]{2,1,0:T(8,128)S(1)}, u32[]{:S(2)}, u32[]{:S(2)}) async-start(f32[32,48,128]{2,1,0:T(8,128)} %bitcast.15), calls=%async_computation.2 | async-start | bytes 1572864 | tf_op jit(solution)/shard_map/all_to_all | solution.py:554
  86.2 21.4 %copy-start = (f32[64,16,384]{2,1,0:T(8,128)S(1)}, f32[64,16,384]{2,1,0:T(8,128)}, u32[]{:S(2)}) copy-start(f32[64,16,384]{2,1,0:T(8,128)} %refs_2_.3) | copy-start | bytes 4718596
  101.8 19.1 %all-to-all-start.3 = ((f32[32,24,128]{2,1,0:T(8,128)}), f32[32,24,128]{2,1,0:T(8,128)S(1)}, u32[]{:S(2)}, u32[]{:S(2)}) async-start(f32[32,24,128]{2,1,0:T(8,128)} %bitcast.17), calls=%async_computation.3 | async-start | bytes 786432 | tf_op jit(solution)/shard_map/all_to_all | solution.py:554
  107.6 1.4 copy-start.1
  177.8 16.9 %all-to-all-start.6 = ((f32[32,24,128]{2,1,0:T(8,128)}), f32[32,24,128]{2,1,0:T(8,128)S(1)}, u32[]{:S(2)}, u32[]{:S(2)}) async-start(f32[32,24,128]{2,1,0:T(8,128)} %bitcast.24), calls=%async_computation.6 | async-start | bytes 786432 | tf_op jit(solution)/shard_map/all_to_all | solution.py:554
  181.4 1.4 copy-start.2
